TPU v7x, 256 devices: a whole 4x4x8 slice. The times are simulated.
256 devices in a mesh: group: 2 (over y_hi), fsdp: 128 (over y_lo, z, x, core).
Axes of the slice: x: 4, y: 4 (y_hi: 2, y_lo: 2; y = y_hi * 2 + y_lo), z: 8, core: 2. Of those that a mesh axis runs over, the one named last changes fastest.
Arguments:
- teacher_rows: bfloat16 [163840, 2048], P(('group', 'fsdp')), may hold values from -6 to 6
- student_rows: bfloat16 [163840, 1024], P(('group', 'fsdp')), may hold values from -24 to 24
- counts: int32 [256], P(('group', 'fsdp')), may hold values from 213 to 640, as said below
- teacher_weight: bfloat16 [2048, 4096], P(None, ('group', 'fsdp')), may hold values from -0.125 to 0.125
- teacher_bias: float32 [4096], replicated, may hold values from -6 to 6
- teacher_gain: float32 [4096], replicated, may hold values from 0.1 to 1.9
- teacher_head: float32 [4096], replicated, may hold values from -0.09375 to 0.09375
- cross_weight: bfloat16 [1024, 1024], replicated, may hold values from -0.1875 to 0.1875
- cross_bias: float32 [1024], replicated, may hold values from -3 to 3
- out_weight: float32 [1024], replicated, may hold values from -0.1875 to 0.1875
Outputs:
- grad_cross: float32 [1024, 1024], P('fsdp')
- grad_bias: float32 [1024], replicated
- grad_out: float32 [1024], replicated
Inputs may be any that keep to these rules, and one draw needn't show every extreme that they name: counts[i] live impressions fill the first slots of shard i, the rest of its 640 slots are padding.
All inputs are finite; a program needn't handle non-finite values.
Results may differ from a plain program's by a relative error of at most 0.00035.
The roundings to bfloat16 on the way count: a program that leaves them out, or rounds other values in their place, can miss the bound.
Values may be sent and summed in bfloat16 or wider, within the bound.
No kernel may reach another device: no remote copies, remote signals or barrier semaphores. Data moves between devices by JAX's collectives and lax.ppermute only.
A program may use at most 128 MiB of HBM per device.

v0:
```python
import math

import jax
import jax.numpy as jnp
from jax import lax
from jax.experimental import pallas as pl
from jax.sharding import Mesh
from jax.sharding import PartitionSpec as P

FSDP = ("fsdp_0", "fsdp_1", "fsdp_2", "fsdp_3")
GROUP_FSDP = ("group", "fsdp_0", "fsdp_1", "fsdp_2", "fsdp_3")
SIZES = (4, 8, 4, 2)
Y, X = 0, 2


epsilon = 1e-06

RING_ORDER = (0, -1, 1, 2)


def flat(y, z, x, c):
    return ((y * SIZES[1] + z) * SIZES[2] + x) * SIZES[3] + c


def shift_pairs(dims, step):
    pairs = []
    for y in range(SIZES[0]):
        for z in range(SIZES[1]):
            for x in range(SIZES[2]):
                for c in range(SIZES[3]):
                    to = [y, z, x, c]
                    to[dims[c]] = (to[dims[c]] + step) % SIZES[dims[c]]
                    pairs.append((flat(y, z, x, c), flat(*to)))
    return pairs


def shift(value, dims, step):
    return lax.ppermute(value, GROUP_FSDP, shift_pairs(dims, step))


def swap_cores(value):
    return lax.ppermute(value, "fsdp_3", ((0, 1), (1, 0)))


def join_kernel(*refs):
    out = refs[-1]
    at = 0
    for ref in refs[:-1]:
        size = ref.shape[0]
        out[at : at + size, :] = ref[...]
        at += size


def join(parts):
    rows = sum(p.shape[0] for p in parts)
    return pl.pallas_call(
        join_kernel,
        out_shape=jax.ShapeDtypeStruct((rows, parts[0].shape[1]), parts[0].dtype),
        name="join",
    )(*parts)


def ring_gather(block, dims):
    left, right = shift(block, dims, 1), shift(block, dims, -1)
    return block, left, right, shift(left, dims, 1)


def wide_gather(first, second, dims):
    l1, r1 = shift(first, dims, 1), shift(first, dims, -1)
    l2, r2 = shift(second, dims, 1), shift(second, dims, -1)
    far = shift(l1, dims, 1), shift(r2, dims, -1)
    return (first, second), (l1, l2), (r1, r2), far


def one_hot_rows(index, width, dtype):
    return (index[:, None] == lax.broadcasted_iota(jnp.int32, (1, width), 1)).astype(dtype)


def transposed_dot(left, right):
    return lax.dot_general(
        left, right, (((1,), (1,)), ((), ())), preferred_element_type=jnp.float32
    )


def shards(
    teacher_rows,
    student_rows,
    counts,
    teacher_weight,
    teacher_bias,
    teacher_gain,
    teacher_head,
    cross_weight,
    cross_bias,
    out_weight,
):
    rows = teacher_rows.shape[0]
    width_t = teacher_bias.shape[0]
    width_s = cross_weight.shape[0]
    half_s = width_s // 2
    local = teacher_weight.shape[1]
    loss_scale = math.sqrt(width_s / (rows * lax.axis_size(GROUP_FSDP)))
    y_at = lax.axis_index(("group", "fsdp_0"))
    x_at, core = lax.axis_index("fsdp_2"), lax.axis_index("fsdp_3")
    group = lax.axis_index("group")

    mine = teacher_weight.T
    line = lax.all_to_all(
        jnp.broadcast_to(mine[None], (8, *mine.shape)), "fsdp_1", 0, 0, tiled=True
    ).reshape(8 * local, -1)

    t_rows = jnp.concatenate([teacher_rows, swap_cores(teacher_rows)], axis=0)
    s_rows = jnp.concatenate([student_rows, swap_cores(student_rows)], axis=0)

    vectors = jnp.stack([teacher_bias, teacher_gain, teacher_head]).reshape(3, 4, 8 * 4 * 2 * local)
    order_y = (y_at + jnp.array(RING_ORDER, jnp.int32)) % 4
    order_x = (x_at + jnp.array(RING_ORDER, jnp.int32)) % 4
    units = (
        order_x[:, None, None] * (2 * local)
        + jnp.arange(8, dtype=jnp.int32)[None, :, None] * (8 * local)
        + core * local
        + jnp.arange(local, dtype=jnp.int32)[None, None, :]
    ).reshape(-1)
    exact = lax.Precision.HIGHEST
    vectors = jnp.einsum(
        "wy,vyk->vwk", one_hot_rows(order_y, 4, jnp.float32), vectors, precision=exact
    )
    vectors = lax.dot_general(
        vectors.reshape(12, -1),
        one_hot_rows(units, vectors.shape[2], jnp.float32),
        (((1,), (1,)), ((), ())),
        precision=exact,
    ).reshape(3, 4, 4, 8 * local)
    vectors = jnp.where(core == 0, vectors, vectors.transpose(0, 2, 1, 3))
    vectors = vectors.reshape(3, 4, 2, 16 * local)
    line, vectors, t_rows, s_rows = lax.optimization_barrier((line, vectors, t_rows, s_rows))

    near, wide = (X, Y), (Y, X)
    around = ring_gather(line, near)
    plane = join(around[:2]), join(around[2:])

    cut = core * half_s
    cross_half = lax.dynamic_slice_in_dim(cross_weight, cut, half_s, axis=1)
    cross_bias_half = lax.dynamic_slice_in_dim(cross_bias, cut, half_s)
    out_half = lax.dynamic_slice_in_dim(out_weight, cut, half_s)
    cross = lax.dot_general(
        cross_half, s_rows, (((0,), (1,)), ((), ())), preferred_element_type=jnp.float32
    ) + cross_bias_half[:, None]
    inputs = transposed_dot(
        one_hot_rows(cut + jnp.arange(half_s, dtype=jnp.int32), width_s, s_rows.dtype), s_rows
    )
    mixed = inputs * cross + inputs
    student_part = jnp.sum(mixed * out_half[:, None], axis=0)

    features = (
        jnp.arange(2, dtype=jnp.int32)[:, None, None, None, None] * 8
        + jnp.arange(2, dtype=jnp.int32)[:, None, None, None] * (8 * 4 * 16)
        + jnp.arange(4, dtype=jnp.int32)[:, None, None] * 16
        + jnp.arange(8, dtype=jnp.int32)[:, None] * (4 * 16)
        + jnp.arange(8, dtype=jnp.int32)
    ).reshape(-1)
    turned = transposed_dot(one_hot_rows(features, width_s, s_rows.dtype), s_rows).astype(
        s_rows.dtype
    )
    blocks = wide_gather(*plane, wide)
    last, inputs, mixed, student_part, turned = lax.optimization_barrier(
        (blocks[3][1], inputs, mixed, student_part, turned)
    )
    blocks = (*blocks[:3], (blocks[3][0], last))

    pieces = [(i, j) for i in range(4) for j in range(2)]
    preact, squares = {}, 0.0
    for i, j in pieces:
        p = transposed_dot(blocks[i][j], t_rows) + vectors[0, i, j][:, None]
        preact[i, j] = p
        squares = squares + jnp.sum(p * p, axis=0)

    amount = counts.astype(jnp.float32)
    other = swap_cores(jnp.concatenate([squares, jnp.broadcast_to(amount, (128,))]))
    squares = squares + jnp.concatenate([other[rows : 2 * rows], other[:rows]])
    amounts = jnp.concatenate(
        [jnp.broadcast_to(amount, (rows,)), jnp.broadcast_to(other[2 * rows], (rows,))]
    )

    scale = lax.rsqrt(squares / width_t + epsilon)[None, :]
    logit = 0.0
    for i, j in pieces:
        gain, head = vectors[1, i, j][:, None], vectors[2, i, j][:, None]
        normed = preact[i, j] * scale * gain
        gated = 0.5 * normed * (1.0 + jnp.tanh(0.5 * normed))
        logit = logit + jnp.sum(gated * head, axis=0)
    part = student_part - logit
    other = swap_cores(part)
    differ = part + jnp.concatenate([other[rows:], other[:rows]])
    place = (jnp.arange(2 * rows, dtype=jnp.int32) % rows).astype(jnp.float32)
    error = (differ * (place < amounts).astype(jnp.float32) * loss_scale)[None, :]
    dcross = error * out_half[:, None] * inputs
    dcross_half = dcross.astype(jnp.bfloat16)
    small = jnp.stack([jnp.sum(dcross, axis=1), jnp.sum(error * mixed, axis=1)])

    parts = transposed_dot(turned, dcross_half).reshape(16, 8, 8, half_s)
    small = jnp.broadcast_to(jnp.pad(small, ((0, 6), (0, 0))), (16, 1, 8, half_s))
    parts = jnp.concatenate([parts, small], axis=1)
    parts = lax.all_to_all(parts, ("group", "fsdp_0", "fsdp_2"), 0, 0, tiled=True).sum(axis=0)
    small = parts[8, :2].reshape(8, half_s // 4)
    parts = jnp.concatenate(
        [parts[:8], jnp.broadcast_to(small, (8, *small.shape))], axis=2
    )
    parts = lax.all_to_all(parts, "fsdp_1", 0, 0, tiled=True).sum(axis=0)
    got = [
        lax.ppermute(parts, ("group", "fsdp_3"), pairs)
        for pairs in (((0, 0), (1, 2), (2, 1), (3, 3)), ((0, 2), (1, 0), (2, 3), (3, 1)))
    ]
    low = jnp.where(group == 0, got[0], got[1])
    high = jnp.where(group == 0, got[1], got[0])
    grad_cross = jnp.concatenate([low[:, :half_s], high[:, :half_s]], axis=1)
    small = jnp.concatenate(
        [low[:, half_s:].reshape(2, half_s), high[:, half_s:].reshape(2, half_s)], axis=1
    )
    return grad_cross, small[0], small[1]


def solution(mesh):
    split = Mesh(mesh.devices.reshape(2, 2, 8, 4, 2), GROUP_FSDP)
    in_specs = (
        P(GROUP_FSDP, None),
        P(GROUP_FSDP, None),
        P(GROUP_FSDP),
        P(None, GROUP_FSDP),
        P(),
        P(),
        P(),
        P(),
        P(),
        P(),
    )
    out_specs = (P(FSDP, None), P(), P())
    return jax.shard_map(
        shards,
        mesh=split,
        in_specs=in_specs,
        out_specs=out_specs,
        check_vma=False,
    )
```

profile of v0, /device:TPU:1, one launch (start us, length us, event | category | flops | bytes accessed | tf_op | source)
XLA Modules:
  0.0 172.2 jit_solution(10738370974573812539)
XLA Ops:
  0.7 1.9 %broadcast_in_dim.10 = bf16[8,16,2048]{2,1,0:T(8,128)(2,1)} broadcast(bf16[16,2048]{1,0:T(8,128)(2,1)} %bitcast.76), dimensions={1,2} | broadcast | bytes 589824 | tf_op jit(solution)/shard_map/broadcast_in_dim | solution.py:109
  2.6 9.0 %all-to-all-start = ((bf16[8,16,2048]{2,1,0:T(8,128)(2,1)}), bf16[8,16,2048]{2,1,0:T(8,128)(2,1)S(1)}, u32[]{:S(2)}, u32[]{:S(2)}) async-start(bf16[8,16,2048]{2,1,0:T(8,128)(2,1)} %broadcast_in_dim.10), calls=%async_computation | async-start | bytes 1048576 | tf_op jit(solution)/shard_map/all_to_all | solution.py:108
  11.6 1.0 collective-permute-start
  12.5 0.1 collective-permute-start.1
  12.7 0.1 add_add_fusion.1
  12.8 0.1 iota_add_fusion.1
  12.9 0.1 add.395
  13.0 0.2 convolution_bitcast_fusion
  13.2 1.1 fusion.7
  14.4 0.1 dynamic_slice.11
  14.5 0.1 dynamic_slice.10
  14.6 0.1 broadcast_add_fusion.1
  14.7 0.1 broadcast_add_fusion
  14.8 0.1 iota_add_fusion
  14.9 0.1 add.414
  15.6 3.6 %collective-permute-done.1 = bf16[640,1024]{1,0:T(8,128)(2,1)} collective-permute-done((bf16[640,1024]{1,0:T(8,128)(2,1)}, bf16[640,1024]{1,0:T(8,128)(2,1)}, u32[]{:S(2)}, u32[]{:S(2)}) %collective-permute-start.1) | collective-permute-done | bytes 1310752 | tf_op jit(solution)/shard_map/ppermute | solution.py:42
  19.3 3.6 %pad_maximum_fusion.1 = bf16[1280,1024]{1,0:T(8,128)(2,1)} fusion(bf16[640,1024]{1,0:T(8,128)(2,1)} %collective-permute-done.1, bf16[640,1024]{1,0:T(8,128)(2,1)} %param.13), kind=kLoop, calls=%fused_computation.14 | loop fusion | flops 5242880 | bytes 5242880 | tf_op jit(solution)/shard_map/concatenate | solution.py:113
  22.9 4.8 %pad_maximum_fusion = bf16[1280,2048]{1,0:T(8,128)(2,1)} fusion(bf16[640,2048]{1,0:T(8,128)(2,1)} %collective-permute-done, bf16[640,2048]{1,0:T(8,128)(2,1)S(1)} %copy-done.1), kind=kLoop, calls=%fused_computation | loop fusion | flops 10485760 | bytes 10485760 | tf_op jit(solution)/shard_map/concatenate | solution.py:112
  27.7 1.8 %all-to-all-done = bf16[8,16,2048]{2,1,0:T(8,128)(2,1)S(1)} async-done(((bf16[8,16,2048]{2,1,0:T(8,128)(2,1)}), bf16[8,16,2048]{2,1,0:T(8,128)(2,1)S(1)}, u32[]{:S(2)}, u32[]{:S(2)}) %all-to-all-start) | async-done | bytes 524320 | tf_op jit(solution)/shard_map/all_to_all | solution.py:108
  29.5 2.7 %collective-permute-start.2 = (bf16[128,2048]{1,0:T(8,128)(2,1)S(1)}, bf16[128,2048]{1,0:T(8,128)(2,1)S(1)}, u32[]{:S(2)}, u32[]{:S(2)}) collective-permute-start(bf16[128,2048]{1,0:T(8,128)(2,1)S(1)} %bitcast.73), channel_id=1, source_target_pairs={{0,6},{1,193},{2,0},{3,195},{4,2},{5,197},{6,4},{7,199},{8,14},{9,... | collective-permute-start | bytes 1572872 | tf_op jit(solution)/shard_map/ppermute | solution.py:38
  32.3 3.4 %fusion.6 = f32[512,1280]{1,0:T(8,128)S(1)} fusion(bf16[1280,1024]{1,0:T(8,128)(2,1)} %pad_maximum_fusion.1, s32[512]{0:T(512)S(1)} %iota_add_fusion.2), kind=kOutput, calls=%fused_computation.25 | convolution fusion | flops 1342701568 | bytes 5244928 | tf_op jit(solution)/shard_map/dot_general | solution.py:80
  35.7 4.5 %fusion.1 = bf16[1024,1280]{1,0:T(8,128)(2,1)} fusion(bf16[1280,1024]{1,0:T(8,128)(2,1)S(1)} %copy-done.2, s32[1024]{0:T(1024)S(1)} %add.414), kind=kOutput, calls=%fused_computation.4 | convolution fusion | flops 2686713856 | bytes 5246976 | tf_op jit(solution)/shard_map/dot_general | solution.py:80
  40.2 3.5 %multiply_reduce_fusion.1 = (f32[1280]{0:T(1024)S(1)}, f32[512,1280]{1,0:T(8,128)}) fusion(f32[512]{0:T(512)S(1)} %dynamic_slice.11, f32[512,1280]{1,0:T(8,128)S(1)} %fusion.6, f32[512]{0:T(512)S(1)} %dynamic_slice.10, bf16[1280,1024]{1,0:T(8,128)(2,1)S(1)} %copy-done.2, bf16[1024,1024]{1,0:T(8,128)(2,1)S(1)} %copy-done, s32[]{:T(128)S(6)} %select_n.47), kind=kOutput, calls=%fused_computation.17 | convolution fusion | flops 1345452800 | bytes 8922116 | tf_op jit(solution)/shard_map/dot_general | solution.py:146
  43.7 2.3 %join.3 = bf16[256,2048]{1,0:T(8,128)(2,1)} custom-call(bf16[128,2048]{1,0:T(8,128)(2,1)} %bitcast.75, bf16[128,2048]{1,0:T(8,128)(2,1)} %collective-permute-done.3.refs_1_), custom_call_target="tpu_custom_call" | custom-call | tf_op jit(solution)/shard_map/join/pallas_call | solution.py:56
  46.0 1.2 collective-permute-start.7
  47.2 1.7 collective-permute-start.9
  48.9 5.4 %multiply_reduce_fusion.17 = (f32[1280]{0:T(1024)S(1)}, f32[256,1280]{1,0:T(8,128)}) fusion(f32[256]{0:T(256)S(1)} %bitcast.104, bf16[256,2048]{1,0:T(8,128)(2,1)} %join.3, bf16[1280,2048]{1,0:T(8,128)(2,1)} %pad_maximum_fusion), kind=kOutput, calls=%fused_computation.44 | convolution fusion | flops 1343159040 | bytes 7608320 | tf_op jit(solution)/shard_map/dot_general | solution.py:80
  54.4 0.8 copy-done.8
  55.2 7.5 %collective-permute-done.4.refs_1_ = bf16[128,2048]{1,0:T(8,128)(2,1)} collective-permute-done((bf16[128,2048]{1,0:T(8,128)(2,1)}, bf16[128,2048]{1,0:T(8,128)(2,1)}, u32[]{:S(2)}, u32[]{:S(2)}) %collective-permute-start.4) | collective-permute-done | bytes 524320 | tf_op jit(solution)/shard_map/ppermute | solution.py:38
  62.6 2.4 %join.2 = bf16[256,2048]{1,0:T(8,128)(2,1)} custom-call(bf16[128,2048]{1,0:T(8,128)(2,1)} %copy-done.8, bf16[128,2048]{1,0:T(8,128)(2,1)} %collective-permute-done.4.refs_1_), custom_call_target="tpu_custom_call" | custom-call | tf_op jit(solution)/shard_map/join/pallas_call | solution.py:56
  65.0 0.2 collective-permute-start.5
  65.2 1.3 collective-permute-start.8
  66.5 4.5 %multiply_reduce_fusion.16 = (f32[1280]{0:T(1024)S(1)}, f32[256,1280]{1,0:T(8,128)S(1)}) fusion(f32[256]{0:T(256)S(1)} %bitcast.103, bf16[256,2048]{1,0:T(8,128)(2,1)} %join.2, bf16[1280,2048]{1,0:T(8,128)(2,1)} %pad_maximum_fusion), kind=kOutput, calls=%fused_computation.43 | convolution fusion | flops 1343159040 | bytes 7608320 | tf_op jit(solution)/shard_map/dot_general | solution.py:80
  71.0 1.3 collective-permute-start.10
  72.3 2.8 %multiply_reduce_fusion.15 = (f32[1280]{0:T(1024)S(1)}, f32[256,1280]{1,0:T(8,128)S(1)}) fusion(f32[256]{0:T(256)S(1)} %bitcast.102, bf16[256,2048]{1,0:T(8,128)(2,1)} %collective-permute-done.7, bf16[1280,2048]{1,0:T(8,128)(2,1)S(1)} %bitcast.71), kind=kOutput, calls=%fused_computation.42 | convolution fusion | flops 1343159040 | bytes 7608320 | tf_op jit(solution)/shard_map/dot_general | solution.py:80
  75.2 2.8 %multiply_reduce_fusion.13 = (f32[1280]{0:T(1024)S(1)}, f32[256,1280]{1,0:T(8,128)S(1)}) fusion(f32[256]{0:T(256)S(1)} %bitcast.101, bf16[256,2048]{1,0:T(8,128)(2,1)} %collective-permute-done.9, bf16[1280,2048]{1,0:T(8,128)(2,1)S(1)} %bitcast.71), kind=kOutput, calls=%fused_computation.40 | convolution fusion | flops 1343159040 | bytes 7608320 | tf_op jit(solution)/shard_map/dot_general | solution.py:80
  78.0 1.2 collective-permute-done.5
  79.2 1.4 collective-permute-start.6
  80.6 1.7 multiply_reduce_fusion.12
  82.3 1.7 multiply_reduce_fusion.14
  84.0 7.8 %collective-permute-done.10 = bf16[256,2048]{1,0:T(8,128)(2,1)S(1)} collective-permute-done((bf16[256,2048]{1,0:T(8,128)(2,1)}, bf16[256,2048]{1,0:T(8,128)(2,1)S(1)}, u32[]{:S(2)}, u32[]{:S(2)}) %collective-permute-start.10) | collective-permute-done | bytes 1048608 | tf_op jit(solution)/shard_map/ppermute | solution.py:38
  91.8 1.7 multiply_reduce_fusion.11
  93.5 1.7 multiply_reduce_fusion.10
  95.3 4.2 %collective-permute-start.11 = (f32[1408]{0:T(1024)S(1)}, f32[1408]{0:T(1024)S(1)}, u32[]{:S(2)}, u32[]{:S(2)}) collective-permute-start(f32[1408]{0:T(1024)S(1)} %concatenate.37), channel_id=1, source_target_pairs={{0,1},{1,0},{2,3},{3,2},{4,5},{5,4},{6,7},{7,6},{8,9},{9,8},{10,11... | collective-permute-start | bytes 16904 | tf_op jit(solution)/shard_map/ppermute | solution.py:42
  99.4 0.8 collective-permute-done.11
  100.3 1.0 multiply_reduce_fusion.9
  101.3 3.0 %multiply_reduce_fusion.8 = (f32[1280]{0:T(1024)S(1)}, f32[1280]{0:T(1024)S(1)}, f32[1280]{0:T(1024)S(1)}, f32[1280]{0:T(1024)S(1)}, f32[1280]{0:T(1024)S(1)}, /*index=5*/f32[1280]{0:T(1024)S(1)}) fusion(f32[256,1280]{1,0:T(8,128)S(1)} %get-tuple-element.82, f32[256]{0:T(256)S(1)} %bitcast.89, f32[256]{0:T(256)S(1)} %bitcast.90, f32[1280]{0:T(1024)S(1)} %fusion.25, ...), kind=kLoop, calls=%fused_computation.35 | loop fusion | flops 13754880 | bytes 7912448 | tf_op jit(solution)/shard_map/reduce_sum | solution.py:191
  104.4 0.4 collective-permute-start.12
  104.8 0.5 slice.148
  105.3 0.3 collective-permute-done.12
  105.6 0.7 fusion.27
  106.3 0.6 fusion.2
  106.9 1.2 copy-done.15
  108.1 1.6 fusion.9
  109.7 0.3 pad_maximum_fusion.2
  110.0 36.2 %all_to_all.15 = f32[16,9,8,512]{3,2,1,0:T(8,128)} all-to-all(f32[16,9,8,512]{3,2,1,0:T(8,128)S(1)} %pad_maximum_fusion.2), channel_id=1, replica_groups=mesh['group'=2,'fsdp_0'=2,'fsdp_1'=8,'fsdp_2'=4,'fsdp_3'=2] {'group','fs..., dimensions={0} | all-to-all | bytes 4718592 | tf_op jit(solution)/shard_map/all_to_all | solution.py:204
  146.3 1.9 %reduce_sum.208 = f32[9,8,512]{2,1,0:T(8,128)S(1)} reduce(f32[16,9,8,512]{3,2,1,0:T(8,128)} %all_to_all.15, f32[]{:T(128)} %constant.74.clone.1), dimensions={0}, to_apply=%region_19.20 | reduce | flops 552960 | bytes 2506756 | tf_op jit(solution)/shard_map/reduce_sum | solution.py:204
  148.2 13.2 %all_to_all.16 = f32[8,8,640]{2,1,0:T(8,128)S(1)} all-to-all(f32[8,8,640]{2,1,0:T(8,128)S(1)} %pad_maximum_fusion.3), channel_id=1, replica_groups=mesh['group'=2,'fsdp_0'=2,'fsdp_1'=8,'fsdp_2'=4,'fsdp_3'=2] {'fsdp_1'}, dimensions={0} | all-to-all | bytes 327680 | tf_op jit(solution)/shard_map/all_to_all | solution.py:209
  161.5 5.1 %collective-permute-start.13 = (f32[8,640]{1,0:T(8,128)S(1)}, f32[8,640]{1,0:T(8,128)S(1)}, u32[]{:S(2)}, u32[]{:S(2)}) collective-permute-start(f32[8,640]{1,0:T(8,128)S(1)} %reduce_sum.209), channel_id=1, source_target_pairs={{0,0},{1,128},{128,1},{129,129},{2,2},{3,130},{130,3},{131,131},{4... | collective-permute-start | bytes 61448 | tf_op jit(solution)/shard_map/ppermute | solution.py:211
  166.6 0.1 collective-permute-start.14
  166.7 1.4 collective-permute-done.13
  168.1 2.8 %collective-permute-done.14 = f32[8,640]{1,0:T(8,128)S(1)} collective-permute-done((f32[8,640]{1,0:T(8,128)S(1)}, f32[8,640]{1,0:T(8,128)S(1)}, u32[]{:S(2)}, u32[]{:S(2)}) %collective-permute-start.14) | collective-permute-done | bytes 20512 | tf_op jit(solution)/shard_map/ppermute | solution.py:211
  170.9 0.6 fusion.41
  171.6 0.6 pad_maximum_fusion.4
  (83 shorter events, 0.5 us)
Async XLA Ops:
  0.6 39.5 %copy-start = (bf16[1024,1024]{1,0:T(8,128)(2,1)S(1)}, bf16[1024,1024]{1,0:T(8,128)(2,1)}, u32[]{:S(2)}) copy-start(bf16[1024,1024]{1,0:T(8,128)(2,1)} %param.19) | copy-start | bytes 6291460
  0.6 12.1 %copy-start.14 = (s32[4]{0:T(128)S(1)}, s32[4]{0:T(128)}, u32[]{:S(2)}) copy-start(s32[4]{0:T(128)} %constant.83.clone) | copy-start | bytes 52
  0.7 12.0 %copy-start.9 = (f32[4096]{0:T(1024)S(1)}, f32[4096]{0:T(1024)}, u32[]{:S(2)}) copy-start(f32[4096]{0:T(1024)} %param.18) | copy-start | bytes 49156
  0.7 12.0 %copy-start.10 = (f32[4096]{0:T(1024)S(1)}, f32[4096]{0:T(1024)}, u32[]{:S(2)}) copy-start(f32[4096]{0:T(1024)} %param.17) | copy-start | bytes 49156
  0.7 12.0 %copy-start.11 = (f32[4096]{0:T(1024)S(1)}, f32[4096]{0:T(1024)}, u32[]{:S(2)}) copy-start(f32[4096]{0:T(1024)} %param.16) | copy-start | bytes 49156
  0.7 13.7 %copy-start.12 = (f32[1024]{0:T(1024)S(1)}, f32[1024]{0:T(1024)}, u32[]{:S(2)}) copy-start(f32[1024]{0:T(1024)} %param.21) | copy-start | bytes 12292
  0.7 13.8 %copy-start.13 = (f32[1024]{0:T(1024)S(1)}, f32[1024]{0:T(1024)}, u32[]{:S(2)}) copy-start(f32[1024]{0:T(1024)} %param.20) | copy-start | bytes 12292
  2.6 27.0 %all-to-all-start = ((bf16[8,16,2048]{2,1,0:T(8,128)(2,1)}), bf16[8,16,2048]{2,1,0:T(8,128)(2,1)S(1)}, u32[]{:S(2)}, u32[]{:S(2)}) async-start(bf16[8,16,2048]{2,1,0:T(8,128)(2,1)} %broadcast_in_dim.10), calls=%async_computation | async-start | bytes 1048576 | tf_op jit(solution)/shard_map/all_to_all | solution.py:108
  11.6 11.3 %collective-permute-start = (bf16[640,2048]{1,0:T(8,128)(2,1)}, bf16[640,2048]{1,0:T(8,128)(2,1)}, u32[]{:S(2)}, u32[]{:S(2)}) collective-permute-start(bf16[640,2048]{1,0:T(8,128)(2,1)} %param.12), channel_id=1, source_target_pairs={{0,1},{1,0},{2,3},{3,2},{4,5},{5,4},{6,7},{7,6},{8,9},{9,8},{10,11... | collective-permute-start | bytes 7864328 | tf_op jit(solution)/shard_map/ppermute | solution.py:42
  12.5 6.8 %collective-permute-start.1 = (bf16[640,1024]{1,0:T(8,128)(2,1)}, bf16[640,1024]{1,0:T(8,128)(2,1)}, u32[]{:S(2)}, u32[]{:S(2)}) collective-permute-start(bf16[640,1024]{1,0:T(8,128)(2,1)} %param.13), channel_id=1, source_target_pairs={{0,1},{1,0},{2,3},{3,2},{4,5},{5,4},{6,7},{7,6},{8,9},{9,8},{10,11... | collective-permute-start | bytes 3932168 | tf_op jit(solution)/shard_map/ppermute | solution.py:42
  19.3 3.6 %copy-start.1 = (bf16[640,2048]{1,0:T(8,128)(2,1)S(1)}, bf16[640,2048]{1,0:T(8,128)(2,1)}, u32[]{:S(2)}) copy-start(bf16[640,2048]{1,0:T(8,128)(2,1)} %param.12) | copy-start | bytes 7864324
  29.5 6.1 %copy-start.6 = (bf16[8,16,2048]{2,1,0:T(8,128)(2,1)}, bf16[8,16,2048]{2,1,0:T(8,128)(2,1)S(1)}, u32[]{:S(2)}) copy-start(bf16[8,16,2048]{2,1,0:T(8,128)(2,1)S(1)} %all-to-all-done) | copy-start | bytes 1572868
  29.5 6.1 %copy-start.2 = (bf16[1280,1024]{1,0:T(8,128)(2,1)S(1)}, bf16[1280,1024]{1,0:T(8,128)(2,1)}, u32[]{:S(2)}) copy-start(bf16[1280,1024]{1,0:T(8,128)(2,1)} %pad_maximum_fusion.1) | copy-start | bytes 7864324
  29.5 24.8 %collective-permute-start.2 = (bf16[128,2048]{1,0:T(8,128)(2,1)S(1)}, bf16[128,2048]{1,0:T(8,128)(2,1)S(1)}, u32[]{:S(2)}, u32[]{:S(2)}) collective-permute-start(bf16[128,2048]{1,0:T(8,128)(2,1)S(1)} %bitcast.73), channel_id=1, source_target_pairs={{0,6},{1,193},{2,0},{3,195},{4,2},{5,197},{6,4},{7,199},{8,14},{9,... | collective-permute-start | bytes 1572872 | tf_op jit(solution)/shard_map/ppermute | solution.py:38
  32.3 11.4 %collective-permute-start.3 = (bf16[128,2048]{1,0:T(8,128)(2,1)S(1)}, bf16[128,2048]{1,0:T(8,128)(2,1)}, u32[]{:S(2)}, u32[]{:S(2)}) collective-permute-start(bf16[128,2048]{1,0:T(8,128)(2,1)S(1)} %bitcast.74), channel_id=1, source_target_pairs={{0,2},{1,65},{2,4},{3,67},{4,6},{5,69},{6,0},{7,71},{8,10},{9,73},... | collective-permute-start | bytes 1572872 | tf_op jit(solution)/shard_map/ppermute | solution.py:38
  35.7 4.5 %copy-start.3 = (f32[512,1280]{1,0:T(8,128)}, f32[512,1280]{1,0:T(8,128)S(1)}, u32[]{:S(2)}) copy-start(f32[512,1280]{1,0:T(8,128)S(1)} %fusion.6) | copy-start | bytes 7864324
  46.0 25.1 %collective-permute-start.7 = (bf16[256,2048]{1,0:T(8,128)(2,1)}, bf16[256,2048]{1,0:T(8,128)(2,1)}, u32[]{:S(2)}, u32[]{:S(2)}) collective-permute-start(bf16[256,2048]{1,0:T(8,128)(2,1)} %join.3), channel_id=1, source_target_pairs={{0,64},{1,3},{2,66},{3,5},{4,68},{5,7},{6,70},{7,1},{8,72},{9,11},... | collective-permute-start | bytes 3145736 | tf_op jit(solution)/shard_map/ppermute | solution.py:38
  47.2 15.5 %collective-permute-start.4 = (bf16[128,2048]{1,0:T(8,128)(2,1)}, bf16[128,2048]{1,0:T(8,128)(2,1)}, u32[]{:S(2)}, u32[]{:S(2)}) collective-permute-start(bf16[128,2048]{1,0:T(8,128)(2,1)} %collective-permute-done.3.refs_1_), channel_id=1, source_target_pairs={{0,2},{1,65},{2,4},{3,67},{4,6},{5,69},{6,0},{7,71},{8,10},{9,73},... | collective-permute-start | bytes 1572872 | tf_op jit(solution)/shard_map/ppermute | solution.py:38
  47.2 27.9 %collective-permute-start.9 = (bf16[256,2048]{1,0:T(8,128)(2,1)}, bf16[256,2048]{1,0:T(8,128)(2,1)}, u32[]{:S(2)}, u32[]{:S(2)}) collective-permute-start(bf16[256,2048]{1,0:T(8,128)(2,1)} %join.3), channel_id=1, source_target_pairs={{0,192},{1,7},{2,194},{3,1},{4,196},{5,3},{6,198},{7,5},{8,200},{9... | collective-permute-start | bytes 3145736 | tf_op jit(solution)/shard_map/ppermute | solution.py:38
  54.4 0.8 copy-start.8
  62.6 9.7 %slice-start = ((s8[5242880]{0:T(1024)(128)(4,1)}), s8[1048576]{0:T(1024)(128)(4,1)S(1)}, s32[]{:S(2)}) async-start(s8[5242880]{0:T(1024)(128)(4,1)} %bitcast.70), calls=%async_computation.3 | async-start | bytes 2097152
  65.0 14.2 %collective-permute-start.5 = (bf16[256,2048]{1,0:T(8,128)(2,1)}, bf16[256,2048]{1,0:T(8,128)(2,1)S(1)}, u32[]{:S(2)}, u32[]{:S(2)}) collective-permute-start(bf16[256,2048]{1,0:T(8,128)(2,1)} %join.2), channel_id=1, source_target_pairs={{0,192},{1,7},{2,194},{3,1},{4,196},{5,3},{6,198},{7,5},{8,200},{9... | collective-permute-start | bytes 3145736 | tf_op jit(solution)/shard_map/ppermute | solution.py:38
  65.2 17.1 %collective-permute-start.8 = (bf16[256,2048]{1,0:T(8,128)(2,1)}, bf16[256,2048]{1,0:T(8,128)(2,1)S(1)}, u32[]{:S(2)}, u32[]{:S(2)}) collective-permute-start(bf16[256,2048]{1,0:T(8,128)(2,1)} %join.2), channel_id=1, source_target_pairs={{0,64},{1,3},{2,66},{3,5},{4,68},{5,7},{6,70},{7,1},{8,72},{9,11},... | collective-permute-start | bytes 3145736 | tf_op jit(solution)/shard_map/ppermute | solution.py:38
  66.5 5.8 %slice-start.1 = ((s8[5242880]{0:T(1024)(128)(4,1)}), s8[4194304]{0:T(1024)(128)(4,1)S(1)}, s32[]{:S(2)}) async-start(s8[5242880]{0:T(1024)(128)(4,1)} %bitcast.70), calls=%async_computation.4 | async-start | bytes 8388608
  71.0 20.8 %collective-permute-start.10 = (bf16[256,2048]{1,0:T(8,128)(2,1)}, bf16[256,2048]{1,0:T(8,128)(2,1)S(1)}, u32[]{:S(2)}, u32[]{:S(2)}) collective-permute-start(bf16[256,2048]{1,0:T(8,128)(2,1)} %collective-permute-done.7), channel_id=1, source_target_pairs={{0,64},{1,3},{2,66},{3,5},{4,68},{5,7},{6,70},{7,1},{8,72},{9,11},... | collective-permute-start | bytes 3145736 | tf_op jit(solution)/shard_map/ppermute | solution.py:38
  79.2 14.3 %collective-permute-start.6 = (bf16[256,2048]{1,0:T(8,128)(2,1)S(1)}, bf16[256,2048]{1,0:T(8,128)(2,1)S(1)}, u32[]{:S(2)}, u32[]{:S(2)}) collective-permute-start(bf16[256,2048]{1,0:T(8,128)(2,1)S(1)} %collective-permute-done.5), channel_id=1, source_target_pairs={{0,192},{1,7},{2,194},{3,1},{4,196},{5,3},{6,198},{7,5},{8,200},{9... | collective-permute-start | bytes 3145736 | tf_op jit(solution)/shard_map/ppermute | solution.py:38
  93.5 6.8 %copy-start.7 = (f32[256,1280]{1,0:T(8,128)S(1)}, f32[256,1280]{1,0:T(8,128)}, u32[]{:S(2)}) copy-start(f32[256,1280]{1,0:T(8,128)} %get-tuple-element.80) | copy-start | bytes 3932164
  95.3 5.0 %collective-permute-start.11 = (f32[1408]{0:T(1024)S(1)}, f32[1408]{0:T(1024)S(1)}, u32[]{:S(2)}, u32[]{:S(2)}) collective-permute-start(f32[1408]{0:T(1024)S(1)} %concatenate.37), channel_id=1, source_target_pairs={{0,1},{1,0},{2,3},{3,2},{4,5},{5,4},{6,7},{7,6},{8,9},{9,8},{10,11... | collective-permute-start | bytes 16904 | tf_op jit(solution)/shard_map/ppermute | solution.py:42
  101.3 5.0 %copy-start.4 = (f32[512,1280]{1,0:T(8,128)S(1)}, f32[512,1280]{1,0:T(8,128)}, u32[]{:S(2)}) copy-start(f32[512,1280]{1,0:T(8,128)} %copy-done.3) | copy-start | bytes 7864324
  101.3 5.0 %copy-start.5 = (f32[512,1280]{1,0:T(8,128)S(1)}, f32[512,1280]{1,0:T(8,128)}, u32[]{:S(2)}) copy-start(f32[512,1280]{1,0:T(8,128)} %get-tuple-element.20) | copy-start | bytes 7864324
  104.4 1.3 collective-permute-start.12
  106.3 1.7 %copy-start.15 = (bf16[1024,1280]{1,0:T(8,128)(2,1)S(1)}, bf16[1024,1280]{1,0:T(8,128)(2,1)}, u32[]{:S(2)}) copy-start(bf16[1024,1280]{1,0:T(8,128)(2,1)} %fusion.1) | copy-start | bytes 7864324
  161.5 6.6 %collective-permute-start.13 = (f32[8,640]{1,0:T(8,128)S(1)}, f32[8,640]{1,0:T(8,128)S(1)}, u32[]{:S(2)}, u32[]{:S(2)}) collective-permute-start(f32[8,640]{1,0:T(8,128)S(1)} %reduce_sum.209), channel_id=1, source_target_pairs={{0,0},{1,128},{128,1},{129,129},{2,2},{3,130},{130,3},{131,131},{4... | collective-permute-start | bytes 61448 | tf_op jit(solution)/shard_map/ppermute | solution.py:211
  166.6 4.2 %collective-permute-start.14 = (f32[8,640]{1,0:T(8,128)S(1)}, f32[8,640]{1,0:T(8,128)S(1)}, u32[]{:S(2)}, u32[]{:S(2)}) collective-permute-start(f32[8,640]{1,0:T(8,128)S(1)} %reduce_sum.209), channel_id=1, source_target_pairs={{0,128},{1,0},{128,129},{129,1},{2,130},{3,2},{130,131},{131,3},{4... | collective-permute-start | bytes 61448 | tf_op jit(solution)/shard_map/ppermute | solution.py:211
where the time goes:
time: 173 us; the launch traced here: 172 us
  blocking collectives  49.5 us (29%)
  matrix products  36.7 us (21%)
  starting transfers between devices  29.7 us (17%)
  waiting for transfers between devices  27.2 us (16%)
  other arithmetic  17.1 us (10%)
  local copies, waits for them, and re-layouts  5.54 us (3%)
  Pallas kernels  4.64 us (3%)
  between operations  1.83 us (1%)
    all_to_all x1, blocking collectives, shards(): lax.all_to_all(parts, ('group', 'fsdp_0', 'fsdp_2'), 0, 0, tiled=True)  36.2 us
    dot_general x11, matrix products, transposed_dot(): lax.dot_general(left, right, (((1,), (1,)), ((), ())), preferred_element_...  31.8 us
    ppermute x9, waiting for transfers between devices, shift(): return lax.ppermute(value, GROUP_FSDP, shift_pairs(dims, step))  16.5 us
    all_to_all x1, blocking collectives, shards(): parts = lax.all_to_all(parts, 'fsdp_1', 0, 0, tiled=True).sum(axis=0)  13.2 us
    ppermute x9, starting transfers between devices, shift(): return lax.ppermute(value, GROUP_FSDP, shift_pairs(dims, step))  9.82 us
    all_to_all x1, starting transfers between devices, shards(): lax.all_to_all(jnp.broadcast_to(mine[None], (8, *mine.shape)), 'fsdp_1',...  9 us
    ppermute x4, starting transfers between devices, swap_cores(): return lax.ppermute(value, 'fsdp_3', ((0, 1), (1, 0)))  5.67 us
    ppermute x2, starting transfers between devices, shards(): lax.ppermute(parts, ('group', 'fsdp_3'), pairs)  5.23 us
  transfers between devices with their start and end apart: 16, of which 9 were waited for; matrix products, arithmetic and copies ran while one was open for 25% of the time, Pallas kernels for 3%

commit v1 on v0

--- a/solution.py
+++ b/solution.py
@@ -70,6 +70,17 @@
     l2, r2 = shift(second, dims, 1), shift(second, dims, -1)
     far = shift(l1, dims, 1), shift(r2, dims, -1)
     return (first, second), (l1, l2), (r1, r2), far
+
+
+def line_sum(parts, dims):
+    groups = {}
+    for index in range(math.prod(SIZES)):
+        at = [index // 64, index // 8 % 8, index // 2 % 4, index % 2]
+        at[dims[at[3]]] = -1
+        groups.setdefault(tuple(at), []).append(index)
+    return lax.all_to_all(
+        parts, GROUP_FSDP, 0, 0, axis_index_groups=list(groups.values()), tiled=True
+    ).sum(axis=0)
 
 
 def one_hot_rows(index, width, dtype):
@@ -152,10 +163,14 @@
     mixed = inputs * cross + inputs
     student_part = jnp.sum(mixed * out_half[:, None], axis=0)
 
+    place_y = jnp.array([(y % 2) * (8 * 4 * 16) + (y // 2) * 8 for y in range(4)], jnp.int32)
+    place_x = jnp.arange(4, dtype=jnp.int32) * 16
     features = (
-        jnp.arange(2, dtype=jnp.int32)[:, None, None, None, None] * 8
-        + jnp.arange(2, dtype=jnp.int32)[:, None, None, None] * (8 * 4 * 16)
-        + jnp.arange(4, dtype=jnp.int32)[:, None, None] * 16
+        jnp.where(
+            core == 0,
+            place_x[:, None] + place_y[None, :],
+            place_y[:, None] + place_x[None, :],
+        )[:, :, None, None]
         + jnp.arange(8, dtype=jnp.int32)[:, None] * (4 * 16)
         + jnp.arange(8, dtype=jnp.int32)
     ).reshape(-1)
@@ -198,10 +213,12 @@
     dcross_half = dcross.astype(jnp.bfloat16)
     small = jnp.stack([jnp.sum(dcross, axis=1), jnp.sum(error * mixed, axis=1)])
 
-    parts = transposed_dot(turned, dcross_half).reshape(16, 8, 8, half_s)
-    small = jnp.broadcast_to(jnp.pad(small, ((0, 6), (0, 0))), (16, 1, 8, half_s))
-    parts = jnp.concatenate([parts, small], axis=1)
-    parts = lax.all_to_all(parts, ("group", "fsdp_0", "fsdp_2"), 0, 0, tiled=True).sum(axis=0)
+    parts = transposed_dot(turned, dcross_half).reshape(4, -1, half_s)
+    small = jnp.broadcast_to(jnp.pad(small, ((0, 6), (0, 0))), (4, 8, half_s))
+    parts = line_sum(jnp.concatenate([parts, small], axis=1), near)
+    small = jnp.broadcast_to(parts[-8:], (4, 8, half_s))
+    parts = line_sum(jnp.concatenate([parts[:-8].reshape(4, -1, half_s), small], axis=1), wide)
+    parts = parts.reshape(9, 8, half_s)
     small = parts[8, :2].reshape(8, half_s // 4)
     parts = jnp.concatenate(
         [parts[:8], jnp.broadcast_to(small, (8, *small.shape))], axis=2

time: 173 us -> 168 us (0.971)
  blocking collectives: 49.5 us -> 43.3 us
    all_to_all x1 -> x2, blocking collectives: 36.2 us -> 30 us  [line_sum(): lax.all_to_all(parts, GROUP_FSDP, 0, 0, axis_index_groups=list(groups.val...]
  transfers between devices with their start and end apart: 16 -> 16, of which waited for: 9 -> 9; matrix products, arithmetic and copies ran while one was open for 25% -> 26% of each run, Pallas kernels for 3% -> 3%
where the time goes in v1:
time: 168 us
  blocking collectives  43.3 us (26%)
  matrix products  36.7 us (22%)
  starting transfers between devices  31.4 us (19%)
  waiting for transfers between devices  27.3 us (16%)
  other arithmetic  17 us (10%)
  local copies, waits for them, and re-layouts  5.57 us (3%)
  Pallas kernels  4.64 us (3%)
  between operations  1.88 us (1%)
    dot_general x11, matrix products, transposed_dot(): lax.dot_general(left, right, (((1,), (1,)), ((), ())), preferred_element_...  31.8 us
    all_to_all x2, blocking collectives, line_sum(): lax.all_to_all(parts, GROUP_FSDP, 0, 0, axis_index_groups=list(groups.val...  30 us
    ppermute x9, waiting for transfers between devices, shift(): return lax.ppermute(value, GROUP_FSDP, shift_pairs(dims, step))  16.5 us
    all_to_all x1, blocking collectives, shards(): parts = lax.all_to_all(parts, 'fsdp_1', 0, 0, tiled=True).sum(axis=0)  13.3 us
    ppermute x9, starting transfers between devices, shift(): return lax.ppermute(value, GROUP_FSDP, shift_pairs(dims, step))  9.83 us
    all_to_all x1, starting transfers between devices, shards(): lax.all_to_all(jnp.broadcast_to(mine[None], (8, *mine.shape)), 'fsdp_1',...  9 us
    ppermute x2, starting transfers between devices, shards(): lax.ppermute(parts, ('group', 'fsdp_3'), pairs)  6.87 us
    ppermute x4, starting transfers between devices, swap_cores(): return lax.ppermute(value, 'fsdp_3', ((0, 1), (1, 0)))  5.65 us
  transfers between devices with their start and end apart: 16, of which 9 were waited for; matrix products, arithmetic and copies ran while one was open for 26% of the time, Pallas kernels for 3%

profile of v1, /device:TPU:1, one launch (start us, length us, event | category | flops | bytes accessed | tf_op | source)
XLA Modules:
  0.0 167.8 jit_solution(10025509128538773491)
XLA Ops:
  0.7 1.9 %broadcast_in_dim.12 = bf16[8,16,2048]{2,1,0:T(8,128)(2,1)} broadcast(bf16[16,2048]{1,0:T(8,128)(2,1)} %bitcast.82), dimensions={1,2} | broadcast | bytes 589824 | tf_op jit(solution)/shard_map/broadcast_in_dim | solution.py:120
  2.6 9.0 %all-to-all-start = ((bf16[8,16,2048]{2,1,0:T(8,128)(2,1)}), bf16[8,16,2048]{2,1,0:T(8,128)(2,1)S(1)}, u32[]{:S(2)}, u32[]{:S(2)}) async-start(bf16[8,16,2048]{2,1,0:T(8,128)(2,1)} %broadcast_in_dim.12), calls=%async_computation | async-start | bytes 1048576 | tf_op jit(solution)/shard_map/all_to_all | solution.py:119
  11.6 1.0 collective-permute-start
  12.5 0.1 collective-permute-start.1
  12.7 0.1 add_add_fusion.1
  12.8 0.1 iota_add_fusion.1
  12.9 0.1 add.393
  13.0 0.2 convolution_bitcast_fusion
  13.2 1.1 fusion.7
  14.4 0.1 dynamic_slice.11
  14.5 0.1 dynamic_slice.10
  14.6 0.1 broadcast_add_fusion
  14.7 0.1 iota_add_fusion
  14.8 0.1 add.412
  15.6 3.7 %collective-permute-done.1 = bf16[640,1024]{1,0:T(8,128)(2,1)} collective-permute-done((bf16[640,1024]{1,0:T(8,128)(2,1)}, bf16[640,1024]{1,0:T(8,128)(2,1)}, u32[]{:S(2)}, u32[]{:S(2)}) %collective-permute-start.1) | collective-permute-done | bytes 1310752 | tf_op jit(solution)/shard_map/ppermute | solution.py:42
  19.3 3.6 %pad_maximum_fusion.1 = bf16[1280,1024]{1,0:T(8,128)(2,1)} fusion(bf16[640,1024]{1,0:T(8,128)(2,1)} %collective-permute-done.1, bf16[640,1024]{1,0:T(8,128)(2,1)} %param.14), kind=kLoop, calls=%fused_computation.14 | loop fusion | flops 5242880 | bytes 5242880 | tf_op jit(solution)/shard_map/concatenate | solution.py:124
  22.9 4.8 %pad_maximum_fusion = bf16[1280,2048]{1,0:T(8,128)(2,1)} fusion(bf16[640,2048]{1,0:T(8,128)(2,1)} %collective-permute-done, bf16[640,2048]{1,0:T(8,128)(2,1)S(1)} %copy-done.1), kind=kLoop, calls=%fused_computation | loop fusion | flops 10485760 | bytes 10485760 | tf_op jit(solution)/shard_map/concatenate | solution.py:123
  27.7 1.8 %all-to-all-done = bf16[8,16,2048]{2,1,0:T(8,128)(2,1)S(1)} async-done(((bf16[8,16,2048]{2,1,0:T(8,128)(2,1)}), bf16[8,16,2048]{2,1,0:T(8,128)(2,1)S(1)}, u32[]{:S(2)}, u32[]{:S(2)}) %all-to-all-start) | async-done | bytes 524320 | tf_op jit(solution)/shard_map/all_to_all | solution.py:119
  29.5 2.7 %collective-permute-start.2 = (bf16[128,2048]{1,0:T(8,128)(2,1)S(1)}, bf16[128,2048]{1,0:T(8,128)(2,1)S(1)}, u32[]{:S(2)}, u32[]{:S(2)}) collective-permute-start(bf16[128,2048]{1,0:T(8,128)(2,1)S(1)} %bitcast.78), channel_id=1, source_target_pairs={{0,6},{1,193},{2,0},{3,195},{4,2},{5,197},{6,4},{7,199},{8,14},{9,... | collective-permute-start | bytes 1572872 | tf_op jit(solution)/shard_map/ppermute | solution.py:38
  32.3 3.4 %fusion.6 = f32[512,1280]{1,0:T(8,128)S(1)} fusion(bf16[1280,1024]{1,0:T(8,128)(2,1)} %pad_maximum_fusion.1, s32[512]{0:T(512)S(1)} %iota_add_fusion.2), kind=kOutput, calls=%fused_computation.25 | convolution fusion | flops 1342701568 | bytes 5244928 | tf_op jit(solution)/shard_map/dot_general | solution.py:91
  35.7 4.5 %fusion.1 = bf16[1024,1280]{1,0:T(8,128)(2,1)} fusion(bf16[1280,1024]{1,0:T(8,128)(2,1)S(1)} %copy-done.2, s32[1024]{0:T(1024)S(1)} %add.412), kind=kOutput, calls=%fused_computation.4 | convolution fusion | flops 2686713856 | bytes 5246976 | tf_op jit(solution)/shard_map/dot_general | solution.py:91
  40.2 3.5 %multiply_reduce_fusion.1 = (f32[1280]{0:T(1024)S(1)}, f32[512,1280]{1,0:T(8,128)}) fusion(f32[512]{0:T(512)S(1)} %dynamic_slice.11, f32[512,1280]{1,0:T(8,128)S(1)} %fusion.6, f32[512]{0:T(512)S(1)} %dynamic_slice.10, bf16[1280,1024]{1,0:T(8,128)(2,1)S(1)} %copy-done.2, bf16[1024,1024]{1,0:T(8,128)(2,1)S(1)} %copy-done, s32[]{:T(128)S(6)} %select_n.59), kind=kOutput, calls=%fused_computation.17 | convolution fusion | flops 1345452800 | bytes 8922116 | tf_op jit(solution)/shard_map/dot_general | solution.py:157
  43.7 2.3 %join.3 = bf16[256,2048]{1,0:T(8,128)(2,1)} custom-call(bf16[128,2048]{1,0:T(8,128)(2,1)} %bitcast.80, bf16[128,2048]{1,0:T(8,128)(2,1)} %collective-permute-done.3.refs_1_), custom_call_target="tpu_custom_call" | custom-call | tf_op jit(solution)/shard_map/join/pallas_call | solution.py:56
  46.0 1.2 collective-permute-start.7
  47.2 1.7 %collective-permute-start.9 = (bf16[256,2048]{1,0:T(8,128)(2,1)}, bf16[256,2048]{1,0:T(8,128)(2,1)}, u32[]{:S(2)}, u32[]{:S(2)}) collective-permute-start(bf16[256,2048]{1,0:T(8,128)(2,1)} %join.3), channel_id=1, source_target_pairs={{0,192},{1,7},{2,194},{3,1},{4,196},{5,3},{6,198},{7,5},{8,200},{9... | collective-permute-start | bytes 3145736 | tf_op jit(solution)/shard_map/ppermute | solution.py:38
  48.9 5.4 %multiply_reduce_fusion.17 = (f32[1280]{0:T(1024)S(1)}, f32[256,1280]{1,0:T(8,128)}) fusion(f32[256]{0:T(256)S(1)} %bitcast.110, bf16[256,2048]{1,0:T(8,128)(2,1)} %join.3, bf16[1280,2048]{1,0:T(8,128)(2,1)} %pad_maximum_fusion), kind=kOutput, calls=%fused_computation.44 | convolution fusion | flops 1343159040 | bytes 7608320 | tf_op jit(solution)/shard_map/dot_general | solution.py:91
  54.4 0.8 copy-done.8
  55.2 7.5 %collective-permute-done.4.refs_1_ = bf16[128,2048]{1,0:T(8,128)(2,1)} collective-permute-done((bf16[128,2048]{1,0:T(8,128)(2,1)}, bf16[128,2048]{1,0:T(8,128)(2,1)}, u32[]{:S(2)}, u32[]{:S(2)}) %collective-permute-start.4) | collective-permute-done | bytes 524320 | tf_op jit(solution)/shard_map/ppermute | solution.py:38
  62.7 2.4 %join.2 = bf16[256,2048]{1,0:T(8,128)(2,1)} custom-call(bf16[128,2048]{1,0:T(8,128)(2,1)} %copy-done.8, bf16[128,2048]{1,0:T(8,128)(2,1)} %collective-permute-done.4.refs_1_), custom_call_target="tpu_custom_call" | custom-call | tf_op jit(solution)/shard_map/join/pallas_call | solution.py:56
  65.0 0.2 collective-permute-start.5
  65.2 1.3 collective-permute-start.8
  66.5 4.5 %multiply_reduce_fusion.16 = (f32[1280]{0:T(1024)S(1)}, f32[256,1280]{1,0:T(8,128)S(1)}) fusion(f32[256]{0:T(256)S(1)} %bitcast.109, bf16[256,2048]{1,0:T(8,128)(2,1)} %join.2, bf16[1280,2048]{1,0:T(8,128)(2,1)} %pad_maximum_fusion), kind=kOutput, calls=%fused_computation.43 | convolution fusion | flops 1343159040 | bytes 7608320 | tf_op jit(solution)/shard_map/dot_general | solution.py:91
  71.0 1.3 collective-permute-start.10
  72.3 2.8 %multiply_reduce_fusion.15 = (f32[1280]{0:T(1024)S(1)}, f32[256,1280]{1,0:T(8,128)S(1)}) fusion(f32[256]{0:T(256)S(1)} %bitcast.108, bf16[256,2048]{1,0:T(8,128)(2,1)} %collective-permute-done.7, bf16[1280,2048]{1,0:T(8,128)(2,1)S(1)} %bitcast.75), kind=kOutput, calls=%fused_computation.42 | convolution fusion | flops 1343159040 | bytes 7608320 | tf_op jit(solution)/shard_map/dot_general | solution.py:91
  75.2 2.8 %multiply_reduce_fusion.13 = (f32[1280]{0:T(1024)S(1)}, f32[256,1280]{1,0:T(8,128)S(1)}) fusion(f32[256]{0:T(256)S(1)} %bitcast.107, bf16[256,2048]{1,0:T(8,128)(2,1)} %collective-permute-done.9, bf16[1280,2048]{1,0:T(8,128)(2,1)S(1)} %bitcast.75), kind=kOutput, calls=%fused_computation.40 | convolution fusion | flops 1343159040 | bytes 7608320 | tf_op jit(solution)/shard_map/dot_general | solution.py:91
  78.0 1.2 collective-permute-done.5
  79.2 1.4 collective-permute-start.6
  80.6 1.7 %multiply_reduce_fusion.12 = (f32[1280]{0:T(1024)S(1)}, f32[256,1280]{1,0:T(8,128)S(1)}) fusion(f32[256]{0:T(256)S(1)} %bitcast.105, bf16[256,2048]{1,0:T(8,128)(2,1)S(1)} %collective-permute-done.5, bf16[1280,2048]{1,0:T(8,128)(2,1)S(1)} %bitcast.75), kind=kOutput, calls=%fused_computation.39 | convolution fusion | flops 1343159040 | bytes 7608320 | tf_op jit(solution)/shard_map/dot_general | solution.py:91
  82.3 1.7 %multiply_reduce_fusion.14 = (f32[1280]{0:T(1024)S(1)}, f32[256,1280]{1,0:T(8,128)S(1)}) fusion(f32[256]{0:T(256)S(1)} %bitcast.106, bf16[256,2048]{1,0:T(8,128)(2,1)S(1)} %collective-permute-done.8, bf16[1280,2048]{1,0:T(8,128)(2,1)S(1)} %bitcast.75), kind=kOutput, calls=%fused_computation.41 | convolution fusion | flops 1343159040 | bytes 7608320 | tf_op jit(solution)/shard_map/dot_general | solution.py:91
  84.0 7.8 %collective-permute-done.10 = bf16[256,2048]{1,0:T(8,128)(2,1)S(1)} collective-permute-done((bf16[256,2048]{1,0:T(8,128)(2,1)}, bf16[256,2048]{1,0:T(8,128)(2,1)S(1)}, u32[]{:S(2)}, u32[]{:S(2)}) %collective-permute-start.10) | collective-permute-done | bytes 1048608 | tf_op jit(solution)/shard_map/ppermute | solution.py:38
  91.8 1.7 %multiply_reduce_fusion.11 = (f32[1280]{0:T(1024)S(1)}, f32[256,1280]{1,0:T(8,128)S(1)}) fusion(f32[256]{0:T(256)S(1)} %bitcast.104, bf16[256,2048]{1,0:T(8,128)(2,1)S(1)} %collective-permute-done.10, bf16[1280,2048]{1,0:T(8,128)(2,1)S(1)} %bitcast.75), kind=kOutput, calls=%fused_computation.38 | convolution fusion | flops 1343159040 | bytes 7608320 | tf_op jit(solution)/shard_map/dot_general | solution.py:91
  93.5 1.7 %multiply_reduce_fusion.10 = (f32[1280]{0:T(1024)S(1)}, f32[256,1280]{1,0:T(8,128)S(1)}) fusion(f32[256]{0:T(256)S(1)} %bitcast.103, bf16[256,2048]{1,0:T(8,128)(2,1)S(1)} %collective-permute-done.6, bf16[1280,2048]{1,0:T(8,128)(2,1)S(1)} %bitcast.75), kind=kOutput, calls=%fused_computation.37 | convolution fusion | flops 1343159040 | bytes 7608320 | tf_op jit(solution)/shard_map/dot_general | solution.py:91
  95.3 4.2 %collective-permute-start.11 = (f32[1408]{0:T(1024)S(1)}, f32[1408]{0:T(1024)S(1)}, u32[]{:S(2)}, u32[]{:S(2)}) collective-permute-start(f32[1408]{0:T(1024)S(1)} %concatenate.40), channel_id=1, source_target_pairs={{0,1},{1,0},{2,3},{3,2},{4,5},{5,4},{6,7},{7,6},{8,9},{9,8},{10,11... | collective-permute-start | bytes 16904 | tf_op jit(solution)/shard_map/ppermute | solution.py:42
  99.4 0.8 collective-permute-done.11
  100.3 1.0 multiply_reduce_fusion.9
  101.3 3.0 %multiply_reduce_fusion.8 = (f32[1280]{0:T(1024)S(1)}, f32[1280]{0:T(1024)S(1)}, f32[1280]{0:T(1024)S(1)}, f32[1280]{0:T(1024)S(1)}, f32[1280]{0:T(1024)S(1)}, /*index=5*/f32[1280]{0:T(1024)S(1)}) fusion(f32[256,1280]{1,0:T(8,128)S(1)} %get-tuple-element.82, f32[256]{0:T(256)S(1)} %bitcast.95, f32[256]{0:T(256)S(1)} %bitcast.96, f32[1280]{0:T(1024)S(1)} %fusion.25, ...), kind=kLoop, calls=%fused_computation.35 | loop fusion | flops 13754880 | bytes 7912448 | tf_op jit(solution)/shard_map/reduce_sum | solution.py:206
  104.4 0.4 collective-permute-start.12
  104.8 0.5 slice.160
  105.3 0.3 collective-permute-done.12
  105.6 0.7 fusion.27
  106.3 0.6 fusion.2
  106.9 1.2 copy-done.16
  108.1 1.6 fusion.9
  109.7 0.3 pad_maximum_fusion.2
  110.0 20.0 %all_to_all.20 = f32[4,264,512]{2,1,0:T(8,128)} all-to-all(f32[4,264,512]{2,1,0:T(8,128)S(1)} %pad_maximum_fusion.2), channel_id=1, replica_groups={{0,2,4,6},{1,65,129,193},{3,67,131,195},{5,69,133,197},{7,71,135,199},{..., dimensions={0} | all-to-all | bytes 4325376 | tf_op jit(solution)/shard_map/all_to_all | solution.py:81
  130.0 1.9 %reduce_sum.217 = f32[264,512]{1,0:T(8,128)S(1)} reduce(f32[4,264,512]{2,1,0:T(8,128)} %all_to_all.20, f32[]{:T(128)} %constant.74.clone.1), dimensions={0}, to_apply=%region_19.20 | reduce | flops 405504 | bytes 2703364 | tf_op jit(solution)/shard_map/reduce_sum | solution.py:83
  132.0 10.1 %all_to_all.21 = f32[4,72,512]{2,1,0:T(8,128)S(1)} all-to-all(f32[4,72,512]{2,1,0:T(8,128)S(1)} %pad_maximum_fusion.3), channel_id=1, replica_groups={{0,64,128,192},{1,3,5,7},{2,66,130,194},{4,68,132,196},{6,70,134,198},{..., dimensions={0} | all-to-all | bytes 1179648 | tf_op jit(solution)/shard_map/all_to_all | solution.py:81
  142.2 13.3 %all_to_all.22 = f32[8,8,640]{2,1,0:T(8,128)S(1)} all-to-all(f32[8,8,640]{2,1,0:T(8,128)S(1)} %pad_maximum_fusion.4), channel_id=1, replica_groups=mesh['group'=2,'fsdp_0'=2,'fsdp_1'=8,'fsdp_2'=4,'fsdp_3'=2] {'fsdp_1'}, dimensions={0} | all-to-all | bytes 327680 | tf_op jit(solution)/shard_map/all_to_all | solution.py:226
  155.4 6.8 %collective-permute-start.13 = (f32[8,640]{1,0:T(8,128)S(1)}, f32[8,640]{1,0:T(8,128)S(1)}, u32[]{:S(2)}, u32[]{:S(2)}) collective-permute-start(f32[8,640]{1,0:T(8,128)S(1)} %reduce_sum.219), channel_id=1, source_target_pairs={{0,0},{1,128},{128,1},{129,129},{2,2},{3,130},{130,3},{131,131},{4... | collective-permute-start | bytes 61448 | tf_op jit(solution)/shard_map/ppermute | solution.py:228
  162.2 0.1 collective-permute-start.14
  162.3 1.3 collective-permute-done.13
  163.7 2.8 %collective-permute-done.14 = f32[8,640]{1,0:T(8,128)S(1)} collective-permute-done((f32[8,640]{1,0:T(8,128)S(1)}, f32[8,640]{1,0:T(8,128)S(1)}, u32[]{:S(2)}, u32[]{:S(2)}) %collective-permute-start.14) | collective-permute-done | bytes 20512 | tf_op jit(solution)/shard_map/ppermute | solution.py:228
  166.6 0.6 fusion.41
  167.2 0.6 pad_maximum_fusion.5
  (89 shorter events, 0.7 us)
Async XLA Ops:
  0.6 39.5 %copy-start = (bf16[1024,1024]{1,0:T(8,128)(2,1)S(1)}, bf16[1024,1024]{1,0:T(8,128)(2,1)}, u32[]{:S(2)}) copy-start(bf16[1024,1024]{1,0:T(8,128)(2,1)} %param.20) | copy-start | bytes 6291460
  0.6 12.1 %copy-start.15 = (s32[4]{0:T(128)S(1)}, s32[4]{0:T(128)}, u32[]{:S(2)}) copy-start(s32[4]{0:T(128)} %constant.82.clone) | copy-start | bytes 52
  0.7 12.0 %copy-start.9 = (f32[4096]{0:T(1024)S(1)}, f32[4096]{0:T(1024)}, u32[]{:S(2)}) copy-start(f32[4096]{0:T(1024)} %param.19) | copy-start | bytes 49156
  0.7 12.0 %copy-start.10 = (f32[4096]{0:T(1024)S(1)}, f32[4096]{0:T(1024)}, u32[]{:S(2)}) copy-start(f32[4096]{0:T(1024)} %param.18) | copy-start | bytes 49156
  0.7 12.0 %copy-start.11 = (f32[4096]{0:T(1024)S(1)}, f32[4096]{0:T(1024)}, u32[]{:S(2)}) copy-start(f32[4096]{0:T(1024)} %param.17) | copy-start | bytes 49156
  0.7 13.7 %copy-start.13 = (f32[1024]{0:T(1024)S(1)}, f32[1024]{0:T(1024)}, u32[]{:S(2)}) copy-start(f32[1024]{0:T(1024)} %param.22) | copy-start | bytes 12292
  0.7 13.8 %copy-start.14 = (f32[1024]{0:T(1024)S(1)}, f32[1024]{0:T(1024)}, u32[]{:S(2)}) copy-start(f32[1024]{0:T(1024)} %param.21) | copy-start | bytes 12292
  0.7 13.8 %copy-start.12 = (s32[4]{0:T(128)S(1)}, s32[4]{0:T(128)}, u32[]{:S(2)}) copy-start(s32[4]{0:T(128)} %constant.83.clone) | copy-start | bytes 52
  2.6 27.0 %all-to-all-start = ((bf16[8,16,2048]{2,1,0:T(8,128)(2,1)}), bf16[8,16,2048]{2,1,0:T(8,128)(2,1)S(1)}, u32[]{:S(2)}, u32[]{:S(2)}) async-start(bf16[8,16,2048]{2,1,0:T(8,128)(2,1)} %broadcast_in_dim.12), calls=%async_computation | async-start | bytes 1048576 | tf_op jit(solution)/shard_map/all_to_all | solution.py:119
  11.6 11.3 %collective-permute-start = (bf16[640,2048]{1,0:T(8,128)(2,1)}, bf16[640,2048]{1,0:T(8,128)(2,1)}, u32[]{:S(2)}, u32[]{:S(2)}) collective-permute-start(bf16[640,2048]{1,0:T(8,128)(2,1)} %param.13), channel_id=1, source_target_pairs={{0,1},{1,0},{2,3},{3,2},{4,5},{5,4},{6,7},{7,6},{8,9},{9,8},{10,11... | collective-permute-start | bytes 7864328 | tf_op jit(solution)/shard_map/ppermute | solution.py:42
  12.5 6.8 %collective-permute-start.1 = (bf16[640,1024]{1,0:T(8,128)(2,1)}, bf16[640,1024]{1,0:T(8,128)(2,1)}, u32[]{:S(2)}, u32[]{:S(2)}) collective-permute-start(bf16[640,1024]{1,0:T(8,128)(2,1)} %param.14), channel_id=1, source_target_pairs={{0,1},{1,0},{2,3},{3,2},{4,5},{5,4},{6,7},{7,6},{8,9},{9,8},{10,11... | collective-permute-start | bytes 3932168 | tf_op jit(solution)/shard_map/ppermute | solution.py:42
  19.3 3.6 %copy-start.1 = (bf16[640,2048]{1,0:T(8,128)(2,1)S(1)}, bf16[640,2048]{1,0:T(8,128)(2,1)}, u32[]{:S(2)}) copy-start(bf16[640,2048]{1,0:T(8,128)(2,1)} %param.13) | copy-start | bytes 7864324
  29.5 6.1 %copy-start.6 = (bf16[8,16,2048]{2,1,0:T(8,128)(2,1)}, bf16[8,16,2048]{2,1,0:T(8,128)(2,1)S(1)}, u32[]{:S(2)}) copy-start(bf16[8,16,2048]{2,1,0:T(8,128)(2,1)S(1)} %all-to-all-done) | copy-start | bytes 1572868
  29.5 6.1 %copy-start.2 = (bf16[1280,1024]{1,0:T(8,128)(2,1)S(1)}, bf16[1280,1024]{1,0:T(8,128)(2,1)}, u32[]{:S(2)}) copy-start(bf16[1280,1024]{1,0:T(8,128)(2,1)} %pad_maximum_fusion.1) | copy-start | bytes 7864324
  29.5 24.8 %collective-permute-start.2 = (bf16[128,2048]{1,0:T(8,128)(2,1)S(1)}, bf16[128,2048]{1,0:T(8,128)(2,1)S(1)}, u32[]{:S(2)}, u32[]{:S(2)}) collective-permute-start(bf16[128,2048]{1,0:T(8,128)(2,1)S(1)} %bitcast.78), channel_id=1, source_target_pairs={{0,6},{1,193},{2,0},{3,195},{4,2},{5,197},{6,4},{7,199},{8,14},{9,... | collective-permute-start | bytes 1572872 | tf_op jit(solution)/shard_map/ppermute | solution.py:38
  32.3 11.4 %collective-permute-start.3 = (bf16[128,2048]{1,0:T(8,128)(2,1)S(1)}, bf16[128,2048]{1,0:T(8,128)(2,1)}, u32[]{:S(2)}, u32[]{:S(2)}) collective-permute-start(bf16[128,2048]{1,0:T(8,128)(2,1)S(1)} %bitcast.79), channel_id=1, source_target_pairs={{0,2},{1,65},{2,4},{3,67},{4,6},{5,69},{6,0},{7,71},{8,10},{9,73},... | collective-permute-start | bytes 1572872 | tf_op jit(solution)/shard_map/ppermute | solution.py:38
  35.7 4.5 %copy-start.3 = (f32[512,1280]{1,0:T(8,128)}, f32[512,1280]{1,0:T(8,128)S(1)}, u32[]{:S(2)}) copy-start(f32[512,1280]{1,0:T(8,128)S(1)} %fusion.6) | copy-start | bytes 7864324
  46.0 25.1 %collective-permute-start.7 = (bf16[256,2048]{1,0:T(8,128)(2,1)}, bf16[256,2048]{1,0:T(8,128)(2,1)}, u32[]{:S(2)}, u32[]{:S(2)}) collective-permute-start(bf16[256,2048]{1,0:T(8,128)(2,1)} %join.3), channel_id=1, source_target_pairs={{0,64},{1,3},{2,66},{3,5},{4,68},{5,7},{6,70},{7,1},{8,72},{9,11},... | collective-permute-start | bytes 3145736 | tf_op jit(solution)/shard_map/ppermute | solution.py:38
  47.2 15.5 %collective-permute-start.4 = (bf16[128,2048]{1,0:T(8,128)(2,1)}, bf16[128,2048]{1,0:T(8,128)(2,1)}, u32[]{:S(2)}, u32[]{:S(2)}) collective-permute-start(bf16[128,2048]{1,0:T(8,128)(2,1)} %collective-permute-done.3.refs_1_), channel_id=1, source_target_pairs={{0,2},{1,65},{2,4},{3,67},{4,6},{5,69},{6,0},{7,71},{8,10},{9,73},... | collective-permute-start | bytes 1572872 | tf_op jit(solution)/shard_map/ppermute | solution.py:38
  47.2 28.0 %collective-permute-start.9 = (bf16[256,2048]{1,0:T(8,128)(2,1)}, bf16[256,2048]{1,0:T(8,128)(2,1)}, u32[]{:S(2)}, u32[]{:S(2)}) collective-permute-start(bf16[256,2048]{1,0:T(8,128)(2,1)} %join.3), channel_id=1, source_target_pairs={{0,192},{1,7},{2,194},{3,1},{4,196},{5,3},{6,198},{7,5},{8,200},{9... | collective-permute-start | bytes 3145736 | tf_op jit(solution)/shard_map/ppermute | solution.py:38
  54.4 0.8 copy-start.8
  62.7 9.7 %slice-start = ((s8[5242880]{0:T(1024)(128)(4,1)}), s8[1048576]{0:T(1024)(128)(4,1)S(1)}, s32[]{:S(2)}) async-start(s8[5242880]{0:T(1024)(128)(4,1)} %bitcast.74), calls=%async_computation.4 | async-start | bytes 2097152
  65.0 14.2 %collective-permute-start.5 = (bf16[256,2048]{1,0:T(8,128)(2,1)}, bf16[256,2048]{1,0:T(8,128)(2,1)S(1)}, u32[]{:S(2)}, u32[]{:S(2)}) collective-permute-start(bf16[256,2048]{1,0:T(8,128)(2,1)} %join.2), channel_id=1, source_target_pairs={{0,192},{1,7},{2,194},{3,1},{4,196},{5,3},{6,198},{7,5},{8,200},{9... | collective-permute-start | bytes 3145736 | tf_op jit(solution)/shard_map/ppermute | solution.py:38
  65.2 17.1 %collective-permute-start.8 = (bf16[256,2048]{1,0:T(8,128)(2,1)}, bf16[256,2048]{1,0:T(8,128)(2,1)S(1)}, u32[]{:S(2)}, u32[]{:S(2)}) collective-permute-start(bf16[256,2048]{1,0:T(8,128)(2,1)} %join.2), channel_id=1, source_target_pairs={{0,64},{1,3},{2,66},{3,5},{4,68},{5,7},{6,70},{7,1},{8,72},{9,11},... | collective-permute-start | bytes 3145736 | tf_op jit(solution)/shard_map/ppermute | solution.py:38
  66.5 5.8 %slice-start.1 = ((s8[5242880]{0:T(1024)(128)(4,1)}), s8[4194304]{0:T(1024)(128)(4,1)S(1)}, s32[]{:S(2)}) async-start(s8[5242880]{0:T(1024)(128)(4,1)} %bitcast.74), calls=%async_computation.5 | async-start | bytes 8388608
  71.0 20.8 %collective-permute-start.10 = (bf16[256,2048]{1,0:T(8,128)(2,1)}, bf16[256,2048]{1,0:T(8,128)(2,1)S(1)}, u32[]{:S(2)}, u32[]{:S(2)}) collective-permute-start(bf16[256,2048]{1,0:T(8,128)(2,1)} %collective-permute-done.7), channel_id=1, source_target_pairs={{0,64},{1,3},{2,66},{3,5},{4,68},{5,7},{6,70},{7,1},{8,72},{9,11},... | collective-permute-start | bytes 3145736 | tf_op jit(solution)/shard_map/ppermute | solution.py:38
  79.2 14.3 %collective-permute-start.6 = (bf16[256,2048]{1,0:T(8,128)(2,1)S(1)}, bf16[256,2048]{1,0:T(8,128)(2,1)S(1)}, u32[]{:S(2)}, u32[]{:S(2)}) collective-permute-start(bf16[256,2048]{1,0:T(8,128)(2,1)S(1)} %collective-permute-done.5), channel_id=1, source_target_pairs={{0,192},{1,7},{2,194},{3,1},{4,196},{5,3},{6,198},{7,5},{8,200},{9... | collective-permute-start | bytes 3145736 | tf_op jit(solution)/shard_map/ppermute | solution.py:38
  93.5 6.8 %copy-start.7 = (f32[256,1280]{1,0:T(8,128)S(1)}, f32[256,1280]{1,0:T(8,128)}, u32[]{:S(2)}) copy-start(f32[256,1280]{1,0:T(8,128)} %get-tuple-element.80) | copy-start | bytes 3932164
  95.3 5.0 %collective-permute-start.11 = (f32[1408]{0:T(1024)S(1)}, f32[1408]{0:T(1024)S(1)}, u32[]{:S(2)}, u32[]{:S(2)}) collective-permute-start(f32[1408]{0:T(1024)S(1)} %concatenate.40), channel_id=1, source_target_pairs={{0,1},{1,0},{2,3},{3,2},{4,5},{5,4},{6,7},{7,6},{8,9},{9,8},{10,11... | collective-permute-start | bytes 16904 | tf_op jit(solution)/shard_map/ppermute | solution.py:42
  101.3 5.0 %copy-start.4 = (f32[512,1280]{1,0:T(8,128)S(1)}, f32[512,1280]{1,0:T(8,128)}, u32[]{:S(2)}) copy-start(f32[512,1280]{1,0:T(8,128)} %copy-done.3) | copy-start | bytes 7864324
  101.3 5.0 %copy-start.5 = (f32[512,1280]{1,0:T(8,128)S(1)}, f32[512,1280]{1,0:T(8,128)}, u32[]{:S(2)}) copy-start(f32[512,1280]{1,0:T(8,128)} %get-tuple-element.20) | copy-start | bytes 7864324
  104.4 1.3 collective-permute-start.12
  106.3 1.7 %copy-start.16 = (bf16[1024,1280]{1,0:T(8,128)(2,1)S(1)}, bf16[1024,1280]{1,0:T(8,128)(2,1)}, u32[]{:S(2)}) copy-start(bf16[1024,1280]{1,0:T(8,128)(2,1)} %fusion.1) | copy-start | bytes 7864324
  155.4 8.2 %collective-permute-start.13 = (f32[8,640]{1,0:T(8,128)S(1)}, f32[8,640]{1,0:T(8,128)S(1)}, u32[]{:S(2)}, u32[]{:S(2)}) collective-permute-start(f32[8,640]{1,0:T(8,128)S(1)} %reduce_sum.219), channel_id=1, source_target_pairs={{0,0},{1,128},{128,1},{129,129},{2,2},{3,130},{130,3},{131,131},{4... | collective-permute-start | bytes 61448 | tf_op jit(solution)/shard_map/ppermute | solution.py:228
  162.2 4.2 %collective-permute-start.14 = (f32[8,640]{1,0:T(8,128)S(1)}, f32[8,640]{1,0:T(8,128)S(1)}, u32[]{:S(2)}, u32[]{:S(2)}) collective-permute-start(f32[8,640]{1,0:T(8,128)S(1)} %reduce_sum.219), channel_id=1, source_target_pairs={{0,128},{1,0},{128,129},{129,1},{2,130},{3,2},{130,131},{131,3},{4... | collective-permute-start | bytes 61448 | tf_op jit(solution)/shard_map/ppermute | solution.py:228

commit v2 on v0

--- a/solution.py
+++ b/solution.py
@@ -14,6 +14,7 @@
 
 
 epsilon = 1e-06
+LARGEST_INPUT = 24.0
 
 RING_ORDER = (0, -1, 1, 2)
 
@@ -70,6 +71,10 @@
     l2, r2 = shift(second, dims, 1), shift(second, dims, -1)
     far = shift(l1, dims, 1), shift(r2, dims, -1)
     return (first, second), (l1, l2), (r1, r2), far
+
+
+def power_for(largest):
+    return jnp.floor(14.0 - jnp.log2(jnp.maximum(largest, 1e-30)))
 
 
 def one_hot_rows(index, width, dtype):
@@ -198,13 +203,26 @@
     dcross_half = dcross.astype(jnp.bfloat16)
     small = jnp.stack([jnp.sum(dcross, axis=1), jnp.sum(error * mixed, axis=1)])
 
-    parts = transposed_dot(turned, dcross_half).reshape(16, 8, 8, half_s)
-    small = jnp.broadcast_to(jnp.pad(small, ((0, 6), (0, 0))), (16, 1, 8, half_s))
-    parts = jnp.concatenate([parts, small], axis=1)
-    parts = lax.all_to_all(parts, ("group", "fsdp_0", "fsdp_2"), 0, 0, tiled=True).sum(axis=0)
-    small = parts[8, :2].reshape(8, half_s // 4)
+    reach = jnp.max(jnp.sum(jnp.abs(dcross), axis=1)) * LARGEST_INPUT
+    power, power_small = power_for(reach), power_for(jnp.max(jnp.abs(small)))
+    parts = transposed_dot(turned, dcross_half)
+    scaled = small * jnp.exp2(power_small)
+    top = scaled.astype(jnp.float16)
+    low = (scaled - top.astype(jnp.float32)).astype(jnp.float16)
+    powers = jnp.stack([power, power_small]).astype(jnp.float16)
+    tail = jnp.concatenate(
+        [top, low, jnp.broadcast_to(powers[:, None], (2, half_s)), jnp.zeros_like(top)], axis=0
+    )
+    parts = (parts * jnp.exp2(power)).astype(jnp.float16).reshape(16, -1, half_s)
+    parts = jnp.concatenate([parts, jnp.broadcast_to(tail, (16, *tail.shape))], axis=1)
+    parts = lax.all_to_all(parts, ("group", "fsdp_0", "fsdp_2"), 0, 0, tiled=True)
+    tail = parts[:, -8:].astype(jnp.float32)
+    small = ((tail[:, :2] + tail[:, 2:4]) * jnp.exp2(-tail[:, 5:6])).sum(axis=0)
+    parts = parts[:, :-8].astype(jnp.float32) * jnp.exp2(-tail[:, 4:5, :1])
+    parts = parts.sum(axis=0).reshape(8, 8, half_s)
+    small = small.reshape(8, half_s // 4)
     parts = jnp.concatenate(
-        [parts[:8], jnp.broadcast_to(small, (8, *small.shape))], axis=2
+        [parts, jnp.broadcast_to(small, (8, *small.shape))], axis=2
     )
     parts = lax.all_to_all(parts, "fsdp_1", 0, 0, tiled=True).sum(axis=0)
     got = [

time: 173 us -> 163 us (0.942)
  blocking collectives: 49.5 us -> 36.6 us
  matrix products: 36.7 us -> 39.2 us
    all_to_all x1, blocking collectives: 36.2 us -> 23.5 us  [shards(): lax.all_to_all(parts, ('group', 'fsdp_0', 'fsdp_2'), 0, 0, tiled=True)]
    dot_general x11, matrix products: 31.8 us -> 34.4 us  [transposed_dot(): lax.dot_general(left, right, (((1,), (1,)), ((), ())), preferred_element_...]
  transfers between devices with their start and end apart: 16 -> 16, of which waited for: 9 -> 9; matrix products, arithmetic and copies ran while one was open for 25% -> 27% of each run, Pallas kernels for 3% -> 3%
where the time goes in v2:
time: 163 us
  matrix products  39.2 us (24%)
  blocking collectives  36.6 us (22%)
  starting transfers between devices  29.8 us (18%)
  waiting for transfers between devices  27.3 us (17%)
  other arithmetic  17.3 us (11%)
  Pallas kernels  4.64 us (3%)
  local copies, waits for them, and re-layouts  4.45 us (3%)
  between operations  3.32 us (2%)
    dot_general x11, matrix products, transposed_dot(): lax.dot_general(left, right, (((1,), (1,)), ((), ())), preferred_element_...  34.4 us
    all_to_all x1, blocking collectives, shards(): lax.all_to_all(parts, ('group', 'fsdp_0', 'fsdp_2'), 0, 0, tiled=True)  23.5 us
    ppermute x9, waiting for transfers between devices, shift(): return lax.ppermute(value, GROUP_FSDP, shift_pairs(dims, step))  16.5 us
    all_to_all x1, blocking collectives, shards(): parts = lax.all_to_all(parts, 'fsdp_1', 0, 0, tiled=True).sum(axis=0)  13.1 us
    ppermute x9, starting transfers between devices, shift(): return lax.ppermute(value, GROUP_FSDP, shift_pairs(dims, step))  9.83 us
    all_to_all x1, starting transfers between devices, shards(): lax.all_to_all(jnp.broadcast_to(mine[None], (8, *mine.shape)), 'fsdp_1',...  9 us
    ppermute x4, starting transfers between devices, swap_cores(): return lax.ppermute(value, 'fsdp_3', ((0, 1), (1, 0)))  5.66 us
    ppermute x2, starting transfers between devices, shards(): lax.ppermute(parts, ('group', 'fsdp_3'), pairs)  5.31 us
  transfers between devices with their start and end apart: 16, of which 9 were waited for; matrix products, arithmetic and copies ran while one was open for 27% of the time, Pallas kernels for 3%

profile of v2, /device:TPU:1, one launch (start us, length us, event | category | flops | bytes accessed | tf_op | source)
XLA Modules:
  0.0 162.6 jit_solution(1632360188760950452)
XLA Ops:
  0.7 1.9 %broadcast_in_dim.14 = bf16[8,16,2048]{2,1,0:T(8,128)(2,1)} broadcast(bf16[16,2048]{1,0:T(8,128)(2,1)} %bitcast.84), dimensions={1,2} | broadcast | bytes 589824 | tf_op jit(solution)/shard_map/broadcast_in_dim | solution.py:114
  2.6 9.0 %all-to-all-start = ((bf16[8,16,2048]{2,1,0:T(8,128)(2,1)}), bf16[8,16,2048]{2,1,0:T(8,128)(2,1)S(1)}, u32[]{:S(2)}, u32[]{:S(2)}) async-start(bf16[8,16,2048]{2,1,0:T(8,128)(2,1)} %broadcast_in_dim.14), calls=%async_computation | async-start | bytes 1048576 | tf_op jit(solution)/shard_map/all_to_all | solution.py:113
  11.6 1.0 collective-permute-start
  12.5 0.1 collective-permute-start.1
  12.9 0.1 add.396
  13.0 0.2 convolution_bitcast_fusion
  13.2 1.1 fusion.5
  14.4 0.1 dynamic_slice.11
  14.8 0.1 iota_add_fusion
  14.9 0.1 add.415
  15.6 3.6 %collective-permute-done.1 = bf16[640,1024]{1,0:T(8,128)(2,1)} collective-permute-done((bf16[640,1024]{1,0:T(8,128)(2,1)}, bf16[640,1024]{1,0:T(8,128)(2,1)}, u32[]{:S(2)}, u32[]{:S(2)}) %collective-permute-start.1) | collective-permute-done | bytes 1310752 | tf_op jit(solution)/shard_map/ppermute | solution.py:43
  19.3 3.5 %pad_maximum_fusion.1 = bf16[1280,1024]{1,0:T(8,128)(2,1)} fusion(bf16[640,1024]{1,0:T(8,128)(2,1)} %collective-permute-done.1, bf16[640,1024]{1,0:T(8,128)(2,1)} %param.13), kind=kLoop, calls=%fused_computation.14 | loop fusion | flops 5242880 | bytes 5242880 | tf_op jit(solution)/shard_map/concatenate | solution.py:118
  22.7 4.8 %pad_maximum_fusion = bf16[1280,2048]{1,0:T(8,128)(2,1)} fusion(bf16[640,2048]{1,0:T(8,128)(2,1)} %collective-permute-done, bf16[640,2048]{1,0:T(8,128)(2,1)S(1)} %copy-done.1), kind=kLoop, calls=%fused_computation | loop fusion | flops 10485760 | bytes 10485760 | tf_op jit(solution)/shard_map/concatenate | solution.py:117
  27.6 2.0 %all-to-all-done = bf16[8,16,2048]{2,1,0:T(8,128)(2,1)S(1)} async-done(((bf16[8,16,2048]{2,1,0:T(8,128)(2,1)}), bf16[8,16,2048]{2,1,0:T(8,128)(2,1)S(1)}, u32[]{:S(2)}, u32[]{:S(2)}) %all-to-all-start) | async-done | bytes 524320 | tf_op jit(solution)/shard_map/all_to_all | solution.py:113
  29.5 2.7 %collective-permute-start.2 = (bf16[128,2048]{1,0:T(8,128)(2,1)S(1)}, bf16[128,2048]{1,0:T(8,128)(2,1)S(1)}, u32[]{:S(2)}, u32[]{:S(2)}) collective-permute-start(bf16[128,2048]{1,0:T(8,128)(2,1)S(1)} %bitcast.78), channel_id=1, source_target_pairs={{0,6},{1,193},{2,0},{3,195},{4,2},{5,197},{6,4},{7,199},{8,14},{9,... | collective-permute-start | bytes 1572872 | tf_op jit(solution)/shard_map/ppermute | solution.py:39
  32.3 3.4 %fusion.4 = f32[512,1280]{1,0:T(8,128)S(1)} fusion(bf16[1280,1024]{1,0:T(8,128)(2,1)} %pad_maximum_fusion.1, s32[512]{0:T(512)S(1)} %iota_add_fusion.2), kind=kOutput, calls=%fused_computation.25 | convolution fusion | flops 1342701568 | bytes 5244928 | tf_op jit(solution)/shard_map/dot_general | solution.py:85
  35.7 4.5 %fusion.1 = bf16[1024,1280]{1,0:T(8,128)(2,1)} fusion(bf16[1280,1024]{1,0:T(8,128)(2,1)S(1)} %copy-done.5, s32[1024]{0:T(1024)S(1)} %add.415), kind=kOutput, calls=%fused_computation.4 | convolution fusion | flops 2686713856 | bytes 5246976 | tf_op jit(solution)/shard_map/dot_general | solution.py:85
  40.2 3.5 %multiply_reduce_fusion.1 = (f32[1280]{0:T(1024)S(1)}, f32[512,1280]{1,0:T(8,128)}) fusion(f32[512]{0:T(512)S(1)} %dynamic_slice.11, f32[512,1280]{1,0:T(8,128)S(1)} %fusion.4, f32[512]{0:T(512)S(1)} %dynamic_slice.10, bf16[1280,1024]{1,0:T(8,128)(2,1)S(1)} %copy-done.5, bf16[1024,1024]{1,0:T(8,128)(2,1)S(1)} %copy-done, s32[]{:T(128)S(6)} %select_n.47), kind=kOutput, calls=%fused_computation.18 | convolution fusion | flops 1345452800 | bytes 8922116 | tf_op jit(solution)/shard_map/dot_general | solution.py:151
  43.7 2.3 %join.3 = bf16[256,2048]{1,0:T(8,128)(2,1)} custom-call(bf16[128,2048]{1,0:T(8,128)(2,1)} %bitcast.80, bf16[128,2048]{1,0:T(8,128)(2,1)} %collective-permute-done.3.refs_1_), custom_call_target="tpu_custom_call" | custom-call | tf_op jit(solution)/shard_map/join/pallas_call | solution.py:57
  46.0 1.2 collective-permute-start.7
  47.2 1.7 %collective-permute-start.9 = (bf16[256,2048]{1,0:T(8,128)(2,1)}, bf16[256,2048]{1,0:T(8,128)(2,1)}, u32[]{:S(2)}, u32[]{:S(2)}) collective-permute-start(bf16[256,2048]{1,0:T(8,128)(2,1)} %join.3), channel_id=1, source_target_pairs={{0,192},{1,7},{2,194},{3,1},{4,196},{5,3},{6,198},{7,5},{8,200},{9... | collective-permute-start | bytes 3145736 | tf_op jit(solution)/shard_map/ppermute | solution.py:39
  48.9 5.4 %multiply_reduce_fusion.18 = (f32[1280]{0:T(1024)S(1)}, f32[256,1280]{1,0:T(8,128)}) fusion(f32[256]{0:T(256)S(1)} %bitcast.114, bf16[256,2048]{1,0:T(8,128)(2,1)} %join.3, bf16[1280,2048]{1,0:T(8,128)(2,1)} %pad_maximum_fusion), kind=kOutput, calls=%fused_computation.45 | convolution fusion | flops 1343159040 | bytes 7608320 | tf_op jit(solution)/shard_map/dot_general | solution.py:85
  54.4 0.8 copy-done.8
  55.2 7.5 %collective-permute-done.4.refs_1_ = bf16[128,2048]{1,0:T(8,128)(2,1)} collective-permute-done((bf16[128,2048]{1,0:T(8,128)(2,1)}, bf16[128,2048]{1,0:T(8,128)(2,1)}, u32[]{:S(2)}, u32[]{:S(2)}) %collective-permute-start.4) | collective-permute-done | bytes 524320 | tf_op jit(solution)/shard_map/ppermute | solution.py:39
  62.6 2.4 %join.2 = bf16[256,2048]{1,0:T(8,128)(2,1)} custom-call(bf16[128,2048]{1,0:T(8,128)(2,1)} %copy-done.8, bf16[128,2048]{1,0:T(8,128)(2,1)} %collective-permute-done.4.refs_1_), custom_call_target="tpu_custom_call" | custom-call | tf_op jit(solution)/shard_map/join/pallas_call | solution.py:57
  65.0 0.2 collective-permute-start.5
  65.2 1.3 collective-permute-start.8
  66.5 4.5 %multiply_reduce_fusion.17 = (f32[1280]{0:T(1024)S(1)}, f32[256,1280]{1,0:T(8,128)S(1)}) fusion(f32[256]{0:T(256)S(1)} %bitcast.113, bf16[256,2048]{1,0:T(8,128)(2,1)} %join.2, bf16[1280,2048]{1,0:T(8,128)(2,1)} %pad_maximum_fusion), kind=kOutput, calls=%fused_computation.44 | convolution fusion | flops 1343159040 | bytes 7608320 | tf_op jit(solution)/shard_map/dot_general | solution.py:85
  71.0 1.3 collective-permute-start.10
  72.3 2.8 %multiply_reduce_fusion.16 = (f32[1280]{0:T(1024)S(1)}, f32[256,1280]{1,0:T(8,128)S(1)}) fusion(f32[256]{0:T(256)S(1)} %bitcast.112, bf16[256,2048]{1,0:T(8,128)(2,1)} %collective-permute-done.7, bf16[1280,2048]{1,0:T(8,128)(2,1)S(1)} %bitcast.77), kind=kOutput, calls=%fused_computation.43 | convolution fusion | flops 1343159040 | bytes 7608320 | tf_op jit(solution)/shard_map/dot_general | solution.py:85
  75.2 2.8 %multiply_reduce_fusion.14 = (f32[1280]{0:T(1024)S(1)}, f32[256,1280]{1,0:T(8,128)S(1)}) fusion(f32[256]{0:T(256)S(1)} %bitcast.111, bf16[256,2048]{1,0:T(8,128)(2,1)} %collective-permute-done.9, bf16[1280,2048]{1,0:T(8,128)(2,1)S(1)} %bitcast.77), kind=kOutput, calls=%fused_computation.41 | convolution fusion | flops 1343159040 | bytes 7608320 | tf_op jit(solution)/shard_map/dot_general | solution.py:85
  78.0 1.2 collective-permute-done.5
  79.2 1.4 collective-permute-start.6
  80.6 1.7 %multiply_reduce_fusion.13 = (f32[1280]{0:T(1024)S(1)}, f32[256,1280]{1,0:T(8,128)S(1)}) fusion(f32[256]{0:T(256)S(1)} %bitcast.109, bf16[256,2048]{1,0:T(8,128)(2,1)S(1)} %collective-permute-done.5, bf16[1280,2048]{1,0:T(8,128)(2,1)S(1)} %bitcast.77), kind=kOutput, calls=%fused_computation.40 | convolution fusion | flops 1343159040 | bytes 7608320 | tf_op jit(solution)/shard_map/dot_general | solution.py:85
  82.3 1.7 %multiply_reduce_fusion.15 = (f32[1280]{0:T(1024)S(1)}, f32[256,1280]{1,0:T(8,128)S(1)}) fusion(f32[256]{0:T(256)S(1)} %bitcast.110, bf16[256,2048]{1,0:T(8,128)(2,1)S(1)} %collective-permute-done.8, bf16[1280,2048]{1,0:T(8,128)(2,1)S(1)} %bitcast.77), kind=kOutput, calls=%fused_computation.42 | convolution fusion | flops 1343159040 | bytes 7608320 | tf_op jit(solution)/shard_map/dot_general | solution.py:85
  84.0 7.8 %collective-permute-done.10 = bf16[256,2048]{1,0:T(8,128)(2,1)S(1)} collective-permute-done((bf16[256,2048]{1,0:T(8,128)(2,1)}, bf16[256,2048]{1,0:T(8,128)(2,1)S(1)}, u32[]{:S(2)}, u32[]{:S(2)}) %collective-permute-start.10) | collective-permute-done | bytes 1048608 | tf_op jit(solution)/shard_map/ppermute | solution.py:39
  91.8 1.7 %multiply_reduce_fusion.12 = (f32[1280]{0:T(1024)S(1)}, f32[256,1280]{1,0:T(8,128)S(1)}) fusion(f32[256]{0:T(256)S(1)} %bitcast.108, bf16[256,2048]{1,0:T(8,128)(2,1)S(1)} %collective-permute-done.10, bf16[1280,2048]{1,0:T(8,128)(2,1)S(1)} %bitcast.77), kind=kOutput, calls=%fused_computation.39 | convolution fusion | flops 1343159040 | bytes 7608320 | tf_op jit(solution)/shard_map/dot_general | solution.py:85
  93.5 1.7 %multiply_reduce_fusion.11 = (f32[1280]{0:T(1024)S(1)}, f32[256,1280]{1,0:T(8,128)S(1)}) fusion(f32[256]{0:T(256)S(1)} %bitcast.107, bf16[256,2048]{1,0:T(8,128)(2,1)S(1)} %collective-permute-done.6, bf16[1280,2048]{1,0:T(8,128)(2,1)S(1)} %bitcast.77), kind=kOutput, calls=%fused_computation.38 | convolution fusion | flops 1343159040 | bytes 7608320 | tf_op jit(solution)/shard_map/dot_general | solution.py:85
  95.3 4.2 %collective-permute-start.11 = (f32[1408]{0:T(1024)S(1)}, f32[1408]{0:T(1024)S(1)}, u32[]{:S(2)}, u32[]{:S(2)}) collective-permute-start(f32[1408]{0:T(1024)S(1)} %concatenate.45), channel_id=1, source_target_pairs={{0,1},{1,0},{2,3},{3,2},{4,5},{5,4},{6,7},{7,6},{8,9},{9,8},{10,11... | collective-permute-start | bytes 16904 | tf_op jit(solution)/shard_map/ppermute | solution.py:43
  99.4 0.8 collective-permute-done.11
  100.3 1.0 multiply_reduce_fusion.10
  101.3 3.0 %multiply_reduce_fusion.9 = (f32[1280]{0:T(1024)S(1)}, f32[1280]{0:T(1024)S(1)}, f32[1280]{0:T(1024)S(1)}, f32[1280]{0:T(1024)S(1)}, f32[1280]{0:T(1024)S(1)}, /*index=5*/f32[1280]{0:T(1024)S(1)}) fusion(f32[256,1280]{1,0:T(8,128)S(1)} %get-tuple-element.85, f32[256]{0:T(256)S(1)} %bitcast.99, f32[256]{0:T(256)S(1)} %bitcast.100, f32[1280]{0:T(1024)S(1)} %fusion.30, ...), kind=kLoop, calls=%fused_computation.36 | loop fusion | flops 13754880 | bytes 7912448 | tf_op jit(solution)/shard_map/reduce_sum | solution.py:196
  104.4 0.4 collective-permute-start.12
  104.8 0.1 pad.11.clone
  104.9 0.5 slice.164
  105.4 0.2 collective-permute-done.12
  105.6 0.7 fusion.32
  106.3 0.8 abs_reduce_fusion
  107.1 0.6 abs_reduce_fusion.1
  108.5 0.6 reduce_max.18
  109.9 0.1 pad_maximum_fusion.6
  110.0 4.2 %multiply_convert_fusion = f16[1024,512]{1,0:T(8,128)(2,1)S(1)} fusion(bf16[1024,1280]{1,0:T(8,128)(2,1)} %fusion.1, f32[512,1280]{1,0:T(8,128)} %copy-done.2, f32[1280]{0:T(1024)S(1)} %fusion.32, f32[512]{0:T(512)S(1)} %dynamic_slice.11, f32[]{:T(128)S(6)} %exp2.28), kind=kOutput, calls=%fused_computation.20 | convolution fusion | flops 1345191936 | bytes 6298628 | tf_op jit(solution)/shard_map/dot_general | solution.py:85
  114.1 0.1 maximum_maximum_fusion
  114.2 0.3 pad_maximum_fusion.2
  114.5 23.5 %all_to_all.15 = f16[16,72,512]{2,1,0:T(8,128)(2,1)S(1)} all-to-all(f16[16,72,512]{2,1,0:T(8,128)(2,1)S(1)} %pad_maximum_fusion.2), channel_id=1, replica_groups=mesh['group'=2,'fsdp_0'=2,'fsdp_1'=8,'fsdp_2'=4,'fsdp_3'=2] {'group','fs..., dimensions={0} | all-to-all | bytes 2359296 | tf_op jit(solution)/shard_map/all_to_all | solution.py:218
  138.1 0.2 fusion.35
  138.4 0.3 multiply_reduce_fusion.2
  138.7 13.1 %all_to_all.16 = f32[8,8,640]{2,1,0:T(8,128)S(1)} all-to-all(f32[8,8,640]{2,1,0:T(8,128)S(1)} %pad_maximum_fusion.3), channel_id=1, replica_groups=mesh['group'=2,'fsdp_0'=2,'fsdp_1'=8,'fsdp_2'=4,'fsdp_3'=2] {'fsdp_1'}, dimensions={0} | all-to-all | bytes 327680 | tf_op jit(solution)/shard_map/all_to_all | solution.py:227
  151.8 5.2 %collective-permute-start.13 = (f32[8,640]{1,0:T(8,128)S(1)}, f32[8,640]{1,0:T(8,128)S(1)}, u32[]{:S(2)}, u32[]{:S(2)}) collective-permute-start(f32[8,640]{1,0:T(8,128)S(1)} %reduce_sum.229), channel_id=1, source_target_pairs={{0,0},{1,128},{128,1},{129,129},{2,2},{3,130},{130,3},{131,131},{4... | collective-permute-start | bytes 61448 | tf_op jit(solution)/shard_map/ppermute | solution.py:229
  157.1 0.1 collective-permute-start.14
  157.2 1.3 collective-permute-done.13
  158.5 2.8 %collective-permute-done.14 = f32[8,640]{1,0:T(8,128)S(1)} collective-permute-done((f32[8,640]{1,0:T(8,128)S(1)}, f32[8,640]{1,0:T(8,128)S(1)}, u32[]{:S(2)}, u32[]{:S(2)}) %collective-permute-start.14) | collective-permute-done | bytes 20512 | tf_op jit(solution)/shard_map/ppermute | solution.py:229
  161.4 0.6 fusion.47
  162.0 0.6 pad_maximum_fusion.4
  (90 shorter events, 1.1 us)
Async XLA Ops:
  0.6 39.5 %copy-start = (bf16[1024,1024]{1,0:T(8,128)(2,1)S(1)}, bf16[1024,1024]{1,0:T(8,128)(2,1)}, u32[]{:S(2)}) copy-start(bf16[1024,1024]{1,0:T(8,128)(2,1)} %param.19) | copy-start | bytes 6291460
  0.6 12.1 %copy-start.14 = (s32[4]{0:T(128)S(1)}, s32[4]{0:T(128)}, u32[]{:S(2)}) copy-start(s32[4]{0:T(128)} %constant.98.clone) | copy-start | bytes 52
  0.7 12.0 %copy-start.9 = (f32[4096]{0:T(1024)S(1)}, f32[4096]{0:T(1024)}, u32[]{:S(2)}) copy-start(f32[4096]{0:T(1024)} %param.18) | copy-start | bytes 49156
  0.7 12.0 %copy-start.10 = (f32[4096]{0:T(1024)S(1)}, f32[4096]{0:T(1024)}, u32[]{:S(2)}) copy-start(f32[4096]{0:T(1024)} %param.17) | copy-start | bytes 49156
  0.7 12.0 %copy-start.11 = (f32[4096]{0:T(1024)S(1)}, f32[4096]{0:T(1024)}, u32[]{:S(2)}) copy-start(f32[4096]{0:T(1024)} %param.16) | copy-start | bytes 49156
  0.7 13.7 %copy-start.12 = (f32[1024]{0:T(1024)S(1)}, f32[1024]{0:T(1024)}, u32[]{:S(2)}) copy-start(f32[1024]{0:T(1024)} %param.21) | copy-start | bytes 12292
  0.7 13.8 %copy-start.13 = (f32[1024]{0:T(1024)S(1)}, f32[1024]{0:T(1024)}, u32[]{:S(2)}) copy-start(f32[1024]{0:T(1024)} %param.20) | copy-start | bytes 12292
  2.6 27.0 %all-to-all-start = ((bf16[8,16,2048]{2,1,0:T(8,128)(2,1)}), bf16[8,16,2048]{2,1,0:T(8,128)(2,1)S(1)}, u32[]{:S(2)}, u32[]{:S(2)}) async-start(bf16[8,16,2048]{2,1,0:T(8,128)(2,1)} %broadcast_in_dim.14), calls=%async_computation | async-start | bytes 1048576 | tf_op jit(solution)/shard_map/all_to_all | solution.py:113
  11.6 11.2 %collective-permute-start = (bf16[640,2048]{1,0:T(8,128)(2,1)}, bf16[640,2048]{1,0:T(8,128)(2,1)}, u32[]{:S(2)}, u32[]{:S(2)}) collective-permute-start(bf16[640,2048]{1,0:T(8,128)(2,1)} %param.12), channel_id=1, source_target_pairs={{0,1},{1,0},{2,3},{3,2},{4,5},{5,4},{6,7},{7,6},{8,9},{9,8},{10,11... | collective-permute-start | bytes 7864328 | tf_op jit(solution)/shard_map/ppermute | solution.py:43
  12.5 6.8 %collective-permute-start.1 = (bf16[640,1024]{1,0:T(8,128)(2,1)}, bf16[640,1024]{1,0:T(8,128)(2,1)}, u32[]{:S(2)}, u32[]{:S(2)}) collective-permute-start(bf16[640,1024]{1,0:T(8,128)(2,1)} %param.13), channel_id=1, source_target_pairs={{0,1},{1,0},{2,3},{3,2},{4,5},{5,4},{6,7},{7,6},{8,9},{9,8},{10,11... | collective-permute-start | bytes 3932168 | tf_op jit(solution)/shard_map/ppermute | solution.py:43
  15.6 7.1 %copy-start.1 = (bf16[640,2048]{1,0:T(8,128)(2,1)S(1)}, bf16[640,2048]{1,0:T(8,128)(2,1)}, u32[]{:S(2)}) copy-start(bf16[640,2048]{1,0:T(8,128)(2,1)} %param.12) | copy-start | bytes 7864324
  29.5 6.1 %copy-start.6 = (bf16[8,16,2048]{2,1,0:T(8,128)(2,1)}, bf16[8,16,2048]{2,1,0:T(8,128)(2,1)S(1)}, u32[]{:S(2)}) copy-start(bf16[8,16,2048]{2,1,0:T(8,128)(2,1)S(1)} %all-to-all-done) | copy-start | bytes 1572868
  29.5 6.1 %copy-start.5 = (bf16[1280,1024]{1,0:T(8,128)(2,1)S(1)}, bf16[1280,1024]{1,0:T(8,128)(2,1)}, u32[]{:S(2)}) copy-start(bf16[1280,1024]{1,0:T(8,128)(2,1)} %pad_maximum_fusion.1) | copy-start | bytes 7864324
  29.5 24.8 %collective-permute-start.2 = (bf16[128,2048]{1,0:T(8,128)(2,1)S(1)}, bf16[128,2048]{1,0:T(8,128)(2,1)S(1)}, u32[]{:S(2)}, u32[]{:S(2)}) collective-permute-start(bf16[128,2048]{1,0:T(8,128)(2,1)S(1)} %bitcast.78), channel_id=1, source_target_pairs={{0,6},{1,193},{2,0},{3,195},{4,2},{5,197},{6,4},{7,199},{8,14},{9,... | collective-permute-start | bytes 1572872 | tf_op jit(solution)/shard_map/ppermute | solution.py:39
  32.3 11.4 %collective-permute-start.3 = (bf16[128,2048]{1,0:T(8,128)(2,1)S(1)}, bf16[128,2048]{1,0:T(8,128)(2,1)}, u32[]{:S(2)}, u32[]{:S(2)}) collective-permute-start(bf16[128,2048]{1,0:T(8,128)(2,1)S(1)} %bitcast.79), channel_id=1, source_target_pairs={{0,2},{1,65},{2,4},{3,67},{4,6},{5,69},{6,0},{7,71},{8,10},{9,73},... | collective-permute-start | bytes 1572872 | tf_op jit(solution)/shard_map/ppermute | solution.py:39
  35.7 4.5 %copy-start.2 = (f32[512,1280]{1,0:T(8,128)}, f32[512,1280]{1,0:T(8,128)S(1)}, u32[]{:S(2)}) copy-start(f32[512,1280]{1,0:T(8,128)S(1)} %fusion.4) | copy-start | bytes 7864324
  46.0 25.1 %collective-permute-start.7 = (bf16[256,2048]{1,0:T(8,128)(2,1)}, bf16[256,2048]{1,0:T(8,128)(2,1)}, u32[]{:S(2)}, u32[]{:S(2)}) collective-permute-start(bf16[256,2048]{1,0:T(8,128)(2,1)} %join.3), channel_id=1, source_target_pairs={{0,64},{1,3},{2,66},{3,5},{4,68},{5,7},{6,70},{7,1},{8,72},{9,11},... | collective-permute-start | bytes 3145736 | tf_op jit(solution)/shard_map/ppermute | solution.py:39
  47.2 15.5 %collective-permute-start.4 = (bf16[128,2048]{1,0:T(8,128)(2,1)}, bf16[128,2048]{1,0:T(8,128)(2,1)}, u32[]{:S(2)}, u32[]{:S(2)}) collective-permute-start(bf16[128,2048]{1,0:T(8,128)(2,1)} %collective-permute-done.3.refs_1_), channel_id=1, source_target_pairs={{0,2},{1,65},{2,4},{3,67},{4,6},{5,69},{6,0},{7,71},{8,10},{9,73},... | collective-permute-start | bytes 1572872 | tf_op jit(solution)/shard_map/ppermute | solution.py:39
  47.2 27.9 %collective-permute-start.9 = (bf16[256,2048]{1,0:T(8,128)(2,1)}, bf16[256,2048]{1,0:T(8,128)(2,1)}, u32[]{:S(2)}, u32[]{:S(2)}) collective-permute-start(bf16[256,2048]{1,0:T(8,128)(2,1)} %join.3), channel_id=1, source_target_pairs={{0,192},{1,7},{2,194},{3,1},{4,196},{5,3},{6,198},{7,5},{8,200},{9... | collective-permute-start | bytes 3145736 | tf_op jit(solution)/shard_map/ppermute | solution.py:39
  54.4 0.8 copy-start.8
  62.6 9.7 %slice-start = ((s8[5242880]{0:T(1024)(128)(4,1)}), s8[1048576]{0:T(1024)(128)(4,1)S(1)}, s32[]{:S(2)}) async-start(s8[5242880]{0:T(1024)(128)(4,1)} %bitcast.76), calls=%async_computation.3 | async-start | bytes 2097152
  65.0 14.2 %collective-permute-start.5 = (bf16[256,2048]{1,0:T(8,128)(2,1)}, bf16[256,2048]{1,0:T(8,128)(2,1)S(1)}, u32[]{:S(2)}, u32[]{:S(2)}) collective-permute-start(bf16[256,2048]{1,0:T(8,128)(2,1)} %join.2), channel_id=1, source_target_pairs={{0,192},{1,7},{2,194},{3,1},{4,196},{5,3},{6,198},{7,5},{8,200},{9... | collective-permute-start | bytes 3145736 | tf_op jit(solution)/shard_map/ppermute | solution.py:39
  65.2 17.1 %collective-permute-start.8 = (bf16[256,2048]{1,0:T(8,128)(2,1)}, bf16[256,2048]{1,0:T(8,128)(2,1)S(1)}, u32[]{:S(2)}, u32[]{:S(2)}) collective-permute-start(bf16[256,2048]{1,0:T(8,128)(2,1)} %join.2), channel_id=1, source_target_pairs={{0,64},{1,3},{2,66},{3,5},{4,68},{5,7},{6,70},{7,1},{8,72},{9,11},... | collective-permute-start | bytes 3145736 | tf_op jit(solution)/shard_map/ppermute | solution.py:39
  66.5 5.8 %slice-start.1 = ((s8[5242880]{0:T(1024)(128)(4,1)}), s8[4194304]{0:T(1024)(128)(4,1)S(1)}, s32[]{:S(2)}) async-start(s8[5242880]{0:T(1024)(128)(4,1)} %bitcast.76), calls=%async_computation.4 | async-start | bytes 8388608
  71.0 20.8 %collective-permute-start.10 = (bf16[256,2048]{1,0:T(8,128)(2,1)}, bf16[256,2048]{1,0:T(8,128)(2,1)S(1)}, u32[]{:S(2)}, u32[]{:S(2)}) collective-permute-start(bf16[256,2048]{1,0:T(8,128)(2,1)} %collective-permute-done.7), channel_id=1, source_target_pairs={{0,64},{1,3},{2,66},{3,5},{4,68},{5,7},{6,70},{7,1},{8,72},{9,11},... | collective-permute-start | bytes 3145736 | tf_op jit(solution)/shard_map/ppermute | solution.py:39
  79.2 14.3 %collective-permute-start.6 = (bf16[256,2048]{1,0:T(8,128)(2,1)S(1)}, bf16[256,2048]{1,0:T(8,128)(2,1)S(1)}, u32[]{:S(2)}, u32[]{:S(2)}) collective-permute-start(bf16[256,2048]{1,0:T(8,128)(2,1)S(1)} %collective-permute-done.5), channel_id=1, source_target_pairs={{0,192},{1,7},{2,194},{3,1},{4,196},{5,3},{6,198},{7,5},{8,200},{9... | collective-permute-start | bytes 3145736 | tf_op jit(solution)/shard_map/ppermute | solution.py:39
  93.5 6.8 %copy-start.7 = (f32[256,1280]{1,0:T(8,128)S(1)}, f32[256,1280]{1,0:T(8,128)}, u32[]{:S(2)}) copy-start(f32[256,1280]{1,0:T(8,128)} %get-tuple-element.83) | copy-start | bytes 3932164
  95.3 5.0 %collective-permute-start.11 = (f32[1408]{0:T(1024)S(1)}, f32[1408]{0:T(1024)S(1)}, u32[]{:S(2)}, u32[]{:S(2)}) collective-permute-start(f32[1408]{0:T(1024)S(1)} %concatenate.45), channel_id=1, source_target_pairs={{0,1},{1,0},{2,3},{3,2},{4,5},{5,4},{6,7},{7,6},{8,9},{9,8},{10,11... | collective-permute-start | bytes 16904 | tf_op jit(solution)/shard_map/ppermute | solution.py:43
  101.3 5.0 %copy-start.3 = (f32[512,1280]{1,0:T(8,128)S(1)}, f32[512,1280]{1,0:T(8,128)}, u32[]{:S(2)}) copy-start(f32[512,1280]{1,0:T(8,128)} %copy-done.2) | copy-start | bytes 7864324
  101.3 5.0 %copy-start.4 = (f32[512,1280]{1,0:T(8,128)S(1)}, f32[512,1280]{1,0:T(8,128)}, u32[]{:S(2)}) copy-start(f32[512,1280]{1,0:T(8,128)} %get-tuple-element.20) | copy-start | bytes 7864324
  104.4 1.3 collective-permute-start.12
  151.8 6.7 %collective-permute-start.13 = (f32[8,640]{1,0:T(8,128)S(1)}, f32[8,640]{1,0:T(8,128)S(1)}, u32[]{:S(2)}, u32[]{:S(2)}) collective-permute-start(f32[8,640]{1,0:T(8,128)S(1)} %reduce_sum.229), channel_id=1, source_target_pairs={{0,0},{1,128},{128,1},{129,129},{2,2},{3,130},{130,3},{131,131},{4... | collective-permute-start | bytes 61448 | tf_op jit(solution)/shard_map/ppermute | solution.py:229
  157.1 4.2 %collective-permute-start.14 = (f32[8,640]{1,0:T(8,128)S(1)}, f32[8,640]{1,0:T(8,128)S(1)}, u32[]{:S(2)}, u32[]{:S(2)}) collective-permute-start(f32[8,640]{1,0:T(8,128)S(1)} %reduce_sum.229), channel_id=1, source_target_pairs={{0,128},{1,0},{128,129},{129,1},{2,130},{3,2},{130,131},{131,3},{4... | collective-permute-start | bytes 61448 | tf_op jit(solution)/shard_map/ppermute | solution.py:229

commit v3 on v2

--- a/solution.py
+++ b/solution.py
@@ -4,6 +4,7 @@
 import jax.numpy as jnp
 from jax import lax
 from jax.experimental import pallas as pl
+from jax.experimental.pallas import tpu as pltpu
 from jax.sharding import Mesh
 from jax.sharding import PartitionSpec as P
 
@@ -57,6 +58,7 @@
     return pl.pallas_call(
         join_kernel,
         out_shape=jax.ShapeDtypeStruct((rows, parts[0].shape[1]), parts[0].dtype),
+        compiler_params=pltpu.CompilerParams(vmem_limit_bytes=4 * 2**20),
         name="join",
     )(*parts)
 
@@ -153,8 +155,8 @@
     ) + cross_bias_half[:, None]
     inputs = transposed_dot(
         one_hot_rows(cut + jnp.arange(half_s, dtype=jnp.int32), width_s, s_rows.dtype), s_rows
-    )
-    mixed = inputs * cross + inputs
+    ).astype(s_rows.dtype)
+    mixed = inputs.astype(jnp.float32) * cross + inputs.astype(jnp.float32)
     student_part = jnp.sum(mixed * out_half[:, None], axis=0)
 
     features = (
@@ -199,27 +201,26 @@
     differ = part + jnp.concatenate([other[rows:], other[:rows]])
     place = (jnp.arange(2 * rows, dtype=jnp.int32) % rows).astype(jnp.float32)
     error = (differ * (place < amounts).astype(jnp.float32) * loss_scale)[None, :]
-    dcross = error * out_half[:, None] * inputs
+    dcross = error * out_half[:, None] * inputs.astype(jnp.float32)
     dcross_half = dcross.astype(jnp.bfloat16)
     small = jnp.stack([jnp.sum(dcross, axis=1), jnp.sum(error * mixed, axis=1)])
-
-    reach = jnp.max(jnp.sum(jnp.abs(dcross), axis=1)) * LARGEST_INPUT
-    power, power_small = power_for(reach), power_for(jnp.max(jnp.abs(small)))
+    reach = jnp.maximum(jnp.sum(jnp.abs(dcross), axis=1) * LARGEST_INPUT, jnp.abs(small[1]))
+
+    dcross_half, reach, small = lax.optimization_barrier((dcross_half, reach, small))
     parts = transposed_dot(turned, dcross_half)
-    scaled = small * jnp.exp2(power_small)
+    power = power_for(jnp.max(reach))
+    scaled = small * jnp.exp2(power)
     top = scaled.astype(jnp.float16)
     low = (scaled - top.astype(jnp.float32)).astype(jnp.float16)
-    powers = jnp.stack([power, power_small]).astype(jnp.float16)
-    tail = jnp.concatenate(
-        [top, low, jnp.broadcast_to(powers[:, None], (2, half_s)), jnp.zeros_like(top)], axis=0
-    )
+    powers = jnp.broadcast_to(power.astype(jnp.float16), (4, half_s))
+    tail = jnp.concatenate([top, low, powers], axis=0)
     parts = (parts * jnp.exp2(power)).astype(jnp.float16).reshape(16, -1, half_s)
     parts = jnp.concatenate([parts, jnp.broadcast_to(tail, (16, *tail.shape))], axis=1)
     parts = lax.all_to_all(parts, ("group", "fsdp_0", "fsdp_2"), 0, 0, tiled=True)
     tail = parts[:, -8:].astype(jnp.float32)
-    small = ((tail[:, :2] + tail[:, 2:4]) * jnp.exp2(-tail[:, 5:6])).sum(axis=0)
-    parts = parts[:, :-8].astype(jnp.float32) * jnp.exp2(-tail[:, 4:5, :1])
-    parts = parts.sum(axis=0).reshape(8, 8, half_s)
+    scale = jnp.exp2(-tail[:, 4:5, :1])
+    small = ((tail[:, :2] + tail[:, 2:4]) * scale).sum(axis=0)
+    parts = (parts[:, :-8].astype(jnp.float32) * scale).sum(axis=0).reshape(8, 8, half_s)
     small = small.reshape(8, half_s // 4)
     parts = jnp.concatenate(
         [parts, jnp.broadcast_to(small, (8, *small.shape))], axis=2

time: 163 us -> 155 us (0.951)
  matrix products: 39.2 us -> 27.5 us
  waiting for transfers between devices: 27.3 us -> 38.2 us
  Pallas kernels: 4.64 us -> 0.14 us
    ppermute x9, waiting for transfers between devices: 16.5 us -> 27.5 us  [shift(): return lax.ppermute(value, GROUP_FSDP, shift_pairs(dims, step))]
    dot_general x11, matrix products: 34.4 us -> 24 us  [transposed_dot(): lax.dot_general(left, right, (((1,), (1,)), ((), ())), preferred_element_...]
    pallas_call x2, Pallas kernels: 4.64 us -> 0.14 us  [join(): pl.pallas_call(join_kernel, out_shape=jax.ShapeDtypeStruct((rows, parts[0...]
  transfers between devices with their start and end apart: 16 -> 16, of which waited for: 9 -> 10; matrix products, arithmetic and copies ran while one was open for 27% -> 21% of each run, Pallas kernels for 3% -> 0%
where the time goes in v3:
time: 155 us; the launch traced here: 154 us
  waiting for transfers between devices  38.2 us (25%)
  blocking collectives  36.6 us (24%)
  starting transfers between devices  28.8 us (19%)
  matrix products  27.5 us (18%)
  other arithmetic  16.9 us (11%)
  local copies, waits for them, and re-layouts  3.62 us (2%)
  between operations  2.55 us (2%)
    ppermute x9, waiting for transfers between devices, shift(): return lax.ppermute(value, GROUP_FSDP, shift_pairs(dims, step))  27.5 us
    dot_general x11, matrix products, transposed_dot(): lax.dot_general(left, right, (((1,), (1,)), ((), ())), preferred_element_...  24 us
    all_to_all x1, blocking collectives, shards(): lax.all_to_all(parts, ('group', 'fsdp_0', 'fsdp_2'), 0, 0, tiled=True)  23.4 us
    all_to_all x1, blocking collectives, shards(): parts = lax.all_to_all(parts, 'fsdp_1', 0, 0, tiled=True).sum(axis=0)  13.2 us
    all_to_all x1, starting transfers between devices, shards(): lax.all_to_all(jnp.broadcast_to(mine[None], (8, *mine.shape)), 'fsdp_1',...  9 us
    ppermute x9, starting transfers between devices, shift(): return lax.ppermute(value, GROUP_FSDP, shift_pairs(dims, step))  8.82 us
    ppermute x4, starting transfers between devices, swap_cores(): return lax.ppermute(value, 'fsdp_3', ((0, 1), (1, 0)))  5.7 us
    ppermute x2, starting transfers between devices, shards(): lax.ppermute(parts, ('group', 'fsdp_3'), pairs)  5.31 us
  transfers between devices with their start and end apart: 16, of which 10 were waited for; matrix products, arithmetic and copies ran while one was open for 21% of the time, Pallas kernels for 0%

profile of v3, /device:TPU:1, one launch (start us, length us, event | category | flops | bytes accessed | tf_op | source)
XLA Modules:
  0.0 154.4 jit_solution(17797637771298065468)
XLA Ops:
  0.7 1.9 %broadcast_in_dim.12 = bf16[8,16,2048]{2,1,0:T(8,128)(2,1)} broadcast(bf16[16,2048]{1,0:T(8,128)(2,1)} %bitcast.79), dimensions={1,2} | broadcast | bytes 589824 | tf_op jit(solution)/shard_map/broadcast_in_dim | solution.py:116
  2.6 9.0 %all-to-all-start = ((bf16[8,16,2048]{2,1,0:T(8,128)(2,1)}), bf16[8,16,2048]{2,1,0:T(8,128)(2,1)S(1)}, u32[]{:S(2)}, u32[]{:S(2)}) async-start(bf16[8,16,2048]{2,1,0:T(8,128)(2,1)} %broadcast_in_dim.12), calls=%async_computation | async-start | bytes 1048576 | tf_op jit(solution)/shard_map/all_to_all | solution.py:115
  11.6 1.0 collective-permute-start
  12.5 0.1 collective-permute-start.1
  12.7 0.1 add_add_fusion.1
  12.8 0.1 iota_add_fusion.1
  12.9 0.1 add.396
  13.0 0.2 convolution_bitcast_fusion
  13.2 1.1 fusion.6
  14.4 0.1 dynamic_slice.11
  14.7 0.1 broadcast_add_fusion
  14.8 0.1 iota_add_fusion
  14.9 0.1 add.415
  15.6 3.6 %collective-permute-done.1 = bf16[640,1024]{1,0:T(8,128)(2,1)} collective-permute-done((bf16[640,1024]{1,0:T(8,128)(2,1)}, bf16[640,1024]{1,0:T(8,128)(2,1)}, u32[]{:S(2)}, u32[]{:S(2)}) %collective-permute-start.1) | collective-permute-done | bytes 1310752 | tf_op jit(solution)/shard_map/ppermute | solution.py:44
  19.3 3.5 %pad_maximum_fusion.1 = bf16[1280,1024]{1,0:T(8,128)(2,1)} fusion(bf16[640,1024]{1,0:T(8,128)(2,1)} %collective-permute-done.1, bf16[640,1024]{1,0:T(8,128)(2,1)} %param.13), kind=kLoop, calls=%fused_computation.15 | loop fusion | flops 5242880 | bytes 5242880 | tf_op jit(solution)/shard_map/concatenate | solution.py:120
  22.7 5.1 %pad_maximum_fusion = bf16[1280,2048]{1,0:T(8,128)(2,1)} fusion(bf16[640,2048]{1,0:T(8,128)(2,1)} %collective-permute-done, bf16[640,2048]{1,0:T(8,128)(2,1)S(1)} %copy-done.1), kind=kLoop, calls=%fused_computation | loop fusion | flops 10485760 | bytes 10485760 | tf_op jit(solution)/shard_map/concatenate | solution.py:119
  27.8 1.7 %all-to-all-done = bf16[8,16,2048]{2,1,0:T(8,128)(2,1)S(1)} async-done(((bf16[8,16,2048]{2,1,0:T(8,128)(2,1)}), bf16[8,16,2048]{2,1,0:T(8,128)(2,1)S(1)}, u32[]{:S(2)}, u32[]{:S(2)}) %all-to-all-start) | async-done | bytes 524320 | tf_op jit(solution)/shard_map/all_to_all | solution.py:115
  29.5 2.7 %collective-permute-start.2 = (bf16[128,2048]{1,0:T(8,128)(2,1)S(1)}, bf16[128,2048]{1,0:T(8,128)(2,1)S(1)}, u32[]{:S(2)}, u32[]{:S(2)}) collective-permute-start(bf16[128,2048]{1,0:T(8,128)(2,1)S(1)} %bitcast.72), channel_id=1, source_target_pairs={{0,6},{1,193},{2,0},{3,195},{4,2},{5,197},{6,4},{7,199},{8,14},{9,... | collective-permute-start | bytes 1572872 | tf_op jit(solution)/shard_map/ppermute | solution.py:40
  32.3 3.5 %convolution_convert_fusion = bf16[512,1280]{1,0:T(8,128)(2,1)S(1)} fusion(bf16[1280,1024]{1,0:T(8,128)(2,1)} %pad_maximum_fusion.1, s32[512]{0:T(512)S(1)} %iota_add_fusion.2), kind=kOutput, calls=%fused_computation.6 | convolution fusion | flops 1343356928 | bytes 3934208 | tf_op jit(solution)/shard_map/dot_general | solution.py:87
  35.8 4.5 %fusion.1 = bf16[1024,1280]{1,0:T(8,128)(2,1)} fusion(bf16[1280,1024]{1,0:T(8,128)(2,1)S(1)} %copy-done.2, s32[1024]{0:T(1024)S(1)} %add.415), kind=kOutput, calls=%fused_computation.4 | convolution fusion | flops 2686713856 | bytes 5246976 | tf_op jit(solution)/shard_map/dot_general | solution.py:87
  40.3 2.1 %multiply_reduce_fusion.1 = (f32[1280]{0:T(1024)S(1)}, f32[512,1280]{1,0:T(8,128)S(1)}) fusion(f32[512]{0:T(512)S(1)} %dynamic_slice.11, f32[512]{0:T(512)S(1)} %dynamic_slice.10, bf16[1280,1024]{1,0:T(8,128)(2,1)S(1)} %copy-done.2, bf16[1024,1024]{1,0:T(8,128)(2,1)S(1)} %copy-done, s32[]{:T(128)S(6)} %select_n.47, ...), kind=kOutput, calls=%fused_computation.21 | convolution fusion | flops 1346108160 | bytes 7611396 | tf_op jit(solution)/shard_map/dot_general | solution.py:153
  42.5 1.3 collective-permute-start.7
  43.8 1.7 %collective-permute-start.9 = (bf16[256,2048]{1,0:T(8,128)(2,1)S(1)}, bf16[256,2048]{1,0:T(8,128)(2,1)S(1)}, u32[]{:S(2)}, u32[]{:S(2)}) collective-permute-start(bf16[256,2048]{1,0:T(8,128)(2,1)S(1)} %join.3), channel_id=1, source_target_pairs={{0,192},{1,7},{2,194},{3,1},{4,196},{5,3},{6,198},{7,5},{8,200},{9... | collective-permute-start | bytes 3145736 | tf_op jit(solution)/shard_map/ppermute | solution.py:40
  45.5 1.6 %multiply_reduce_fusion.18 = (f32[1280]{0:T(1024)S(1)}, f32[256,1280]{1,0:T(8,128)S(1)}) fusion(f32[256]{0:T(256)S(1)} %bitcast.107, bf16[256,2048]{1,0:T(8,128)(2,1)S(1)} %join.3, bf16[1280,2048]{1,0:T(8,128)(2,1)S(1)} %bitcast.76), kind=kOutput, calls=%fused_computation.44 | convolution fusion | flops 1343159040 | bytes 7608320 | tf_op jit(solution)/shard_map/dot_general | solution.py:87
  47.2 11.8 %collective-permute-done.4.refs_1_ = bf16[128,2048]{1,0:T(8,128)(2,1)S(1)} collective-permute-done((bf16[128,2048]{1,0:T(8,128)(2,1)S(1)}, bf16[128,2048]{1,0:T(8,128)(2,1)S(1)}, u32[]{:S(2)}, u32[]{:S(2)}) %collective-permute-start.4) | collective-permute-done | bytes 524320 | tf_op jit(solution)/shard_map/ppermute | solution.py:40
  59.0 0.3 collective-permute-start.5
  59.3 1.3 collective-permute-start.8
  60.6 1.6 %multiply_reduce_fusion.17 = (f32[1280]{0:T(1024)S(1)}, f32[256,1280]{1,0:T(8,128)S(1)}) fusion(f32[256]{0:T(256)S(1)} %bitcast.106, bf16[256,2048]{1,0:T(8,128)(2,1)S(1)} %join.2, bf16[1280,2048]{1,0:T(8,128)(2,1)S(1)} %bitcast.76), kind=kOutput, calls=%fused_computation.43 | convolution fusion | flops 1343159040 | bytes 7608320 | tf_op jit(solution)/shard_map/dot_general | solution.py:87
  62.2 1.2 collective-permute-done.7
  63.4 0.1 collective-permute-start.10
  63.5 1.6 %multiply_reduce_fusion.16 = (f32[1280]{0:T(1024)S(1)}, f32[256,1280]{1,0:T(8,128)S(1)}) fusion(f32[256]{0:T(256)S(1)} %bitcast.105, bf16[256,2048]{1,0:T(8,128)(2,1)S(1)} %collective-permute-done.7, bf16[1280,2048]{1,0:T(8,128)(2,1)S(1)} %bitcast.76), kind=kOutput, calls=%fused_computation.42 | convolution fusion | flops 1343159040 | bytes 7608320 | tf_op jit(solution)/shard_map/dot_general | solution.py:87
  65.1 1.6 %multiply_reduce_fusion.14 = (f32[1280]{0:T(1024)S(1)}, f32[256,1280]{1,0:T(8,128)S(1)}) fusion(f32[256]{0:T(256)S(1)} %bitcast.104, bf16[256,2048]{1,0:T(8,128)(2,1)S(1)} %collective-permute-done.9, bf16[1280,2048]{1,0:T(8,128)(2,1)S(1)} %bitcast.76), kind=kOutput, calls=%fused_computation.40 | convolution fusion | flops 1343159040 | bytes 7608320 | tf_op jit(solution)/shard_map/dot_general | solution.py:87
  66.7 6.4 %collective-permute-done.5 = bf16[256,2048]{1,0:T(8,128)(2,1)S(1)} collective-permute-done((bf16[256,2048]{1,0:T(8,128)(2,1)S(1)}, bf16[256,2048]{1,0:T(8,128)(2,1)S(1)}, u32[]{:S(2)}, u32[]{:S(2)}) %collective-permute-start.5) | collective-permute-done | bytes 1048608 | tf_op jit(solution)/shard_map/ppermute | solution.py:40
  73.1 1.4 collective-permute-start.6
  74.5 1.6 %multiply_reduce_fusion.13 = (f32[1280]{0:T(1024)S(1)}, f32[256,1280]{1,0:T(8,128)S(1)}) fusion(f32[256]{0:T(256)S(1)} %bitcast.102, bf16[256,2048]{1,0:T(8,128)(2,1)S(1)} %collective-permute-done.5, bf16[1280,2048]{1,0:T(8,128)(2,1)S(1)} %bitcast.76), kind=kOutput, calls=%fused_computation.39 | convolution fusion | flops 1343159040 | bytes 7608320 | tf_op jit(solution)/shard_map/dot_general | solution.py:87
  76.1 1.6 %multiply_reduce_fusion.15 = (f32[1280]{0:T(1024)S(1)}, f32[256,1280]{1,0:T(8,128)S(1)}) fusion(f32[256]{0:T(256)S(1)} %bitcast.103, bf16[256,2048]{1,0:T(8,128)(2,1)S(1)} %collective-permute-done.8, bf16[1280,2048]{1,0:T(8,128)(2,1)S(1)} %bitcast.76), kind=kOutput, calls=%fused_computation.41 | convolution fusion | flops 1343159040 | bytes 7608320 | tf_op jit(solution)/shard_map/dot_general | solution.py:87
  77.7 8.2 %collective-permute-done.10 = bf16[256,2048]{1,0:T(8,128)(2,1)S(1)} collective-permute-done((bf16[256,2048]{1,0:T(8,128)(2,1)S(1)}, bf16[256,2048]{1,0:T(8,128)(2,1)S(1)}, u32[]{:S(2)}, u32[]{:S(2)}) %collective-permute-start.10) | collective-permute-done | bytes 1048608 | tf_op jit(solution)/shard_map/ppermute | solution.py:40
  85.8 1.6 %multiply_reduce_fusion.12 = (f32[1280]{0:T(1024)S(1)}, f32[256,1280]{1,0:T(8,128)S(1)}) fusion(f32[256]{0:T(256)S(1)} %bitcast.101, bf16[256,2048]{1,0:T(8,128)(2,1)S(1)} %collective-permute-done.10, bf16[1280,2048]{1,0:T(8,128)(2,1)S(1)} %bitcast.76), kind=kOutput, calls=%fused_computation.38 | convolution fusion | flops 1343159040 | bytes 7608320 | tf_op jit(solution)/shard_map/dot_general | solution.py:87
  87.4 1.6 %multiply_reduce_fusion.11 = (f32[1280]{0:T(1024)S(1)}, f32[256,1280]{1,0:T(8,128)S(1)}) fusion(f32[256]{0:T(256)S(1)} %bitcast.100, bf16[256,2048]{1,0:T(8,128)(2,1)S(1)} %collective-permute-done.6, bf16[1280,2048]{1,0:T(8,128)(2,1)S(1)} %bitcast.76), kind=kOutput, calls=%fused_computation.37 | convolution fusion | flops 1343159040 | bytes 7608320 | tf_op jit(solution)/shard_map/dot_general | solution.py:87
  89.1 4.2 %collective-permute-start.11 = (f32[1408]{0:T(1024)S(1)}, f32[1408]{0:T(1024)S(1)}, u32[]{:S(2)}, u32[]{:S(2)}) collective-permute-start(f32[1408]{0:T(1024)S(1)} %concatenate.40), channel_id=1, source_target_pairs={{0,1},{1,0},{2,3},{3,2},{4,5},{5,4},{6,7},{7,6},{8,9},{9,8},{10,11... | collective-permute-start | bytes 16904 | tf_op jit(solution)/shard_map/ppermute | solution.py:44
  93.3 0.8 collective-permute-done.11
  94.2 1.0 multiply_reduce_fusion.10
  95.2 3.0 %multiply_reduce_fusion.9 = (f32[1280]{0:T(1024)S(1)}, f32[1280]{0:T(1024)S(1)}, f32[1280]{0:T(1024)S(1)}, f32[1280]{0:T(1024)S(1)}, f32[1280]{0:T(1024)S(1)}, /*index=5*/f32[1280]{0:T(1024)S(1)}) fusion(f32[256,1280]{1,0:T(8,128)S(1)} %get-tuple-element.92, f32[256]{0:T(256)S(1)} %bitcast.92, f32[256]{0:T(256)S(1)} %bitcast.93, f32[1280]{0:T(1024)S(1)} %fusion.24, ...), kind=kLoop, calls=%fused_computation.35 | loop fusion | flops 13754880 | bytes 7912448 | tf_op jit(solution)/shard_map/reduce_sum | solution.py:198
  98.2 0.4 collective-permute-start.12
  98.7 0.5 slice.160
  99.2 0.3 collective-permute-done.12
  99.5 0.7 fusion.26
  100.2 0.9 fusion.2
  101.1 0.6 reduce_max.9
  102.5 0.1 pad.10.clone
  102.6 3.3 %multiply_convert_fusion = f16[1024,512]{1,0:T(8,128)(2,1)S(1)} fusion(bf16[1024,1280]{1,0:T(8,128)(2,1)} %fusion.1, bf16[512,1280]{1,0:T(8,128)(2,1)S(1)} %get-tuple-element.24, f32[]{:T(128)S(6)} %exp2.15), kind=kOutput, calls=%fused_computation.23 | convolution fusion | flops 1343225856 | bytes 4980740 | tf_op jit(solution)/shard_map/dot_general | solution.py:87
  105.9 0.1 maximum_maximum_fusion
  106.0 0.3 pad_maximum_fusion.2
  106.3 23.4 %all_to_all.15 = f16[16,72,512]{2,1,0:T(8,128)(2,1)S(1)} all-to-all(f16[16,72,512]{2,1,0:T(8,128)(2,1)S(1)} %pad_maximum_fusion.2), channel_id=1, replica_groups=mesh['group'=2,'fsdp_0'=2,'fsdp_1'=8,'fsdp_2'=4,'fsdp_3'=2] {'group','fs..., dimensions={0} | all-to-all | bytes 2359296 | tf_op jit(solution)/shard_map/all_to_all | solution.py:219
  129.7 0.2 fusion.29
  129.9 0.1 fusion.12
  130.0 0.3 multiply_reduce_fusion.2
  130.3 13.2 %all_to_all.16 = f32[8,8,640]{2,1,0:T(8,128)S(1)} all-to-all(f32[8,8,640]{2,1,0:T(8,128)S(1)} %pad_maximum_fusion.3), channel_id=1, replica_groups=mesh['group'=2,'fsdp_0'=2,'fsdp_1'=8,'fsdp_2'=4,'fsdp_3'=2] {'fsdp_1'}, dimensions={0} | all-to-all | bytes 327680 | tf_op jit(solution)/shard_map/all_to_all | solution.py:228
  143.6 5.2 %collective-permute-start.13 = (f32[8,640]{1,0:T(8,128)S(1)}, f32[8,640]{1,0:T(8,128)S(1)}, u32[]{:S(2)}, u32[]{:S(2)}) collective-permute-start(f32[8,640]{1,0:T(8,128)S(1)} %reduce_sum.229), channel_id=1, source_target_pairs={{0,0},{1,128},{128,1},{129,129},{2,2},{3,130},{130,3},{131,131},{4... | collective-permute-start | bytes 61448 | tf_op jit(solution)/shard_map/ppermute | solution.py:230
  148.8 0.1 collective-permute-start.14
  148.9 1.3 collective-permute-done.13
  150.3 2.8 %collective-permute-done.14 = f32[8,640]{1,0:T(8,128)S(1)} collective-permute-done((f32[8,640]{1,0:T(8,128)S(1)}, f32[8,640]{1,0:T(8,128)S(1)}, u32[]{:S(2)}, u32[]{:S(2)}) %collective-permute-start.14) | collective-permute-done | bytes 20512 | tf_op jit(solution)/shard_map/ppermute | solution.py:230
  153.1 0.6 fusion.41
  153.7 0.6 pad_maximum_fusion.4
  (76 shorter events, 0.8 us)
Async XLA Ops:
  0.6 39.7 %copy-start = (bf16[1024,1024]{1,0:T(8,128)(2,1)S(1)}, bf16[1024,1024]{1,0:T(8,128)(2,1)}, u32[]{:S(2)}) copy-start(bf16[1024,1024]{1,0:T(8,128)(2,1)} %param.19) | copy-start | bytes 6291460
  0.6 12.1 %copy-start.8 = (s32[4]{0:T(128)S(1)}, s32[4]{0:T(128)}, u32[]{:S(2)}) copy-start(s32[4]{0:T(128)} %constant.95.clone) | copy-start | bytes 52
  0.7 12.0 %copy-start.3 = (f32[4096]{0:T(1024)S(1)}, f32[4096]{0:T(1024)}, u32[]{:S(2)}) copy-start(f32[4096]{0:T(1024)} %param.18) | copy-start | bytes 49156
  0.7 12.0 %copy-start.4 = (f32[4096]{0:T(1024)S(1)}, f32[4096]{0:T(1024)}, u32[]{:S(2)}) copy-start(f32[4096]{0:T(1024)} %param.17) | copy-start | bytes 49156
  0.7 12.0 %copy-start.5 = (f32[4096]{0:T(1024)S(1)}, f32[4096]{0:T(1024)}, u32[]{:S(2)}) copy-start(f32[4096]{0:T(1024)} %param.16) | copy-start | bytes 49156
  0.7 13.7 %copy-start.6 = (f32[1024]{0:T(1024)S(1)}, f32[1024]{0:T(1024)}, u32[]{:S(2)}) copy-start(f32[1024]{0:T(1024)} %param.21) | copy-start | bytes 12292
  0.7 13.8 %copy-start.7 = (f32[1024]{0:T(1024)S(1)}, f32[1024]{0:T(1024)}, u32[]{:S(2)}) copy-start(f32[1024]{0:T(1024)} %param.20) | copy-start | bytes 12292
  2.6 27.0 %all-to-all-start = ((bf16[8,16,2048]{2,1,0:T(8,128)(2,1)}), bf16[8,16,2048]{2,1,0:T(8,128)(2,1)S(1)}, u32[]{:S(2)}, u32[]{:S(2)}) async-start(bf16[8,16,2048]{2,1,0:T(8,128)(2,1)} %broadcast_in_dim.12), calls=%async_computation | async-start | bytes 1048576 | tf_op jit(solution)/shard_map/all_to_all | solution.py:115
  11.6 11.2 %collective-permute-start = (bf16[640,2048]{1,0:T(8,128)(2,1)}, bf16[640,2048]{1,0:T(8,128)(2,1)}, u32[]{:S(2)}, u32[]{:S(2)}) collective-permute-start(bf16[640,2048]{1,0:T(8,128)(2,1)} %param.12), channel_id=1, source_target_pairs={{0,1},{1,0},{2,3},{3,2},{4,5},{5,4},{6,7},{7,6},{8,9},{9,8},{10,11... | collective-permute-start | bytes 7864328 | tf_op jit(solution)/shard_map/ppermute | solution.py:44
  12.5 6.8 %collective-permute-start.1 = (bf16[640,1024]{1,0:T(8,128)(2,1)}, bf16[640,1024]{1,0:T(8,128)(2,1)}, u32[]{:S(2)}, u32[]{:S(2)}) collective-permute-start(bf16[640,1024]{1,0:T(8,128)(2,1)} %param.13), channel_id=1, source_target_pairs={{0,1},{1,0},{2,3},{3,2},{4,5},{5,4},{6,7},{7,6},{8,9},{9,8},{10,11... | collective-permute-start | bytes 3932168 | tf_op jit(solution)/shard_map/ppermute | solution.py:44
  15.6 7.1 %copy-start.1 = (bf16[640,2048]{1,0:T(8,128)(2,1)S(1)}, bf16[640,2048]{1,0:T(8,128)(2,1)}, u32[]{:S(2)}) copy-start(bf16[640,2048]{1,0:T(8,128)(2,1)} %param.12) | copy-start | bytes 7864324
  29.5 6.3 %copy-start.2 = (bf16[1280,1024]{1,0:T(8,128)(2,1)S(1)}, bf16[1280,1024]{1,0:T(8,128)(2,1)}, u32[]{:S(2)}) copy-start(bf16[1280,1024]{1,0:T(8,128)(2,1)} %pad_maximum_fusion.1) | copy-start | bytes 7864324
  29.5 17.6 %collective-permute-start.2 = (bf16[128,2048]{1,0:T(8,128)(2,1)S(1)}, bf16[128,2048]{1,0:T(8,128)(2,1)S(1)}, u32[]{:S(2)}, u32[]{:S(2)}) collective-permute-start(bf16[128,2048]{1,0:T(8,128)(2,1)S(1)} %bitcast.72), channel_id=1, source_target_pairs={{0,6},{1,193},{2,0},{3,195},{4,2},{5,197},{6,4},{7,199},{8,14},{9,... | collective-permute-start | bytes 1572872 | tf_op jit(solution)/shard_map/ppermute | solution.py:40
  32.3 10.2 %collective-permute-start.3 = (bf16[128,2048]{1,0:T(8,128)(2,1)S(1)}, bf16[128,2048]{1,0:T(8,128)(2,1)S(1)}, u32[]{:S(2)}, u32[]{:S(2)}) collective-permute-start(bf16[128,2048]{1,0:T(8,128)(2,1)S(1)} %bitcast.73), channel_id=1, source_target_pairs={{0,2},{1,65},{2,4},{3,67},{4,6},{5,69},{6,0},{7,71},{8,10},{9,73},... | collective-permute-start | bytes 1572872 | tf_op jit(solution)/shard_map/ppermute | solution.py:40
  32.3 13.3 %slice-start = ((s8[5242880]{0:T(1024)(128)(4,1)}), s8[4194304]{0:T(1024)(128)(4,1)S(1)}, s32[]{:S(2)}) async-start(s8[5242880]{0:T(1024)(128)(4,1)} %bitcast.75), calls=%async_computation.3 | async-start | bytes 8388608
  35.8 9.7 %slice-start.1 = ((s8[5242880]{0:T(1024)(128)(4,1)}), s8[1048576]{0:T(1024)(128)(4,1)S(1)}, s32[]{:S(2)}) async-start(s8[5242880]{0:T(1024)(128)(4,1)} %bitcast.75), calls=%async_computation.4 | async-start | bytes 2097152
  42.5 20.8 %collective-permute-start.7 = (bf16[256,2048]{1,0:T(8,128)(2,1)S(1)}, bf16[256,2048]{1,0:T(8,128)(2,1)S(1)}, u32[]{:S(2)}, u32[]{:S(2)}) collective-permute-start(bf16[256,2048]{1,0:T(8,128)(2,1)S(1)} %join.3), channel_id=1, source_target_pairs={{0,64},{1,3},{2,66},{3,5},{4,68},{5,7},{6,70},{7,1},{8,72},{9,11},... | collective-permute-start | bytes 3145736 | tf_op jit(solution)/shard_map/ppermute | solution.py:40
  43.8 15.2 %collective-permute-start.4 = (bf16[128,2048]{1,0:T(8,128)(2,1)S(1)}, bf16[128,2048]{1,0:T(8,128)(2,1)S(1)}, u32[]{:S(2)}, u32[]{:S(2)}) collective-permute-start(bf16[128,2048]{1,0:T(8,128)(2,1)S(1)} %collective-permute-done.3.refs_1_), channel_id=1, source_target_pairs={{0,2},{1,65},{2,4},{3,67},{4,6},{5,69},{6,0},{7,71},{8,10},{9,73},... | collective-permute-start | bytes 1572872 | tf_op jit(solution)/shard_map/ppermute | solution.py:40
  43.8 21.2 %collective-permute-start.9 = (bf16[256,2048]{1,0:T(8,128)(2,1)S(1)}, bf16[256,2048]{1,0:T(8,128)(2,1)S(1)}, u32[]{:S(2)}, u32[]{:S(2)}) collective-permute-start(bf16[256,2048]{1,0:T(8,128)(2,1)S(1)} %join.3), channel_id=1, source_target_pairs={{0,192},{1,7},{2,194},{3,1},{4,196},{5,3},{6,198},{7,5},{8,200},{9... | collective-permute-start | bytes 3145736 | tf_op jit(solution)/shard_map/ppermute | solution.py:40
  59.0 14.0 %collective-permute-start.5 = (bf16[256,2048]{1,0:T(8,128)(2,1)S(1)}, bf16[256,2048]{1,0:T(8,128)(2,1)S(1)}, u32[]{:S(2)}, u32[]{:S(2)}) collective-permute-start(bf16[256,2048]{1,0:T(8,128)(2,1)S(1)} %join.2), channel_id=1, source_target_pairs={{0,192},{1,7},{2,194},{3,1},{4,196},{5,3},{6,198},{7,5},{8,200},{9... | collective-permute-start | bytes 3145736 | tf_op jit(solution)/shard_map/ppermute | solution.py:40
  59.3 16.8 %collective-permute-start.8 = (bf16[256,2048]{1,0:T(8,128)(2,1)S(1)}, bf16[256,2048]{1,0:T(8,128)(2,1)S(1)}, u32[]{:S(2)}, u32[]{:S(2)}) collective-permute-start(bf16[256,2048]{1,0:T(8,128)(2,1)S(1)} %join.2), channel_id=1, source_target_pairs={{0,64},{1,3},{2,66},{3,5},{4,68},{5,7},{6,70},{7,1},{8,72},{9,11},... | collective-permute-start | bytes 3145736 | tf_op jit(solution)/shard_map/ppermute | solution.py:40
  63.4 22.5 %collective-permute-start.10 = (bf16[256,2048]{1,0:T(8,128)(2,1)S(1)}, bf16[256,2048]{1,0:T(8,128)(2,1)S(1)}, u32[]{:S(2)}, u32[]{:S(2)}) collective-permute-start(bf16[256,2048]{1,0:T(8,128)(2,1)S(1)} %collective-permute-done.7), channel_id=1, source_target_pairs={{0,64},{1,3},{2,66},{3,5},{4,68},{5,7},{6,70},{7,1},{8,72},{9,11},... | collective-permute-start | bytes 3145736 | tf_op jit(solution)/shard_map/ppermute | solution.py:40
  73.1 14.4 %collective-permute-start.6 = (bf16[256,2048]{1,0:T(8,128)(2,1)S(1)}, bf16[256,2048]{1,0:T(8,128)(2,1)S(1)}, u32[]{:S(2)}, u32[]{:S(2)}) collective-permute-start(bf16[256,2048]{1,0:T(8,128)(2,1)S(1)} %collective-permute-done.5), channel_id=1, source_target_pairs={{0,192},{1,7},{2,194},{3,1},{4,196},{5,3},{6,198},{7,5},{8,200},{9... | collective-permute-start | bytes 3145736 | tf_op jit(solution)/shard_map/ppermute | solution.py:40
  89.1 5.0 %collective-permute-start.11 = (f32[1408]{0:T(1024)S(1)}, f32[1408]{0:T(1024)S(1)}, u32[]{:S(2)}, u32[]{:S(2)}) collective-permute-start(f32[1408]{0:T(1024)S(1)} %concatenate.40), channel_id=1, source_target_pairs={{0,1},{1,0},{2,3},{3,2},{4,5},{5,4},{6,7},{7,6},{8,9},{9,8},{10,11... | collective-permute-start | bytes 16904 | tf_op jit(solution)/shard_map/ppermute | solution.py:44
  98.2 1.3 collective-permute-start.12
  143.6 6.7 %collective-permute-start.13 = (f32[8,640]{1,0:T(8,128)S(1)}, f32[8,640]{1,0:T(8,128)S(1)}, u32[]{:S(2)}, u32[]{:S(2)}) collective-permute-start(f32[8,640]{1,0:T(8,128)S(1)} %reduce_sum.229), channel_id=1, source_target_pairs={{0,0},{1,128},{128,1},{129,129},{2,2},{3,130},{130,3},{131,131},{4... | collective-permute-start | bytes 61448 | tf_op jit(solution)/shard_map/ppermute | solution.py:230
  148.8 4.2 %collective-permute-start.14 = (f32[8,640]{1,0:T(8,128)S(1)}, f32[8,640]{1,0:T(8,128)S(1)}, u32[]{:S(2)}, u32[]{:S(2)}) collective-permute-start(f32[8,640]{1,0:T(8,128)S(1)} %reduce_sum.229), channel_id=1, source_target_pairs={{0,128},{1,0},{128,129},{129,1},{2,130},{3,2},{130,131},{131,3},{4... | collective-permute-start | bytes 61448 | tf_op jit(solution)/shard_map/ppermute | solution.py:230

commit v4 on v3

--- a/solution.py
+++ b/solution.py
@@ -64,8 +64,10 @@
 
 
 def ring_gather(block, dims):
+    half = block.shape[0] // 2
     left, right = shift(block, dims, 1), shift(block, dims, -1)
-    return block, left, right, shift(left, dims, 1)
+    far = shift(left[:half], dims, 1), shift(right[half:], dims, -1)
+    return block, left, right, *far
 
 
 def wide_gather(first, second, dims):
@@ -153,22 +155,13 @@
     cross = lax.dot_general(
         cross_half, s_rows, (((0,), (1,)), ((), ())), preferred_element_type=jnp.float32
     ) + cross_bias_half[:, None]
-    inputs = transposed_dot(
-        one_hot_rows(cut + jnp.arange(half_s, dtype=jnp.int32), width_s, s_rows.dtype), s_rows
-    ).astype(s_rows.dtype)
+    flipped = lax.optimization_barrier(s_rows.T)
+    inputs = lax.dynamic_slice_in_dim(flipped, cut, half_s, axis=0)
     mixed = inputs.astype(jnp.float32) * cross + inputs.astype(jnp.float32)
     student_part = jnp.sum(mixed * out_half[:, None], axis=0)
 
-    features = (
-        jnp.arange(2, dtype=jnp.int32)[:, None, None, None, None] * 8
-        + jnp.arange(2, dtype=jnp.int32)[:, None, None, None] * (8 * 4 * 16)
-        + jnp.arange(4, dtype=jnp.int32)[:, None, None] * 16
-        + jnp.arange(8, dtype=jnp.int32)[:, None] * (4 * 16)
-        + jnp.arange(8, dtype=jnp.int32)
-    ).reshape(-1)
-    turned = transposed_dot(one_hot_rows(features, width_s, s_rows.dtype), s_rows).astype(
-        s_rows.dtype
-    )
+    turned = flipped.reshape(2, 8, 4, 2, 8, -1).transpose(3, 0, 2, 1, 4, 5)
+    turned = turned.reshape(flipped.shape)
     blocks = wide_gather(*plane, wide)
     last, inputs, mixed, student_part, turned = lax.optimization_barrier(
         (blocks[3][1], inputs, mixed, student_part, turned)
@@ -208,11 +201,11 @@
 
     dcross_half, reach, small = lax.optimization_barrier((dcross_half, reach, small))
     parts = transposed_dot(turned, dcross_half)
-    power = power_for(jnp.max(reach))
+    power = power_for(jnp.max(reach, keepdims=True))[:, None]
     scaled = small * jnp.exp2(power)
     top = scaled.astype(jnp.float16)
     low = (scaled - top.astype(jnp.float32)).astype(jnp.float16)
-    powers = jnp.broadcast_to(power.astype(jnp.float16), (4, half_s))
+    powers = jnp.broadcast_to(power, (4, half_s)).astype(jnp.float16)
     tail = jnp.concatenate([top, low, powers], axis=0)
     parts = (parts * jnp.exp2(power)).astype(jnp.float16).reshape(16, -1, half_s)
     parts = jnp.concatenate([parts, jnp.broadcast_to(tail, (16, *tail.shape))], axis=1)

time: 155 us -> 153 us (0.987)
  matrix products: 27.5 us -> 21.3 us
  local copies, waits for them, and re-layouts: 3.62 us -> 7.77 us
  starting transfers between devices: 28.8 us -> 32.8 us
  waiting for transfers between devices: 38.2 us -> 36.6 us
    dot_general x11 -> x9, matrix products: 24 us -> 15.9 us  [transposed_dot(): lax.dot_general(left, right, (((1,), (1,)), ((), ())), preferred_element_...]
    ppermute x9 -> x10, starting transfers between devices: 8.82 us -> 13 us  [shift(): return lax.ppermute(value, GROUP_FSDP, shift_pairs(dims, step))]
    ppermute x4, waiting for transfers between devices: 4.78 us -> 1.56 us  [swap_cores(): return lax.ppermute(value, 'fsdp_3', ((0, 1), (1, 0)))]
    all_to_all x1, starting transfers between devices: 9 us -> 6.48 us  [shards(): lax.all_to_all(jnp.broadcast_to(mine[None], (8, *mine.shape)), 'fsdp_1',...]
    unnamed x23 -> x24, local copies, waits for them, and re-layouts: 0.06 us -> 2.53 us
    all_to_all x1, blocking collectives: 13.2 us -> 11 us  [shards(): parts = lax.all_to_all(parts, 'fsdp_1', 0, 0, tiled=True).sum(axis=0)]
    ppermute x4, starting transfers between devices: 5.7 us -> 7.96 us  [swap_cores(): return lax.ppermute(value, 'fsdp_3', ((0, 1), (1, 0)))]
    dot_general x1, matrix products: 2.11 us -> 4.08 us  [shards(): lax.dot_general(cross_half, s_rows, (((0,), (1,)), ((), ())), preferred_e...]
  transfers between devices with their start and end apart: 16 -> 17, of which waited for: 10 -> 12; matrix products, arithmetic and copies ran while one was open for 21% -> 21% of each run, Pallas kernels for 0% -> 0%
where the time goes in v4:
time: 153 us
  waiting for transfers between devices  36.6 us (24%)
  blocking collectives  35.2 us (23%)
  starting transfers between devices  32.8 us (21%)
  matrix products  21.3 us (14%)
  other arithmetic  16.6 us (11%)
  local copies, waits for them, and re-layouts  7.77 us (5%)
  between operations  2.53 us (2%)
    ppermute x10, waiting for transfers between devices, shift(): return lax.ppermute(value, GROUP_FSDP, shift_pairs(dims, step))  27.5 us
    all_to_all x1, blocking collectives, shards(): lax.all_to_all(parts, ('group', 'fsdp_0', 'fsdp_2'), 0, 0, tiled=True)  24.2 us
    dot_general x9, matrix products, transposed_dot(): lax.dot_general(left, right, (((1,), (1,)), ((), ())), preferred_element_...  15.9 us
    ppermute x10, starting transfers between devices, shift(): return lax.ppermute(value, GROUP_FSDP, shift_pairs(dims, step))  13 us
    all_to_all x1, blocking collectives, shards(): parts = lax.all_to_all(parts, 'fsdp_1', 0, 0, tiled=True).sum(axis=0)  11 us
    ppermute x4, starting transfers between devices, swap_cores(): return lax.ppermute(value, 'fsdp_3', ((0, 1), (1, 0)))  7.96 us
    all_to_all x1, starting transfers between devices, shards(): lax.all_to_all(jnp.broadcast_to(mine[None], (8, *mine.shape)), 'fsdp_1',...  6.48 us
    ppermute x2, starting transfers between devices, shards(): lax.ppermute(parts, ('group', 'fsdp_3'), pairs)  5.31 us
  transfers between devices with their start and end apart: 17, of which 12 were waited for; matrix products, arithmetic and copies ran while one was open for 21% of the time, Pallas kernels for 0%

profile of v4, /device:TPU:1, one launch (start us, length us, event | category | flops | bytes accessed | tf_op | source)
XLA Modules:
  0.0 152.9 jit_solution(4834373829599485181)
XLA Ops:
  0.6 3.3 %collective-permute-start = (bf16[640,2048]{1,0:T(8,128)(2,1)}, bf16[640,2048]{1,0:T(8,128)(2,1)}, u32[]{:S(2)}, u32[]{:S(2)}) collective-permute-start(bf16[640,2048]{1,0:T(8,128)(2,1)} %param.12), channel_id=1, source_target_pairs={{0,1},{1,0},{2,3},{3,2},{4,5},{5,4},{6,7},{7,6},{8,9},{9,8},{10,11... | collective-permute-start | bytes 7864328 | tf_op jit(solution)/shard_map/ppermute | solution.py:44
  3.9 1.7 %broadcast_in_dim.12 = bf16[8,16,2048]{2,1,0:T(8,128)(2,1)} broadcast(bf16[16,2048]{1,0:T(8,128)(2,1)} %bitcast.84), dimensions={1,2} | broadcast | bytes 589824 | tf_op jit(solution)/shard_map/broadcast_in_dim | solution.py:118
  5.7 6.5 %all-to-all-start = ((bf16[8,16,2048]{2,1,0:T(8,128)(2,1)}), bf16[8,16,2048]{2,1,0:T(8,128)(2,1)S(1)}, u32[]{:S(2)}, u32[]{:S(2)}) async-start(bf16[8,16,2048]{2,1,0:T(8,128)(2,1)} %broadcast_in_dim.12), calls=%async_computation | async-start | bytes 1048576 | tf_op jit(solution)/shard_map/all_to_all | solution.py:117
  12.2 2.5 %copy.38 = bf16[640,1024]{0,1:T(8,128)(2,1)} copy(bf16[640,1024]{1,0:T(8,128)(2,1)} %param.13) | data formatting | bytes 2621440 | tf_op args[1]
  14.7 0.4 collective-permute-start.1
  15.2 0.1 add_add_fusion.1
  15.4 0.1 add.313
  15.4 0.2 convolution_bitcast_fusion
  15.7 1.1 fusion.3
  16.9 0.1 dynamic_slice.15
  17.7 0.4 collective-permute-done.1
  18.1 3.7 %pad_maximum_fusion.1 = bf16[1280,1024]{0,1:T(8,128)(2,1)} fusion(bf16[640,1024]{0,1:T(8,128)(2,1)} %collective-permute-done.1, bf16[640,1024]{0,1:T(8,128)(2,1)} %copy.38), kind=kLoop, calls=%fused_computation.11 | loop fusion | flops 5242880 | bytes 5242880 | tf_op jit(solution)/shard_map/concatenate | solution.py:122
  21.8 4.8 %pad_maximum_fusion = bf16[1280,2048]{1,0:T(8,128)(2,1)} fusion(bf16[640,2048]{1,0:T(8,128)(2,1)} %collective-permute-done, bf16[640,2048]{1,0:T(8,128)(2,1)S(1)} %copy-done.2), kind=kLoop, calls=%fused_computation | loop fusion | flops 10485760 | bytes 10485760 | tf_op jit(solution)/shard_map/concatenate | solution.py:121
  26.6 3.5 %all-to-all-done = bf16[8,16,2048]{2,1,0:T(8,128)(2,1)S(1)} async-done(((bf16[8,16,2048]{2,1,0:T(8,128)(2,1)}), bf16[8,16,2048]{2,1,0:T(8,128)(2,1)S(1)}, u32[]{:S(2)}, u32[]{:S(2)}) %all-to-all-start) | async-done | bytes 524320 | tf_op jit(solution)/shard_map/all_to_all | solution.py:117
  30.1 2.7 %collective-permute-start.2 = (bf16[128,2048]{1,0:T(8,128)(2,1)S(1)}, bf16[128,2048]{1,0:T(8,128)(2,1)S(1)}, u32[]{:S(2)}, u32[]{:S(2)}) collective-permute-start(bf16[128,2048]{1,0:T(8,128)(2,1)S(1)} %bitcast.73), channel_id=1, source_target_pairs={{0,6},{1,193},{2,0},{3,195},{4,2},{5,197},{6,4},{7,199},{8,14},{9,... | collective-permute-start | bytes 1572872 | tf_op jit(solution)/shard_map/ppermute | solution.py:40
  32.8 4.1 %multiply_reduce_fusion.1 = (f32[1280]{0:T(1024)S(1)}, f32[512,1280]{1,0:T(8,128)S(1)}) fusion(f32[512]{0:T(512)S(1)} %dynamic_slice.15, f32[512]{0:T(512)S(1)} %dynamic_slice.14, bf16[1280,1024]{0,1:T(8,128)(2,1)} %pad_maximum_fusion.1, bf16[1024,1024]{1,0:T(8,128)(2,1)S(1)} %copy-done, s32[]{:T(128)S(6)} %select_n.48, bf16[1024,1280]{1,0:T(8,128)(2,1)} %bitcast.76), kind=kOutput, calls=%fused_computation.17 | convolution fusion | flops 1346108160 | bytes 7612416 | tf_op jit(solution)/shard_map/dot_general | solution.py:155
  37.0 0.1 constant_dynamic-slice_fusion
  37.1 5.3 %collective-permute-done.3.refs_1_ = bf16[128,2048]{1,0:T(8,128)(2,1)S(1)} collective-permute-done((bf16[128,2048]{1,0:T(8,128)(2,1)S(1)}, bf16[128,2048]{1,0:T(8,128)(2,1)S(1)}, u32[]{:S(2)}, u32[]{:S(2)}) %collective-permute-start.3) | collective-permute-done | bytes 524320 | tf_op jit(solution)/shard_map/ppermute | solution.py:40
  42.4 1.0 collective-permute-start.8
  43.4 1.8 %copy.39 = bf16[2,8,4,2,8,1280]{5,4,1,2,0,3:T(8,128)(2,1)} copy(bf16[2,8,4,2,8,1280]{5,4,3,2,1,0:T(8,128)(2,1)S(1)} %bitcast.78) | data formatting | bytes 5242880 | tf_op jit(solution)/shard_map/reshape | solution.py:163
  45.2 1.8 %collective-permute-start.10 = (bf16[256,2048]{1,0:T(8,128)(2,1)S(1)}, bf16[256,2048]{1,0:T(8,128)(2,1)S(1)}, u32[]{:S(2)}, u32[]{:S(2)}) collective-permute-start(bf16[256,2048]{1,0:T(8,128)(2,1)S(1)} %join.3), channel_id=1, source_target_pairs={{0,192},{1,7},{2,194},{3,1},{4,196},{5,3},{6,198},{7,5},{8,200},{9... | collective-permute-start | bytes 3145736 | tf_op jit(solution)/shard_map/ppermute | solution.py:40
  47.0 0.1 collective-permute-start.4
  47.1 2.7 %collective-permute-start.5 = (bf16[64,2048]{1,0:T(8,128)(2,1)S(1)}, bf16[64,2048]{1,0:T(8,128)(2,1)S(1)}, u32[]{:S(2)}, u32[]{:S(2)}) collective-permute-start(bf16[64,2048]{1,0:T(8,128)(2,1)S(1)} %slice.169), channel_id=1, source_target_pairs={{0,6},{1,193},{2,0},{3,195},{4,2},{5,197},{6,4},{7,199},{8,14},{9,... | collective-permute-start | bytes 786440 | tf_op jit(solution)/shard_map/ppermute | solution.py:40
  49.9 1.6 %multiply_reduce_fusion.18 = (f32[1280]{0:T(1024)S(1)}, f32[256,1280]{1,0:T(8,128)S(1)}) fusion(f32[256]{0:T(256)S(1)} %bitcast.112, bf16[256,2048]{1,0:T(8,128)(2,1)S(1)} %join.3, bf16[1280,2048]{1,0:T(8,128)(2,1)S(1)} %bitcast.80), kind=kOutput, calls=%fused_computation.38 | convolution fusion | flops 1343159040 | bytes 7608320 | tf_op jit(solution)/shard_map/dot_general | solution.py:89
  51.4 5.2 %collective-permute-done.4.refs_1_ = bf16[64,2048]{1,0:T(8,128)(2,1)S(1)} collective-permute-done((bf16[64,2048]{1,0:T(8,128)(2,1)S(1)}, bf16[64,2048]{1,0:T(8,128)(2,1)S(1)}, u32[]{:S(2)}, u32[]{:S(2)}) %collective-permute-start.4) | collective-permute-done | bytes 262176 | tf_op jit(solution)/shard_map/ppermute | solution.py:40
  56.7 1.2 collective-permute-start.6
  57.9 0.5 collective-permute-start.9
  58.4 1.6 %multiply_reduce_fusion.17 = (f32[1280]{0:T(1024)S(1)}, f32[256,1280]{1,0:T(8,128)S(1)}) fusion(f32[256]{0:T(256)S(1)} %bitcast.111, bf16[256,2048]{1,0:T(8,128)(2,1)S(1)} %join.2, bf16[1280,2048]{1,0:T(8,128)(2,1)S(1)} %bitcast.80), kind=kOutput, calls=%fused_computation.37 | convolution fusion | flops 1343159040 | bytes 7608320 | tf_op jit(solution)/shard_map/dot_general | solution.py:89
  60.0 0.5 collective-permute-done.8
  60.5 1.6 %multiply_reduce_fusion.16 = (f32[1280]{0:T(1024)S(1)}, f32[256,1280]{1,0:T(8,128)S(1)}) fusion(f32[256]{0:T(256)S(1)} %bitcast.110, bf16[256,2048]{1,0:T(8,128)(2,1)S(1)} %collective-permute-done.8, bf16[1280,2048]{1,0:T(8,128)(2,1)S(1)} %bitcast.80), kind=kOutput, calls=%fused_computation.36 | convolution fusion | flops 1343159040 | bytes 7608320 | tf_op jit(solution)/shard_map/dot_general | solution.py:89
  62.1 1.6 %multiply_reduce_fusion.14 = (f32[1280]{0:T(1024)S(1)}, f32[256,1280]{1,0:T(8,128)S(1)}) fusion(f32[256]{0:T(256)S(1)} %bitcast.109, bf16[256,2048]{1,0:T(8,128)(2,1)S(1)} %collective-permute-done.10, bf16[1280,2048]{1,0:T(8,128)(2,1)S(1)} %bitcast.80), kind=kOutput, calls=%fused_computation.34 | convolution fusion | flops 1343159040 | bytes 7608320 | tf_op jit(solution)/shard_map/dot_general | solution.py:89
  63.7 9.5 %collective-permute-done.6 = bf16[256,2048]{1,0:T(8,128)(2,1)S(1)} collective-permute-done((bf16[256,2048]{1,0:T(8,128)(2,1)S(1)}, bf16[256,2048]{1,0:T(8,128)(2,1)S(1)}, u32[]{:S(2)}, u32[]{:S(2)}) %collective-permute-start.6) | collective-permute-done | bytes 1048608 | tf_op jit(solution)/shard_map/ppermute | solution.py:40
  73.2 3.0 %collective-permute-start.7 = (bf16[256,2048]{1,0:T(8,128)(2,1)S(1)}, bf16[256,2048]{1,0:T(8,128)(2,1)S(1)}, u32[]{:S(2)}, u32[]{:S(2)}) collective-permute-start(bf16[256,2048]{1,0:T(8,128)(2,1)S(1)} %collective-permute-done.6), channel_id=1, source_target_pairs={{0,192},{1,7},{2,194},{3,1},{4,196},{5,3},{6,198},{7,5},{8,200},{9... | collective-permute-start | bytes 3145736 | tf_op jit(solution)/shard_map/ppermute | solution.py:40
  76.2 1.6 %multiply_reduce_fusion.13 = (f32[1280]{0:T(1024)S(1)}, f32[256,1280]{1,0:T(8,128)S(1)}) fusion(f32[256]{0:T(256)S(1)} %bitcast.107, bf16[256,2048]{1,0:T(8,128)(2,1)S(1)} %collective-permute-done.6, bf16[1280,2048]{1,0:T(8,128)(2,1)S(1)} %bitcast.80), kind=kOutput, calls=%fused_computation.33 | convolution fusion | flops 1343159040 | bytes 7608320 | tf_op jit(solution)/shard_map/dot_general | solution.py:89
  77.8 1.6 %multiply_reduce_fusion.15 = (f32[1280]{0:T(1024)S(1)}, f32[256,1280]{1,0:T(8,128)S(1)}) fusion(f32[256]{0:T(256)S(1)} %bitcast.108, bf16[256,2048]{1,0:T(8,128)(2,1)S(1)} %collective-permute-done.9, bf16[1280,2048]{1,0:T(8,128)(2,1)S(1)} %bitcast.80), kind=kOutput, calls=%fused_computation.35 | convolution fusion | flops 1343159040 | bytes 7608320 | tf_op jit(solution)/shard_map/dot_general | solution.py:89
  79.3 5.0 %collective-permute-done.11 = bf16[256,2048]{1,0:T(8,128)(2,1)S(1)} collective-permute-done((bf16[256,2048]{1,0:T(8,128)(2,1)S(1)}, bf16[256,2048]{1,0:T(8,128)(2,1)S(1)}, u32[]{:S(2)}, u32[]{:S(2)}) %collective-permute-start.11) | collective-permute-done | bytes 1048608 | tf_op jit(solution)/shard_map/ppermute | solution.py:40
  84.3 1.6 %multiply_reduce_fusion.12 = (f32[1280]{0:T(1024)S(1)}, f32[256,1280]{1,0:T(8,128)S(1)}) fusion(f32[256]{0:T(256)S(1)} %bitcast.106, bf16[256,2048]{1,0:T(8,128)(2,1)S(1)} %collective-permute-done.11, bf16[1280,2048]{1,0:T(8,128)(2,1)S(1)} %bitcast.80), kind=kOutput, calls=%fused_computation.32 | convolution fusion | flops 1343159040 | bytes 7608320 | tf_op jit(solution)/shard_map/dot_general | solution.py:89
  85.9 2.0 %collective-permute-done.7 = bf16[256,2048]{1,0:T(8,128)(2,1)S(1)} collective-permute-done((bf16[256,2048]{1,0:T(8,128)(2,1)S(1)}, bf16[256,2048]{1,0:T(8,128)(2,1)S(1)}, u32[]{:S(2)}, u32[]{:S(2)}) %collective-permute-start.7) | collective-permute-done | bytes 1048608 | tf_op jit(solution)/shard_map/ppermute | solution.py:40
  87.9 1.6 %multiply_reduce_fusion.11 = (f32[1280]{0:T(1024)S(1)}, f32[256,1280]{1,0:T(8,128)S(1)}) fusion(f32[256]{0:T(256)S(1)} %bitcast.105, bf16[256,2048]{1,0:T(8,128)(2,1)S(1)} %collective-permute-done.7, bf16[1280,2048]{1,0:T(8,128)(2,1)S(1)} %bitcast.80), kind=kOutput, calls=%fused_computation.31 | convolution fusion | flops 1343159040 | bytes 7608320 | tf_op jit(solution)/shard_map/dot_general | solution.py:89
  89.5 3.8 %collective-permute-start.12 = (f32[1408]{0:T(1024)S(1)}, f32[1408]{0:T(1024)S(1)}, u32[]{:S(2)}, u32[]{:S(2)}) collective-permute-start(f32[1408]{0:T(1024)S(1)} %concatenate.40), channel_id=1, source_target_pairs={{0,1},{1,0},{2,3},{3,2},{4,5},{5,4},{6,7},{7,6},{8,9},{9,8},{10,11... | collective-permute-start | bytes 16904 | tf_op jit(solution)/shard_map/ppermute | solution.py:44
  93.4 0.8 collective-permute-done.12
  94.2 1.0 multiply_reduce_fusion.10
  95.2 3.0 %multiply_reduce_fusion.9 = (f32[1280]{0:T(1024)S(1)}, f32[1280]{0:T(1024)S(1)}, f32[1280]{0:T(1024)S(1)}, f32[1280]{0:T(1024)S(1)}, f32[1280]{0:T(1024)S(1)}, /*index=5*/f32[1280]{0:T(1024)S(1)}) fusion(f32[256,1280]{1,0:T(8,128)S(1)} %get-tuple-element.92, f32[256]{0:T(256)S(1)} %bitcast.97, f32[256]{0:T(256)S(1)} %bitcast.98, f32[1280]{0:T(1024)S(1)} %fusion.20, ...), kind=kLoop, calls=%fused_computation.29 | loop fusion | flops 13754880 | bytes 7912448 | tf_op jit(solution)/shard_map/reduce_sum | solution.py:191
  98.2 0.4 collective-permute-start.13
  98.7 0.5 slice.170
  99.2 0.3 collective-permute-done.13
  99.5 0.7 fusion.22
  100.2 0.9 fusion
  101.1 0.6 reduce_max.9
  102.5 0.1 pad.10.clone
  102.6 3.3 %multiply_convert_fusion = f16[1024,512]{1,0:T(8,128)(2,1)S(1)} fusion(bf16[1024,1280]{1,0:T(8,128)(2,1)} %bitcast.81, bf16[512,1280]{1,0:T(8,128)(2,1)S(1)} %get-tuple-element.24, f32[]{:T(128)S(6)} %exp2.21), kind=kOutput, calls=%fused_computation.19 | convolution fusion | flops 1343225856 | bytes 4980740 | tf_op jit(solution)/shard_map/dot_general | solution.py:89
  105.9 0.1 maximum_maximum_fusion
  106.0 0.3 pad_maximum_fusion.2
  106.3 24.2 %all_to_all.15 = f16[16,72,512]{2,1,0:T(8,128)(2,1)S(1)} all-to-all(f16[16,72,512]{2,1,0:T(8,128)(2,1)S(1)} %pad_maximum_fusion.2), channel_id=1, replica_groups=mesh['group'=2,'fsdp_0'=2,'fsdp_1'=8,'fsdp_2'=4,'fsdp_3'=2] {'group','fs..., dimensions={0} | all-to-all | bytes 2359296 | tf_op jit(solution)/shard_map/all_to_all | solution.py:212
  130.5 0.2 fusion.25
  130.7 0.1 fusion.8
  130.8 0.3 multiply_reduce_fusion.2
  131.2 11.0 %all_to_all.16 = f32[8,8,640]{2,1,0:T(8,128)S(1)} all-to-all(f32[8,8,640]{2,1,0:T(8,128)S(1)} %pad_maximum_fusion.3), channel_id=1, replica_groups=mesh['group'=2,'fsdp_0'=2,'fsdp_1'=8,'fsdp_2'=4,'fsdp_3'=2] {'fsdp_1'}, dimensions={0} | all-to-all | bytes 327680 | tf_op jit(solution)/shard_map/all_to_all | solution.py:221
  142.1 5.2 %collective-permute-start.14 = (f32[8,640]{1,0:T(8,128)S(1)}, f32[8,640]{1,0:T(8,128)S(1)}, u32[]{:S(2)}, u32[]{:S(2)}) collective-permute-start(f32[8,640]{1,0:T(8,128)S(1)} %reduce_sum.229), channel_id=1, source_target_pairs={{0,0},{1,128},{128,1},{129,129},{2,2},{3,130},{130,3},{131,131},{4... | collective-permute-start | bytes 61448 | tf_op jit(solution)/shard_map/ppermute | solution.py:223
  147.4 0.1 collective-permute-start.15
  147.5 1.3 collective-permute-done.14
  148.8 2.8 %collective-permute-done.15 = f32[8,640]{1,0:T(8,128)S(1)} collective-permute-done((f32[8,640]{1,0:T(8,128)S(1)}, f32[8,640]{1,0:T(8,128)S(1)}, u32[]{:S(2)}, u32[]{:S(2)}) %collective-permute-start.15) | collective-permute-done | bytes 20512 | tf_op jit(solution)/shard_map/ppermute | solution.py:223
  151.7 0.6 fusion.37
  152.3 0.6 pad_maximum_fusion.4
  (72 shorter events, 0.8 us)
Async XLA Ops:
  0.6 32.2 %copy-start = (bf16[1024,1024]{1,0:T(8,128)(2,1)S(1)}, bf16[1024,1024]{1,0:T(8,128)(2,1)}, u32[]{:S(2)}) copy-start(bf16[1024,1024]{1,0:T(8,128)(2,1)} %param.19) | copy-start | bytes 6291460
  0.6 21.1 %collective-permute-start = (bf16[640,2048]{1,0:T(8,128)(2,1)}, bf16[640,2048]{1,0:T(8,128)(2,1)}, u32[]{:S(2)}, u32[]{:S(2)}) collective-permute-start(bf16[640,2048]{1,0:T(8,128)(2,1)} %param.12), channel_id=1, source_target_pairs={{0,1},{1,0},{2,3},{3,2},{4,5},{5,4},{6,7},{7,6},{8,9},{9,8},{10,11... | collective-permute-start | bytes 7864328 | tf_op jit(solution)/shard_map/ppermute | solution.py:44
  5.7 24.4 %all-to-all-start = ((bf16[8,16,2048]{2,1,0:T(8,128)(2,1)}), bf16[8,16,2048]{2,1,0:T(8,128)(2,1)S(1)}, u32[]{:S(2)}, u32[]{:S(2)}) async-start(bf16[8,16,2048]{2,1,0:T(8,128)(2,1)} %broadcast_in_dim.12), calls=%async_computation | async-start | bytes 1048576 | tf_op jit(solution)/shard_map/all_to_all | solution.py:117
  12.1 3.0 %copy-start.3 = (f32[4096]{0:T(1024)S(1)}, f32[4096]{0:T(1024)}, u32[]{:S(2)}) copy-start(f32[4096]{0:T(1024)} %param.18) | copy-start | bytes 49156
  12.1 3.0 %copy-start.4 = (f32[4096]{0:T(1024)S(1)}, f32[4096]{0:T(1024)}, u32[]{:S(2)}) copy-start(f32[4096]{0:T(1024)} %param.17) | copy-start | bytes 49156
  12.1 3.0 %copy-start.5 = (f32[4096]{0:T(1024)S(1)}, f32[4096]{0:T(1024)}, u32[]{:S(2)}) copy-start(f32[4096]{0:T(1024)} %param.16) | copy-start | bytes 49156
  12.2 3.0 %copy-start.8 = (s32[4]{0:T(128)S(1)}, s32[4]{0:T(128)}, u32[]{:S(2)}) copy-start(s32[4]{0:T(128)} %constant.94.clone) | copy-start | bytes 52
  12.2 4.7 %copy-start.6 = (f32[1024]{0:T(1024)S(1)}, f32[1024]{0:T(1024)}, u32[]{:S(2)}) copy-start(f32[1024]{0:T(1024)} %param.21) | copy-start | bytes 12292
  12.2 4.8 %copy-start.7 = (f32[1024]{0:T(1024)S(1)}, f32[1024]{0:T(1024)}, u32[]{:S(2)}) copy-start(f32[1024]{0:T(1024)} %param.20) | copy-start | bytes 12292
  14.7 3.4 %collective-permute-start.1 = (bf16[640,1024]{0,1:T(8,128)(2,1)}, bf16[640,1024]{0,1:T(8,128)(2,1)}, u32[]{:S(2)}, u32[]{:S(2)}) collective-permute-start(bf16[640,1024]{0,1:T(8,128)(2,1)} %copy.38), channel_id=1, source_target_pairs={{0,1},{1,0},{2,3},{3,2},{4,5},{5,4},{6,7},{7,6},{8,9},{9,8},{10,11... | collective-permute-start | bytes 3932168 | tf_op jit(solution)/shard_map/ppermute | solution.py:44
  17.7 4.1 %copy-start.2 = (bf16[640,2048]{1,0:T(8,128)(2,1)S(1)}, bf16[640,2048]{1,0:T(8,128)(2,1)}, u32[]{:S(2)}) copy-start(bf16[640,2048]{1,0:T(8,128)(2,1)} %param.12) | copy-start | bytes 7864324
  30.1 17.0 %collective-permute-start.2 = (bf16[128,2048]{1,0:T(8,128)(2,1)S(1)}, bf16[128,2048]{1,0:T(8,128)(2,1)S(1)}, u32[]{:S(2)}, u32[]{:S(2)}) collective-permute-start(bf16[128,2048]{1,0:T(8,128)(2,1)S(1)} %bitcast.73), channel_id=1, source_target_pairs={{0,6},{1,193},{2,0},{3,195},{4,2},{5,197},{6,4},{7,199},{8,14},{9,... | collective-permute-start | bytes 1572872 | tf_op jit(solution)/shard_map/ppermute | solution.py:40
  32.8 9.5 %collective-permute-start.3 = (bf16[128,2048]{1,0:T(8,128)(2,1)S(1)}, bf16[128,2048]{1,0:T(8,128)(2,1)S(1)}, u32[]{:S(2)}, u32[]{:S(2)}) collective-permute-start(bf16[128,2048]{1,0:T(8,128)(2,1)S(1)} %bitcast.74), channel_id=1, source_target_pairs={{0,2},{1,65},{2,4},{3,67},{4,6},{5,69},{6,0},{7,71},{8,10},{9,73},... | collective-permute-start | bytes 1572872 | tf_op jit(solution)/shard_map/ppermute | solution.py:40
  32.8 4.1 %copy-start.1 = (bf16[1280,1024]{0,1:T(8,128)(2,1)S(1)}, bf16[1280,1024]{0,1:T(8,128)(2,1)}, u32[]{:S(2)}) copy-start(bf16[1280,1024]{0,1:T(8,128)(2,1)} %pad_maximum_fusion.1) | copy-start | bytes 7864324
  32.8 17.0 %slice-start = ((s8[5242880]{0:T(1024)(128)(4,1)}), s8[4194304]{0:T(1024)(128)(4,1)S(1)}, s32[]{:S(2)}) async-start(s8[5242880]{0:T(1024)(128)(4,1)} %bitcast.79), calls=%async_computation.3 | async-start | bytes 8388608
  37.0 12.9 %slice-start.1 = ((s8[5242880]{0:T(1024)(128)(4,1)}), s8[1048576]{0:T(1024)(128)(4,1)S(1)}, s32[]{:S(2)}) async-start(s8[5242880]{0:T(1024)(128)(4,1)} %bitcast.79), calls=%async_computation.4 | async-start | bytes 2097152
  42.4 18.0 %collective-permute-start.8 = (bf16[256,2048]{1,0:T(8,128)(2,1)S(1)}, bf16[256,2048]{1,0:T(8,128)(2,1)S(1)}, u32[]{:S(2)}, u32[]{:S(2)}) collective-permute-start(bf16[256,2048]{1,0:T(8,128)(2,1)S(1)} %join.3), channel_id=1, source_target_pairs={{0,64},{1,3},{2,66},{3,5},{4,68},{5,7},{6,70},{7,1},{8,72},{9,11},... | collective-permute-start | bytes 3145736 | tf_op jit(solution)/shard_map/ppermute | solution.py:40
  45.2 16.9 %collective-permute-start.10 = (bf16[256,2048]{1,0:T(8,128)(2,1)S(1)}, bf16[256,2048]{1,0:T(8,128)(2,1)S(1)}, u32[]{:S(2)}, u32[]{:S(2)}) collective-permute-start(bf16[256,2048]{1,0:T(8,128)(2,1)S(1)} %join.3), channel_id=1, source_target_pairs={{0,192},{1,7},{2,194},{3,1},{4,196},{5,3},{6,198},{7,5},{8,200},{9... | collective-permute-start | bytes 3145736 | tf_op jit(solution)/shard_map/ppermute | solution.py:40
  47.0 9.6 %collective-permute-start.4 = (bf16[64,2048]{1,0:T(8,128)(2,1)S(1)}, bf16[64,2048]{1,0:T(8,128)(2,1)S(1)}, u32[]{:S(2)}, u32[]{:S(2)}) collective-permute-start(bf16[64,2048]{1,0:T(8,128)(2,1)S(1)} %slice.168), channel_id=1, source_target_pairs={{0,2},{1,65},{2,4},{3,67},{4,6},{5,69},{6,0},{7,71},{8,10},{9,73},... | collective-permute-start | bytes 786440 | tf_op jit(solution)/shard_map/ppermute | solution.py:40
  47.1 9.5 %collective-permute-start.5 = (bf16[64,2048]{1,0:T(8,128)(2,1)S(1)}, bf16[64,2048]{1,0:T(8,128)(2,1)S(1)}, u32[]{:S(2)}, u32[]{:S(2)}) collective-permute-start(bf16[64,2048]{1,0:T(8,128)(2,1)S(1)} %slice.169), channel_id=1, source_target_pairs={{0,6},{1,193},{2,0},{3,195},{4,2},{5,197},{6,4},{7,199},{8,14},{9,... | collective-permute-start | bytes 786440 | tf_op jit(solution)/shard_map/ppermute | solution.py:40
  56.7 16.5 %collective-permute-start.6 = (bf16[256,2048]{1,0:T(8,128)(2,1)S(1)}, bf16[256,2048]{1,0:T(8,128)(2,1)S(1)}, u32[]{:S(2)}, u32[]{:S(2)}) collective-permute-start(bf16[256,2048]{1,0:T(8,128)(2,1)S(1)} %join.2), channel_id=1, source_target_pairs={{0,192},{1,7},{2,194},{3,1},{4,196},{5,3},{6,198},{7,5},{8,200},{9... | collective-permute-start | bytes 3145736 | tf_op jit(solution)/shard_map/ppermute | solution.py:40
  57.9 19.8 %collective-permute-start.9 = (bf16[256,2048]{1,0:T(8,128)(2,1)S(1)}, bf16[256,2048]{1,0:T(8,128)(2,1)S(1)}, u32[]{:S(2)}, u32[]{:S(2)}) collective-permute-start(bf16[256,2048]{1,0:T(8,128)(2,1)S(1)} %join.2), channel_id=1, source_target_pairs={{0,64},{1,3},{2,66},{3,5},{4,68},{5,7},{6,70},{7,1},{8,72},{9,11},... | collective-permute-start | bytes 3145736 | tf_op jit(solution)/shard_map/ppermute | solution.py:40
  60.5 23.8 %collective-permute-start.11 = (bf16[256,2048]{1,0:T(8,128)(2,1)S(1)}, bf16[256,2048]{1,0:T(8,128)(2,1)S(1)}, u32[]{:S(2)}, u32[]{:S(2)}) collective-permute-start(bf16[256,2048]{1,0:T(8,128)(2,1)S(1)} %collective-permute-done.8), channel_id=1, source_target_pairs={{0,64},{1,3},{2,66},{3,5},{4,68},{5,7},{6,70},{7,1},{8,72},{9,11},... | collective-permute-start | bytes 3145736 | tf_op jit(solution)/shard_map/ppermute | solution.py:40
  73.2 14.7 %collective-permute-start.7 = (bf16[256,2048]{1,0:T(8,128)(2,1)S(1)}, bf16[256,2048]{1,0:T(8,128)(2,1)S(1)}, u32[]{:S(2)}, u32[]{:S(2)}) collective-permute-start(bf16[256,2048]{1,0:T(8,128)(2,1)S(1)} %collective-permute-done.6), channel_id=1, source_target_pairs={{0,192},{1,7},{2,194},{3,1},{4,196},{5,3},{6,198},{7,5},{8,200},{9... | collective-permute-start | bytes 3145736 | tf_op jit(solution)/shard_map/ppermute | solution.py:40
  89.5 4.6 %collective-permute-start.12 = (f32[1408]{0:T(1024)S(1)}, f32[1408]{0:T(1024)S(1)}, u32[]{:S(2)}, u32[]{:S(2)}) collective-permute-start(f32[1408]{0:T(1024)S(1)} %concatenate.40), channel_id=1, source_target_pairs={{0,1},{1,0},{2,3},{3,2},{4,5},{5,4},{6,7},{7,6},{8,9},{9,8},{10,11... | collective-permute-start | bytes 16904 | tf_op jit(solution)/shard_map/ppermute | solution.py:44
  98.2 1.3 collective-permute-start.13
  142.1 6.7 %collective-permute-start.14 = (f32[8,640]{1,0:T(8,128)S(1)}, f32[8,640]{1,0:T(8,128)S(1)}, u32[]{:S(2)}, u32[]{:S(2)}) collective-permute-start(f32[8,640]{1,0:T(8,128)S(1)} %reduce_sum.229), channel_id=1, source_target_pairs={{0,0},{1,128},{128,1},{129,129},{2,2},{3,130},{130,3},{131,131},{4... | collective-permute-start | bytes 61448 | tf_op jit(solution)/shard_map/ppermute | solution.py:223
  147.4 4.2 %collective-permute-start.15 = (f32[8,640]{1,0:T(8,128)S(1)}, f32[8,640]{1,0:T(8,128)S(1)}, u32[]{:S(2)}, u32[]{:S(2)}) collective-permute-start(f32[8,640]{1,0:T(8,128)S(1)} %reduce_sum.229), channel_id=1, source_target_pairs={{0,128},{1,0},{128,129},{129,1},{2,130},{3,2},{130,131},{131,3},{4... | collective-permute-start | bytes 61448 | tf_op jit(solution)/shard_map/ppermute | solution.py:223

commit v5 on v4

--- a/solution.py
+++ b/solution.py
@@ -64,10 +64,8 @@
 
 
 def ring_gather(block, dims):
-    half = block.shape[0] // 2
     left, right = shift(block, dims, 1), shift(block, dims, -1)
-    far = shift(left[:half], dims, 1), shift(right[half:], dims, -1)
-    return block, left, right, *far
+    return block, left, right, shift(left, dims, 1)
 
 
 def wide_gather(first, second, dims):
@@ -201,11 +199,11 @@
 
     dcross_half, reach, small = lax.optimization_barrier((dcross_half, reach, small))
     parts = transposed_dot(turned, dcross_half)
-    power = power_for(jnp.max(reach, keepdims=True))[:, None]
+    power = power_for(jnp.max(reach))
     scaled = small * jnp.exp2(power)
     top = scaled.astype(jnp.float16)
     low = (scaled - top.astype(jnp.float32)).astype(jnp.float16)
-    powers = jnp.broadcast_to(power, (4, half_s)).astype(jnp.float16)
+    powers = jnp.broadcast_to(power.astype(jnp.float16), (4, half_s))
     tail = jnp.concatenate([top, low, powers], axis=0)
     parts = (parts * jnp.exp2(power)).astype(jnp.float16).reshape(16, -1, half_s)
     parts = jnp.concatenate([parts, jnp.broadcast_to(tail, (16, *tail.shape))], axis=1)

time: 153 us -> 152 us (level)
  waiting for transfers between devices: 36.6 us -> 39 us
  matrix products: 21.3 us -> 19 us
  blocking collectives: 35.2 us -> 33.2 us
  local copies, waits for them, and re-layouts: 7.77 us -> 9.73 us
    ppermute x10 -> x9, waiting for transfers between devices: 27.5 us -> 29.8 us  [shift(): return lax.ppermute(value, GROUP_FSDP, shift_pairs(dims, step))]
    dot_general x1, matrix products: 4.08 us -> 1.82 us  [shards(): lax.dot_general(cross_half, s_rows, (((0,), (1,)), ((), ())), preferred_e...]
    all_to_all x1, blocking collectives: 24.2 us -> 22.2 us  [shards(): lax.all_to_all(parts, ('group', 'fsdp_0', 'fsdp_2'), 0, 0, tiled=True)]
    ppermute x10 -> x9, starting transfers between devices: 13 us -> 11.6 us  [shift(): return lax.ppermute(value, GROUP_FSDP, shift_pairs(dims, step))]
  transfers between devices with their start and end apart: 17 -> 16, of which waited for: 12 -> 11; matrix products, arithmetic and copies ran while one was open for 21% -> 21% of each run, Pallas kernels for 0% -> 0%
where the time goes in v5:
time: 152 us
  waiting for transfers between devices  39 us (26%)
  blocking collectives  33.2 us (22%)
  starting transfers between devices  31.7 us (21%)
  matrix products  19 us (12%)
  other arithmetic  16.6 us (11%)
  local copies, waits for them, and re-layouts  9.73 us (6%)
  between operations  2.5 us (2%)
    ppermute x9, waiting for transfers between devices, shift(): return lax.ppermute(value, GROUP_FSDP, shift_pairs(dims, step))  29.8 us
    all_to_all x1, blocking collectives, shards(): lax.all_to_all(parts, ('group', 'fsdp_0', 'fsdp_2'), 0, 0, tiled=True)  22.2 us
    dot_general x9, matrix products, transposed_dot(): lax.dot_general(left, right, (((1,), (1,)), ((), ())), preferred_element_...  15.9 us
    ppermute x9, starting transfers between devices, shift(): return lax.ppermute(value, GROUP_FSDP, shift_pairs(dims, step))  11.6 us
    all_to_all x1, blocking collectives, shards(): parts = lax.all_to_all(parts, 'fsdp_1', 0, 0, tiled=True).sum(axis=0)  11.1 us
    ppermute x4, starting transfers between devices, swap_cores(): return lax.ppermute(value, 'fsdp_3', ((0, 1), (1, 0)))  8.31 us
    all_to_all x1, starting transfers between devices, shards(): lax.all_to_all(jnp.broadcast_to(mine[None], (8, *mine.shape)), 'fsdp_1',...  6.48 us
    ppermute x2, starting transfers between devices, shards(): lax.ppermute(parts, ('group', 'fsdp_3'), pairs)  5.31 us
  transfers between devices with their start and end apart: 16, of which 11 were waited for; matrix products, arithmetic and copies ran while one was open for 21% of the time, Pallas kernels for 0%

profile of v5, /device:TPU:1, one launch (start us, length us, event | category | flops | bytes accessed | tf_op | source)
XLA Modules:
  0.0 151.8 jit_solution(11680322021355150640)
XLA Ops:
  0.6 3.3 %collective-permute-start = (bf16[640,2048]{1,0:T(8,128)(2,1)}, bf16[640,2048]{1,0:T(8,128)(2,1)}, u32[]{:S(2)}, u32[]{:S(2)}) collective-permute-start(bf16[640,2048]{1,0:T(8,128)(2,1)} %param.12), channel_id=1, source_target_pairs={{0,1},{1,0},{2,3},{3,2},{4,5},{5,4},{6,7},{7,6},{8,9},{9,8},{10,11... | collective-permute-start | bytes 7864328 | tf_op jit(solution)/shard_map/ppermute | solution.py:44
  3.9 1.7 %broadcast_in_dim.12 = bf16[8,16,2048]{2,1,0:T(8,128)(2,1)} broadcast(bf16[16,2048]{1,0:T(8,128)(2,1)} %bitcast.84), dimensions={1,2} | broadcast | bytes 589824 | tf_op jit(solution)/shard_map/broadcast_in_dim | solution.py:116
  5.7 6.5 %all-to-all-start = ((bf16[8,16,2048]{2,1,0:T(8,128)(2,1)}), bf16[8,16,2048]{2,1,0:T(8,128)(2,1)S(1)}, u32[]{:S(2)}, u32[]{:S(2)}) async-start(bf16[8,16,2048]{2,1,0:T(8,128)(2,1)} %broadcast_in_dim.12), calls=%async_computation | async-start | bytes 1048576 | tf_op jit(solution)/shard_map/all_to_all | solution.py:115
  12.2 2.5 %copy.38 = bf16[640,1024]{0,1:T(8,128)(2,1)} copy(bf16[640,1024]{1,0:T(8,128)(2,1)} %param.13) | data formatting | bytes 2621440 | tf_op args[1]
  14.7 0.4 collective-permute-start.1
  15.2 0.1 add_add_fusion.1
  15.3 0.1 iota_add_fusion
  15.4 0.1 add.313
  15.4 0.2 convolution_bitcast_fusion
  15.7 1.1 fusion.3
  16.9 0.1 dynamic_slice.15
  16.9 0.1 dynamic_slice.14
  17.7 0.4 collective-permute-done.1
  18.1 3.7 %pad_maximum_fusion.1 = bf16[1280,1024]{0,1:T(8,128)(2,1)} fusion(bf16[640,1024]{0,1:T(8,128)(2,1)} %collective-permute-done.1, bf16[640,1024]{0,1:T(8,128)(2,1)} %copy.38), kind=kLoop, calls=%fused_computation.11 | loop fusion | flops 5242880 | bytes 5242880 | tf_op jit(solution)/shard_map/concatenate | solution.py:120
  21.8 4.8 %pad_maximum_fusion = bf16[1280,2048]{1,0:T(8,128)(2,1)} fusion(bf16[640,2048]{1,0:T(8,128)(2,1)} %collective-permute-done, bf16[640,2048]{1,0:T(8,128)(2,1)S(1)} %copy-done.2), kind=kLoop, calls=%fused_computation | loop fusion | flops 10485760 | bytes 10485760 | tf_op jit(solution)/shard_map/concatenate | solution.py:119
  26.6 3.5 %all-to-all-done = bf16[8,16,2048]{2,1,0:T(8,128)(2,1)S(1)} async-done(((bf16[8,16,2048]{2,1,0:T(8,128)(2,1)}), bf16[8,16,2048]{2,1,0:T(8,128)(2,1)S(1)}, u32[]{:S(2)}, u32[]{:S(2)}) %all-to-all-start) | async-done | bytes 524320 | tf_op jit(solution)/shard_map/all_to_all | solution.py:115
  30.1 2.7 %collective-permute-start.2 = (bf16[128,2048]{1,0:T(8,128)(2,1)S(1)}, bf16[128,2048]{1,0:T(8,128)(2,1)S(1)}, u32[]{:S(2)}, u32[]{:S(2)}) collective-permute-start(bf16[128,2048]{1,0:T(8,128)(2,1)S(1)} %bitcast.73), channel_id=1, source_target_pairs={{0,6},{1,193},{2,0},{3,195},{4,2},{5,197},{6,4},{7,199},{8,14},{9,... | collective-permute-start | bytes 1572872 | tf_op jit(solution)/shard_map/ppermute | solution.py:40
  32.8 1.6 %constant_dynamic-slice_fusion = bf16[512,1280]{1,0:T(8,128)(2,1)S(1)} fusion(bf16[1024,1280]{1,0:T(8,128)(2,1)} %bitcast.76, s32[]{:T(128)S(6)} %select_n.48), kind=kLoop, calls=%fused_computation.100 | loop fusion | bytes 2621444 | tf_op jit(solution)/shard_map/dynamic_slice | solution.py:157
  34.4 0.5 copy-done.1
  35.0 1.8 %multiply_reduce_fusion.1 = (f32[1280]{0:T(1024)S(1)}, f32[512,1280]{1,0:T(8,128)S(1)}) fusion(f32[512]{0:T(512)S(1)} %dynamic_slice.15, f32[512]{0:T(512)S(1)} %dynamic_slice.14, bf16[1280,1024]{0,1:T(8,128)(2,1)S(1)} %copy-done.1, bf16[1024,1024]{1,0:T(8,128)(2,1)S(1)} %copy-done, s32[]{:T(128)S(6)} %select_n.48, bf16[1024,1280]{1,0:T(8,128)(2,1)S(1)} %bitcast.77), kind=kOutput, calls=%fused_computation.17 | convolution fusion | flops 1346108160 | bytes 7612416 | tf_op jit(solution)/shard_map/dot_general | solution.py:153
  36.8 5.6 %collective-permute-done.3.refs_1_ = bf16[128,2048]{1,0:T(8,128)(2,1)S(1)} collective-permute-done((bf16[128,2048]{1,0:T(8,128)(2,1)S(1)}, bf16[128,2048]{1,0:T(8,128)(2,1)S(1)}, u32[]{:S(2)}, u32[]{:S(2)}) %collective-permute-start.3) | collective-permute-done | bytes 524320 | tf_op jit(solution)/shard_map/ppermute | solution.py:40
  42.4 0.1 join.3
  42.4 1.0 collective-permute-start.7
  43.4 1.8 %copy.39 = bf16[2,8,4,2,8,1280]{5,4,1,2,0,3:T(8,128)(2,1)} copy(bf16[2,8,4,2,8,1280]{5,4,3,2,1,0:T(8,128)(2,1)S(1)} %bitcast.78) | data formatting | bytes 5242880 | tf_op jit(solution)/shard_map/reshape | solution.py:161
  45.2 1.8 %collective-permute-start.9 = (bf16[256,2048]{1,0:T(8,128)(2,1)S(1)}, bf16[256,2048]{1,0:T(8,128)(2,1)S(1)}, u32[]{:S(2)}, u32[]{:S(2)}) collective-permute-start(bf16[256,2048]{1,0:T(8,128)(2,1)S(1)} %join.3), channel_id=1, source_target_pairs={{0,192},{1,7},{2,194},{3,1},{4,196},{5,3},{6,198},{7,5},{8,200},{9... | collective-permute-start | bytes 3145736 | tf_op jit(solution)/shard_map/ppermute | solution.py:40
  47.0 1.6 %multiply_reduce_fusion.18 = (f32[1280]{0:T(1024)S(1)}, f32[256,1280]{1,0:T(8,128)S(1)}) fusion(f32[256]{0:T(256)S(1)} %bitcast.112, bf16[256,2048]{1,0:T(8,128)(2,1)S(1)} %join.3, bf16[1280,2048]{1,0:T(8,128)(2,1)S(1)} %bitcast.80), kind=kOutput, calls=%fused_computation.38 | convolution fusion | flops 1343159040 | bytes 7608320 | tf_op jit(solution)/shard_map/dot_general | solution.py:87
  48.6 9.0 %collective-permute-done.4.refs_1_ = bf16[128,2048]{1,0:T(8,128)(2,1)S(1)} collective-permute-done((bf16[128,2048]{1,0:T(8,128)(2,1)S(1)}, bf16[128,2048]{1,0:T(8,128)(2,1)S(1)}, u32[]{:S(2)}, u32[]{:S(2)}) %collective-permute-start.4) | collective-permute-done | bytes 524320 | tf_op jit(solution)/shard_map/ppermute | solution.py:40
  57.6 2.9 %collective-permute-start.5 = (bf16[256,2048]{1,0:T(8,128)(2,1)S(1)}, bf16[256,2048]{1,0:T(8,128)(2,1)S(1)}, u32[]{:S(2)}, u32[]{:S(2)}) collective-permute-start(bf16[256,2048]{1,0:T(8,128)(2,1)S(1)} %join.2), channel_id=1, source_target_pairs={{0,192},{1,7},{2,194},{3,1},{4,196},{5,3},{6,198},{7,5},{8,200},{9... | collective-permute-start | bytes 3145736 | tf_op jit(solution)/shard_map/ppermute | solution.py:40
  60.5 1.6 %multiply_reduce_fusion.17 = (f32[1280]{0:T(1024)S(1)}, f32[256,1280]{1,0:T(8,128)S(1)}) fusion(f32[256]{0:T(256)S(1)} %bitcast.111, bf16[256,2048]{1,0:T(8,128)(2,1)S(1)} %join.2, bf16[1280,2048]{1,0:T(8,128)(2,1)S(1)} %bitcast.80), kind=kOutput, calls=%fused_computation.37 | convolution fusion | flops 1343159040 | bytes 7608320 | tf_op jit(solution)/shard_map/dot_general | solution.py:87
  62.1 1.2 collective-permute-done.7
  63.3 1.6 %multiply_reduce_fusion.16 = (f32[1280]{0:T(1024)S(1)}, f32[256,1280]{1,0:T(8,128)S(1)}) fusion(f32[256]{0:T(256)S(1)} %bitcast.110, bf16[256,2048]{1,0:T(8,128)(2,1)S(1)} %collective-permute-done.7, bf16[1280,2048]{1,0:T(8,128)(2,1)S(1)} %bitcast.80), kind=kOutput, calls=%fused_computation.36 | convolution fusion | flops 1343159040 | bytes 7608320 | tf_op jit(solution)/shard_map/dot_general | solution.py:87
  64.9 1.6 %multiply_reduce_fusion.14 = (f32[1280]{0:T(1024)S(1)}, f32[256,1280]{1,0:T(8,128)S(1)}) fusion(f32[256]{0:T(256)S(1)} %bitcast.109, bf16[256,2048]{1,0:T(8,128)(2,1)S(1)} %collective-permute-done.9, bf16[1280,2048]{1,0:T(8,128)(2,1)S(1)} %bitcast.80), kind=kOutput, calls=%fused_computation.34 | convolution fusion | flops 1343159040 | bytes 7608320 | tf_op jit(solution)/shard_map/dot_general | solution.py:87
  66.5 6.0 %collective-permute-done.5 = bf16[256,2048]{1,0:T(8,128)(2,1)S(1)} collective-permute-done((bf16[256,2048]{1,0:T(8,128)(2,1)S(1)}, bf16[256,2048]{1,0:T(8,128)(2,1)S(1)}, u32[]{:S(2)}, u32[]{:S(2)}) %collective-permute-start.5) | collective-permute-done | bytes 1048608 | tf_op jit(solution)/shard_map/ppermute | solution.py:40
  72.4 3.2 %collective-permute-start.6 = (bf16[256,2048]{1,0:T(8,128)(2,1)S(1)}, bf16[256,2048]{1,0:T(8,128)(2,1)S(1)}, u32[]{:S(2)}, u32[]{:S(2)}) collective-permute-start(bf16[256,2048]{1,0:T(8,128)(2,1)S(1)} %collective-permute-done.5), channel_id=1, source_target_pairs={{0,192},{1,7},{2,194},{3,1},{4,196},{5,3},{6,198},{7,5},{8,200},{9... | collective-permute-start | bytes 3145736 | tf_op jit(solution)/shard_map/ppermute | solution.py:40
  75.7 1.6 %multiply_reduce_fusion.13 = (f32[1280]{0:T(1024)S(1)}, f32[256,1280]{1,0:T(8,128)S(1)}) fusion(f32[256]{0:T(256)S(1)} %bitcast.107, bf16[256,2048]{1,0:T(8,128)(2,1)S(1)} %collective-permute-done.5, bf16[1280,2048]{1,0:T(8,128)(2,1)S(1)} %bitcast.80), kind=kOutput, calls=%fused_computation.33 | convolution fusion | flops 1343159040 | bytes 7608320 | tf_op jit(solution)/shard_map/dot_general | solution.py:87
  77.2 1.6 %multiply_reduce_fusion.15 = (f32[1280]{0:T(1024)S(1)}, f32[256,1280]{1,0:T(8,128)S(1)}) fusion(f32[256]{0:T(256)S(1)} %bitcast.108, bf16[256,2048]{1,0:T(8,128)(2,1)S(1)} %collective-permute-done.8, bf16[1280,2048]{1,0:T(8,128)(2,1)S(1)} %bitcast.80), kind=kOutput, calls=%fused_computation.35 | convolution fusion | flops 1343159040 | bytes 7608320 | tf_op jit(solution)/shard_map/dot_general | solution.py:87
  78.8 8.1 %collective-permute-done.10 = bf16[256,2048]{1,0:T(8,128)(2,1)S(1)} collective-permute-done((bf16[256,2048]{1,0:T(8,128)(2,1)S(1)}, bf16[256,2048]{1,0:T(8,128)(2,1)S(1)}, u32[]{:S(2)}, u32[]{:S(2)}) %collective-permute-start.10) | collective-permute-done | bytes 1048608 | tf_op jit(solution)/shard_map/ppermute | solution.py:40
  86.9 1.6 %multiply_reduce_fusion.12 = (f32[1280]{0:T(1024)S(1)}, f32[256,1280]{1,0:T(8,128)S(1)}) fusion(f32[256]{0:T(256)S(1)} %bitcast.106, bf16[256,2048]{1,0:T(8,128)(2,1)S(1)} %collective-permute-done.10, bf16[1280,2048]{1,0:T(8,128)(2,1)S(1)} %bitcast.80), kind=kOutput, calls=%fused_computation.32 | convolution fusion | flops 1343159040 | bytes 7608320 | tf_op jit(solution)/shard_map/dot_general | solution.py:87
  88.5 1.6 %multiply_reduce_fusion.11 = (f32[1280]{0:T(1024)S(1)}, f32[256,1280]{1,0:T(8,128)S(1)}) fusion(f32[256]{0:T(256)S(1)} %bitcast.105, bf16[256,2048]{1,0:T(8,128)(2,1)S(1)} %collective-permute-done.6, bf16[1280,2048]{1,0:T(8,128)(2,1)S(1)} %bitcast.80), kind=kOutput, calls=%fused_computation.31 | convolution fusion | flops 1343159040 | bytes 7608320 | tf_op jit(solution)/shard_map/dot_general | solution.py:87
  90.1 4.2 %collective-permute-start.11 = (f32[1408]{0:T(1024)S(1)}, f32[1408]{0:T(1024)S(1)}, u32[]{:S(2)}, u32[]{:S(2)}) collective-permute-start(f32[1408]{0:T(1024)S(1)} %concatenate.40), channel_id=1, source_target_pairs={{0,1},{1,0},{2,3},{3,2},{4,5},{5,4},{6,7},{7,6},{8,9},{9,8},{10,11... | collective-permute-start | bytes 16904 | tf_op jit(solution)/shard_map/ppermute | solution.py:44
  94.3 0.8 collective-permute-done.11
  95.1 1.0 multiply_reduce_fusion.10
  96.1 3.0 %multiply_reduce_fusion.9 = (f32[1280]{0:T(1024)S(1)}, f32[1280]{0:T(1024)S(1)}, f32[1280]{0:T(1024)S(1)}, f32[1280]{0:T(1024)S(1)}, f32[1280]{0:T(1024)S(1)}, /*index=5*/f32[1280]{0:T(1024)S(1)}) fusion(f32[256,1280]{1,0:T(8,128)S(1)} %get-tuple-element.92, f32[256]{0:T(256)S(1)} %bitcast.97, f32[256]{0:T(256)S(1)} %bitcast.98, f32[1280]{0:T(1024)S(1)} %fusion.20, ...), kind=kLoop, calls=%fused_computation.29 | loop fusion | flops 13754880 | bytes 7912448 | tf_op jit(solution)/shard_map/reduce_sum | solution.py:189
  99.1 0.4 collective-permute-start.12
  99.6 0.5 slice.160
  100.1 0.3 collective-permute-done.12
  100.4 0.7 fusion.22
  101.1 0.9 fusion
  102.0 0.6 reduce_max.9
  103.4 0.1 pad.10.clone
  103.5 3.3 %multiply_convert_fusion = f16[1024,512]{1,0:T(8,128)(2,1)S(1)} fusion(bf16[1024,1280]{1,0:T(8,128)(2,1)} %bitcast.81, bf16[512,1280]{1,0:T(8,128)(2,1)S(1)} %get-tuple-element.24, f32[]{:T(128)S(6)} %exp2.15), kind=kOutput, calls=%fused_computation.19 | convolution fusion | flops 1343225856 | bytes 4980740 | tf_op jit(solution)/shard_map/dot_general | solution.py:87
  106.8 0.1 maximum_maximum_fusion
  106.9 0.3 pad_maximum_fusion.2
  107.2 22.2 %all_to_all.15 = f16[16,72,512]{2,1,0:T(8,128)(2,1)S(1)} all-to-all(f16[16,72,512]{2,1,0:T(8,128)(2,1)S(1)} %pad_maximum_fusion.2), channel_id=1, replica_groups=mesh['group'=2,'fsdp_0'=2,'fsdp_1'=8,'fsdp_2'=4,'fsdp_3'=2] {'group','fs..., dimensions={0} | all-to-all | bytes 2359296 | tf_op jit(solution)/shard_map/all_to_all | solution.py:210
  129.3 0.2 fusion.25
  129.6 0.1 fusion.8
  129.7 0.3 multiply_reduce_fusion.2
  130.0 11.1 %all_to_all.16 = f32[8,8,640]{2,1,0:T(8,128)S(1)} all-to-all(f32[8,8,640]{2,1,0:T(8,128)S(1)} %pad_maximum_fusion.3), channel_id=1, replica_groups=mesh['group'=2,'fsdp_0'=2,'fsdp_1'=8,'fsdp_2'=4,'fsdp_3'=2] {'fsdp_1'}, dimensions={0} | all-to-all | bytes 327680 | tf_op jit(solution)/shard_map/all_to_all | solution.py:219
  141.1 5.2 %collective-permute-start.13 = (f32[8,640]{1,0:T(8,128)S(1)}, f32[8,640]{1,0:T(8,128)S(1)}, u32[]{:S(2)}, u32[]{:S(2)}) collective-permute-start(f32[8,640]{1,0:T(8,128)S(1)} %reduce_sum.229), channel_id=1, source_target_pairs={{0,0},{1,128},{128,1},{129,129},{2,2},{3,130},{130,3},{131,131},{4... | collective-permute-start | bytes 61448 | tf_op jit(solution)/shard_map/ppermute | solution.py:221
  146.3 0.1 collective-permute-start.14
  146.4 1.3 collective-permute-done.13
  147.8 2.8 %collective-permute-done.14 = f32[8,640]{1,0:T(8,128)S(1)} collective-permute-done((f32[8,640]{1,0:T(8,128)S(1)}, f32[8,640]{1,0:T(8,128)S(1)}, u32[]{:S(2)}, u32[]{:S(2)}) %collective-permute-start.14) | collective-permute-done | bytes 20512 | tf_op jit(solution)/shard_map/ppermute | solution.py:221
  150.6 0.6 fusion.37
  151.2 0.6 pad_maximum_fusion.4
  (68 shorter events, 0.5 us)
Async XLA Ops:
  0.6 33.8 %copy-start = (bf16[1024,1024]{1,0:T(8,128)(2,1)S(1)}, bf16[1024,1024]{1,0:T(8,128)(2,1)}, u32[]{:S(2)}) copy-start(bf16[1024,1024]{1,0:T(8,128)(2,1)} %param.19) | copy-start | bytes 6291460
  0.6 21.1 %collective-permute-start = (bf16[640,2048]{1,0:T(8,128)(2,1)}, bf16[640,2048]{1,0:T(8,128)(2,1)}, u32[]{:S(2)}, u32[]{:S(2)}) collective-permute-start(bf16[640,2048]{1,0:T(8,128)(2,1)} %param.12), channel_id=1, source_target_pairs={{0,1},{1,0},{2,3},{3,2},{4,5},{5,4},{6,7},{7,6},{8,9},{9,8},{10,11... | collective-permute-start | bytes 7864328 | tf_op jit(solution)/shard_map/ppermute | solution.py:44
  5.7 24.4 %all-to-all-start = ((bf16[8,16,2048]{2,1,0:T(8,128)(2,1)}), bf16[8,16,2048]{2,1,0:T(8,128)(2,1)S(1)}, u32[]{:S(2)}, u32[]{:S(2)}) async-start(bf16[8,16,2048]{2,1,0:T(8,128)(2,1)} %broadcast_in_dim.12), calls=%async_computation | async-start | bytes 1048576 | tf_op jit(solution)/shard_map/all_to_all | solution.py:115
  12.1 3.0 %copy-start.3 = (f32[4096]{0:T(1024)S(1)}, f32[4096]{0:T(1024)}, u32[]{:S(2)}) copy-start(f32[4096]{0:T(1024)} %param.18) | copy-start | bytes 49156
  12.1 3.0 %copy-start.4 = (f32[4096]{0:T(1024)S(1)}, f32[4096]{0:T(1024)}, u32[]{:S(2)}) copy-start(f32[4096]{0:T(1024)} %param.17) | copy-start | bytes 49156
  12.1 3.0 %copy-start.5 = (f32[4096]{0:T(1024)S(1)}, f32[4096]{0:T(1024)}, u32[]{:S(2)}) copy-start(f32[4096]{0:T(1024)} %param.16) | copy-start | bytes 49156
  12.2 3.0 %copy-start.8 = (s32[4]{0:T(128)S(1)}, s32[4]{0:T(128)}, u32[]{:S(2)}) copy-start(s32[4]{0:T(128)} %constant.89.clone) | copy-start | bytes 52
  12.2 4.7 %copy-start.6 = (f32[1024]{0:T(1024)S(1)}, f32[1024]{0:T(1024)}, u32[]{:S(2)}) copy-start(f32[1024]{0:T(1024)} %param.21) | copy-start | bytes 12292
  12.2 4.8 %copy-start.7 = (f32[1024]{0:T(1024)S(1)}, f32[1024]{0:T(1024)}, u32[]{:S(2)}) copy-start(f32[1024]{0:T(1024)} %param.20) | copy-start | bytes 12292
  14.7 3.4 %collective-permute-start.1 = (bf16[640,1024]{0,1:T(8,128)(2,1)}, bf16[640,1024]{0,1:T(8,128)(2,1)}, u32[]{:S(2)}, u32[]{:S(2)}) collective-permute-start(bf16[640,1024]{0,1:T(8,128)(2,1)} %copy.38), channel_id=1, source_target_pairs={{0,1},{1,0},{2,3},{3,2},{4,5},{5,4},{6,7},{7,6},{8,9},{9,8},{10,11... | collective-permute-start | bytes 3932168 | tf_op jit(solution)/shard_map/ppermute | solution.py:44
  17.7 4.1 %copy-start.2 = (bf16[640,2048]{1,0:T(8,128)(2,1)S(1)}, bf16[640,2048]{1,0:T(8,128)(2,1)}, u32[]{:S(2)}) copy-start(bf16[640,2048]{1,0:T(8,128)(2,1)} %param.12) | copy-start | bytes 7864324
  30.1 18.5 %collective-permute-start.2 = (bf16[128,2048]{1,0:T(8,128)(2,1)S(1)}, bf16[128,2048]{1,0:T(8,128)(2,1)S(1)}, u32[]{:S(2)}, u32[]{:S(2)}) collective-permute-start(bf16[128,2048]{1,0:T(8,128)(2,1)S(1)} %bitcast.73), channel_id=1, source_target_pairs={{0,6},{1,193},{2,0},{3,195},{4,2},{5,197},{6,4},{7,199},{8,14},{9,... | collective-permute-start | bytes 1572872 | tf_op jit(solution)/shard_map/ppermute | solution.py:40
  32.8 9.5 %collective-permute-start.3 = (bf16[128,2048]{1,0:T(8,128)(2,1)S(1)}, bf16[128,2048]{1,0:T(8,128)(2,1)S(1)}, u32[]{:S(2)}, u32[]{:S(2)}) collective-permute-start(bf16[128,2048]{1,0:T(8,128)(2,1)S(1)} %bitcast.74), channel_id=1, source_target_pairs={{0,2},{1,65},{2,4},{3,67},{4,6},{5,69},{6,0},{7,71},{8,10},{9,73},... | collective-permute-start | bytes 1572872 | tf_op jit(solution)/shard_map/ppermute | solution.py:40
  32.8 2.1 %copy-start.1 = (bf16[1280,1024]{0,1:T(8,128)(2,1)S(1)}, bf16[1280,1024]{0,1:T(8,128)(2,1)}, u32[]{:S(2)}) copy-start(bf16[1280,1024]{0,1:T(8,128)(2,1)} %pad_maximum_fusion.1) | copy-start | bytes 7864324
  32.8 14.1 %slice-start = ((s8[5242880]{0:T(1024)(128)(4,1)}), s8[4194304]{0:T(1024)(128)(4,1)S(1)}, s32[]{:S(2)}) async-start(s8[5242880]{0:T(1024)(128)(4,1)} %bitcast.79), calls=%async_computation.3 | async-start | bytes 8388608
  35.0 12.0 %slice-start.1 = ((s8[5242880]{0:T(1024)(128)(4,1)}), s8[1048576]{0:T(1024)(128)(4,1)S(1)}, s32[]{:S(2)}) async-start(s8[5242880]{0:T(1024)(128)(4,1)} %bitcast.79), calls=%async_computation.4 | async-start | bytes 2097152
  42.4 20.8 %collective-permute-start.7 = (bf16[256,2048]{1,0:T(8,128)(2,1)S(1)}, bf16[256,2048]{1,0:T(8,128)(2,1)S(1)}, u32[]{:S(2)}, u32[]{:S(2)}) collective-permute-start(bf16[256,2048]{1,0:T(8,128)(2,1)S(1)} %join.3), channel_id=1, source_target_pairs={{0,64},{1,3},{2,66},{3,5},{4,68},{5,7},{6,70},{7,1},{8,72},{9,11},... | collective-permute-start | bytes 3145736 | tf_op jit(solution)/shard_map/ppermute | solution.py:40
  43.4 14.1 %collective-permute-start.4 = (bf16[128,2048]{1,0:T(8,128)(2,1)S(1)}, bf16[128,2048]{1,0:T(8,128)(2,1)S(1)}, u32[]{:S(2)}, u32[]{:S(2)}) collective-permute-start(bf16[128,2048]{1,0:T(8,128)(2,1)S(1)} %collective-permute-done.3.refs_1_), channel_id=1, source_target_pairs={{0,2},{1,65},{2,4},{3,67},{4,6},{5,69},{6,0},{7,71},{8,10},{9,73},... | collective-permute-start | bytes 1572872 | tf_op jit(solution)/shard_map/ppermute | solution.py:40
  45.2 19.7 %collective-permute-start.9 = (bf16[256,2048]{1,0:T(8,128)(2,1)S(1)}, bf16[256,2048]{1,0:T(8,128)(2,1)S(1)}, u32[]{:S(2)}, u32[]{:S(2)}) collective-permute-start(bf16[256,2048]{1,0:T(8,128)(2,1)S(1)} %join.3), channel_id=1, source_target_pairs={{0,192},{1,7},{2,194},{3,1},{4,196},{5,3},{6,198},{7,5},{8,200},{9... | collective-permute-start | bytes 3145736 | tf_op jit(solution)/shard_map/ppermute | solution.py:40
  57.6 14.8 %collective-permute-start.5 = (bf16[256,2048]{1,0:T(8,128)(2,1)S(1)}, bf16[256,2048]{1,0:T(8,128)(2,1)S(1)}, u32[]{:S(2)}, u32[]{:S(2)}) collective-permute-start(bf16[256,2048]{1,0:T(8,128)(2,1)S(1)} %join.2), channel_id=1, source_target_pairs={{0,192},{1,7},{2,194},{3,1},{4,196},{5,3},{6,198},{7,5},{8,200},{9... | collective-permute-start | bytes 3145736 | tf_op jit(solution)/shard_map/ppermute | solution.py:40
  60.5 16.7 %collective-permute-start.8 = (bf16[256,2048]{1,0:T(8,128)(2,1)S(1)}, bf16[256,2048]{1,0:T(8,128)(2,1)S(1)}, u32[]{:S(2)}, u32[]{:S(2)}) collective-permute-start(bf16[256,2048]{1,0:T(8,128)(2,1)S(1)} %join.2), channel_id=1, source_target_pairs={{0,64},{1,3},{2,66},{3,5},{4,68},{5,7},{6,70},{7,1},{8,72},{9,11},... | collective-permute-start | bytes 3145736 | tf_op jit(solution)/shard_map/ppermute | solution.py:40
  63.3 23.6 %collective-permute-start.10 = (bf16[256,2048]{1,0:T(8,128)(2,1)S(1)}, bf16[256,2048]{1,0:T(8,128)(2,1)S(1)}, u32[]{:S(2)}, u32[]{:S(2)}) collective-permute-start(bf16[256,2048]{1,0:T(8,128)(2,1)S(1)} %collective-permute-done.7), channel_id=1, source_target_pairs={{0,64},{1,3},{2,66},{3,5},{4,68},{5,7},{6,70},{7,1},{8,72},{9,11},... | collective-permute-start | bytes 3145736 | tf_op jit(solution)/shard_map/ppermute | solution.py:40
  72.4 16.0 %collective-permute-start.6 = (bf16[256,2048]{1,0:T(8,128)(2,1)S(1)}, bf16[256,2048]{1,0:T(8,128)(2,1)S(1)}, u32[]{:S(2)}, u32[]{:S(2)}) collective-permute-start(bf16[256,2048]{1,0:T(8,128)(2,1)S(1)} %collective-permute-done.5), channel_id=1, source_target_pairs={{0,192},{1,7},{2,194},{3,1},{4,196},{5,3},{6,198},{7,5},{8,200},{9... | collective-permute-start | bytes 3145736 | tf_op jit(solution)/shard_map/ppermute | solution.py:40
  90.1 5.0 %collective-permute-start.11 = (f32[1408]{0:T(1024)S(1)}, f32[1408]{0:T(1024)S(1)}, u32[]{:S(2)}, u32[]{:S(2)}) collective-permute-start(f32[1408]{0:T(1024)S(1)} %concatenate.40), channel_id=1, source_target_pairs={{0,1},{1,0},{2,3},{3,2},{4,5},{5,4},{6,7},{7,6},{8,9},{9,8},{10,11... | collective-permute-start | bytes 16904 | tf_op jit(solution)/shard_map/ppermute | solution.py:44
  99.1 1.3 collective-permute-start.12
  141.1 6.7 %collective-permute-start.13 = (f32[8,640]{1,0:T(8,128)S(1)}, f32[8,640]{1,0:T(8,128)S(1)}, u32[]{:S(2)}, u32[]{:S(2)}) collective-permute-start(f32[8,640]{1,0:T(8,128)S(1)} %reduce_sum.229), channel_id=1, source_target_pairs={{0,0},{1,128},{128,1},{129,129},{2,2},{3,130},{130,3},{131,131},{4... | collective-permute-start | bytes 61448 | tf_op jit(solution)/shard_map/ppermute | solution.py:221
  146.3 4.2 %collective-permute-start.14 = (f32[8,640]{1,0:T(8,128)S(1)}, f32[8,640]{1,0:T(8,128)S(1)}, u32[]{:S(2)}, u32[]{:S(2)}) collective-permute-start(f32[8,640]{1,0:T(8,128)S(1)} %reduce_sum.229), channel_id=1, source_target_pairs={{0,128},{1,0},{128,129},{129,1},{2,130},{3,2},{130,131},{131,3},{4... | collective-permute-start | bytes 61448 | tf_op jit(solution)/shard_map/ppermute | solution.py:221
